TPU v7x, 256 devices: a whole 4x4x8 slice. The times are simulated.
256 devices in a mesh: brick: 64 (over y, z, core), grp: 4 (over x).
Axes of the slice: x: 4, y: 4, z: 8, core: 2. Of those that a mesh axis runs over, the one named last changes fastest.
Arguments:
- gradients: bfloat16 [512, 1048576], P('grp', 'brick'), may hold values from -33 to 33
- perm: int32 [8192], replicated, may hold values from 0 to 8191, as said below
- weights: float32 [1048576], P(('brick', 'grp')), may hold values from 0.1 to 48
- linear: float32 [1048576], P(('brick', 'grp')), may hold values from -6 to 6
- bound: float32 [512], replicated, may hold values from -0.3 to 0.3
Outputs:
- design_step: float32 [1048576], P(('brick', 'grp'))
- multipliers: float32 [512], replicated
Inputs may be any that keep to these rules, and one draw needn't show every extreme that they name: Design block k is the brick-layout block perm[k]; every value appears once. The 128 design blocks of each brick index (the blocks of one index of brick in design layout) come equally, 2 each, from the blocks of every brick index in brick layout.
All inputs are finite; a program needn't handle non-finite values.
Results may differ from a plain program's by a relative error of at most 0.0041.
Values may be sent and summed in bfloat16 or wider, within the bound.
No kernel may reach another device: no remote copies, remote signals or barrier semaphores. Data moves between devices by JAX's collectives and lax.ppermute only.
A program may use at most 64 MiB of HBM per device.

v0:
```python
import jax
import jax.numpy as jnp
from jax import lax
from jax.sharding import Mesh
from jax.sharding import PartitionSpec as P

ITERS = 4
BRICK = ("brick_0", "brick_1", "brick_2")
BRICK_GRP = ("brick_0", "brick_1", "brick_2", "grp")


move_limit = 1.0


def sent_together(arrays, axis, dim, along):
    widths = [a.shape[along] for a in arrays]
    both = jnp.concatenate(arrays, axis=along)
    filled = lax.all_gather(both, axis, axis=dim, tiled=True)
    return tuple(jnp.split(filled, [sum(widths[:k]) for k in range(1, len(widths))], axis=along))


def in_one_piece(arrays, axis, split_dim, concat_dim, along):
    ends, at = ([], 0)
    for a in arrays[:-1]:
        at += a.shape[along]
        ends.append(at)
    both = jnp.concatenate(arrays, axis=along)
    return tuple(
        jnp.split(
            lax.all_to_all(both, axis, split_axis=split_dim, concat_axis=concat_dim, tiled=True),
            ends,
            axis=along,
        )
    )


def filled_up(lines, devices):
    spare = -len(lines) % devices
    return jnp.pad(lines, [(0, spare)] + [(0, 0)] * (lines.ndim - 1))


def from_everyone(array, axis):
    devices = lax.axis_size(axis)
    return lax.all_to_all(
        jnp.broadcast_to(array[None], (devices, *array.shape)), axis, 0, 0, tiled=True
    )


def in_order(blocks, dim):
    shape = list(blocks.shape[1:])
    shape[dim] *= blocks.shape[0]
    return jnp.moveaxis(blocks, 0, dim).reshape(shape)


def gather_axes(array, axes, dim):
    far, near = axes
    leading = from_everyone(array, far)
    blocks = jnp.swapaxes(from_everyone(leading, near), 0, 1)
    return in_order(blocks.reshape(-1, *array.shape), dim)


def in_blocks(array, dim, devices):
    shape = array.shape
    blocks = array.reshape(*shape[:dim], devices, shape[dim] // devices, *shape[dim + 1 :])
    return jnp.moveaxis(blocks, dim, 0)


def sum_at_owner(array, axis, dim):
    blocks = in_blocks(array, dim, lax.axis_size(axis))
    arrived = lax.all_to_all(blocks, axis, split_axis=0, concat_axis=0, tiled=True)
    return arrived.sum(axis=0)


def sum_by_axis(array, axes, dim):
    far, near = axes
    own = sum_at_owner(in_blocks(array, dim, lax.axis_size(far)), near, dim + 1)
    return jnp.sum(lax.all_to_all(own, far, 0, 0, tiled=True), axis=0)


def sum_by_parts(array, axes):
    lines = array.reshape(-1, array.shape[-1])
    padded = filled_up(lines, lax.axis_size(axes[0]) * lax.axis_size(axes[1]))
    whole = gather_axes(sum_by_axis(padded, axes, 0), axes, 0)
    return lax.slice_in_dim(whole, 0, len(lines)).reshape(array.shape)


def of_everyone(array, axis):
    everything = from_everyone(array, axis)
    return jnp.sum(everything, axis=0)


def by_axis(array, axes):
    far, near = axes
    nearer = of_everyone(array, near)
    return of_everyone(nearer, far)


def collect(array, axis, dim):
    return in_order(from_everyone(array, axis), dim)


def layout_tables(perm, here, per_brick):
    total_blocks = perm.shape[0]
    index = jnp.arange(total_blocks, dtype=jnp.int32)
    owner = perm // per_brick
    keys = jnp.where(owner == here, index, index + total_blocks)
    chosen = jnp.argsort(keys)[:per_brick]
    outgoing = perm[chosen] % per_brick
    mine = lax.dynamic_slice_in_dim(perm, here * per_brick, per_brick)
    source = mine // per_brick
    arrival = jnp.argsort(source * per_brick + jnp.arange(per_brick, dtype=jnp.int32))
    place = jnp.argsort(arrival)
    return (outgoing, arrival, place)


def trial(full, curv, lin, lam_b):
    pushed = jnp.dot(lam_b, full, preferred_element_type=jnp.float32)
    return jnp.clip(-curv * (lin + pushed), -move_limit, move_limit)


def local_product(full, curv, lin, lam):
    moved = trial(full, curv, lin, lam.astype(jnp.bfloat16)).astype(jnp.bfloat16)
    return jnp.dot(full, moved, preferred_element_type=jnp.float32)


def on_device(gradients, perm, weights, linear, bound):
    ngrp = lax.axis_size("grp")
    here = lax.axis_index(BRICK)
    quarter = lax.axis_index("grp")
    rows_part, width = gradients.shape
    per_brick = width // 128
    per_quarter = per_brick // ngrp
    ncols = perm.shape[0] * 128
    outgoing, arrival, place = layout_tables(perm, here, per_brick)
    tiles = gradients.reshape(rows_part, per_brick, 128)
    curv_all, lin_all = sent_together(
        (weights.reshape(-1, 128), linear.reshape(-1, 128)), "grp", 0, 1
    )
    curv_back, lin_back = in_one_piece((curv_all[arrival], lin_all[arrival]), BRICK, 0, 0, 1)
    inverse = jnp.argsort(outgoing)
    start = quarter * per_quarter
    curv = lax.dynamic_slice_in_dim(curv_back[inverse], start, per_quarter, 0).reshape(-1)
    lin = lax.dynamic_slice_in_dim(lin_back[inverse], start, per_quarter, 0).reshape(-1)
    full = lax.all_to_all(tiles, "grp", split_axis=1, concat_axis=0, tiled=True)
    full = full.reshape(full.shape[0], per_quarter * 128)
    nrows = full.shape[0]
    weighted = (full.astype(jnp.float32) * curv).astype(jnp.bfloat16)
    partial_value = lax.dot_general(
        weighted, full, (((1,), (1,)), ((), ())), preferred_element_type=jnp.float32
    )
    lam = jnp.zeros((nrows,), jnp.float32)
    summed = sum_by_parts(partial_value, (("brick_0", "brick_1"), ("brick_2", "grp")))
    hessian = summed / ncols
    chol = jnp.linalg.cholesky(0.5 * (hessian + hessian.T))
    for step in range(ITERS):
        product = by_axis(
            local_product(full, curv, lin, lam), (("brick_0", "brick_1"), ("brick_2", "grp"))
        )
        lam = jnp.maximum(
            lam + jax.scipy.linalg.cho_solve((chol, True), product / ncols - bound), 0.0
        )
    result = trial(full, curv, lin, lam.astype(jnp.bfloat16))
    whole = collect(result.reshape(-1, 128), "grp", 0)
    arrived = lax.all_to_all(whole[outgoing], BRICK, split_axis=0, concat_axis=0, tiled=True)
    ordered = arrived[place]
    start = quarter * per_quarter
    result = lax.dynamic_slice_in_dim(ordered, start, per_quarter, 0).reshape(-1)
    return (result, lam)


def solution(mesh):
    torus = Mesh(
        mesh.devices.reshape(4, 8, 2, mesh.shape["grp"]), ("brick_0", "brick_1", "brick_2", "grp")
    )
    placed = (P("grp", BRICK), P(), P(BRICK_GRP), P(BRICK_GRP), P())
    return jax.shard_map(
        on_device, mesh=torus, in_specs=placed, out_specs=(P(BRICK_GRP), P()), check_vma=False
    )
```

profile of v0, /device:TPU:1, one launch (start us, length us, event | category | flops | bytes accessed | tf_op | source)
XLA Modules:
  0.0 503.0 jit_solution(14940864164833931707)
XLA Ops:
  1.4 6.8 %sort.63 = (s32[8192]{0:T(1024)}, s32[8192]{0:T(1024)S(1)}) sort(s32[8192]{0:T(1024)S(1)} %add_select_fusion.1, s32[8192]{0:T(1024)S(1)} %iota.106), dimensions={0}, to_apply=%region_1.2 | sort | flops 106496 | bytes 131072 | tf_op jit(solution)/shard_map/jit(argsort)/sort | solution.py:107
  14.0 10.3 %all_gather.3 = f32[128,256]{1,0:T(8,128)S(1)} all-gather(f32[32,256]{1,0:T(8,128)S(1)} %pad_maximum_fusion.1), channel_id=1, replica_groups=mesh['brick_0'=4,'brick_1'=8,'brick_2'=2,'grp'=4] {'grp'}, dimensions={0}, use_global_device_ids=true | all-gather | bytes 163840 | tf_op jit(solution)/shard_map/all_gather | solution.py:18
  26.3 15.2 %all-to-all-start = ((f32[64,2,256]{2,1,0:T(2,128)}), f32[64,2,256]{2,1,0:T(2,128)S(1)}, u32[]{:S(2)}, u32[]{:S(2)}) async-start(f32[64,2,256]{2,1,0:T(2,128)} %all_to_all.74), calls=%async_computation | async-start | bytes 262144 | tf_op jit(solution)/shard_map/all_to_all | solution.py:30
  47.9 6.4 %copy.43 = bf16[128,128,128]{2,0,1:T(8,128)(2,1)} copy(bf16[128,128,128]{0,2,1:T(8,128)(2,1)} %bitcast.578) | data formatting | bytes 8388608 | tf_op jit(solution)/shard_map/reshape | solution.py:135
  62.6 45.1 %all-to-all-done.1 = bf16[128,128,128]{2,0,1:T(8,128)(2,1)} async-done(((bf16[128,128,128]{2,0,1:T(8,128)(2,1)}), bf16[128,128,128]{2,0,1:T(8,128)(2,1)}, u32[]{:S(2)}, u32[]{:S(2)}) %all-to-all-start.1) | async-done | bytes 4194336 | tf_op jit(solution)/shard_map/all_to_all | solution.py:144
  117.1 6.9 %convert_element_type.41 = bf16[32,8,2,4096]{3,2,1,0:T(2,128)(2,1)} reshape(bf16[4,128,32,128]{3,2,1,0:T(8,128)(2,1)} %copy.45) | data formatting | bytes 8388608 | tf_op jit(solution)/shard_map/convert_element_type | solution.py:147
  124.0 6.8 %copy.46 = bf16[4,128,32,128]{3,2,1,0:T(8,128)(2,1)} copy(bf16[4,128,32,128]{3,1,2,0:T(8,128)(2,1)} %bitcast.8) | data formatting | bytes 8388608 | tf_op jit(solution)/shard_map/all_to_all | solution.py:144
  130.8 7.5 %reshape.367 = bf16[512,4096,1,1]{1,0,2,3:T(8,128)(2,1)} reshape(bf16[4,128,32,128]{3,2,1,0:T(8,128)(2,1)} %copy.46) | data formatting | bytes 8388608 | tf_op jit(solution)/shard_map/reshape | solution.py:145
  157.6 8.6 %all-to-all-done.2 = f32[8,32,2,512]{3,2,1,0:T(2,128)S(1)} async-done(((f32[8,32,2,512]{3,2,1,0:T(2,128)}), f32[8,32,2,512]{3,2,1,0:T(2,128)S(1)}, u32[]{:S(2)}, u32[]{:S(2)}) %all-to-all-start.2) | async-done | bytes 1048608 | tf_op jit(solution)/shard_map/all_to_all | solution.py:70
  175.3 9.5 %all-to-all-start.3 = ((f32[32,2,512]{2,1,0:T(2,128)}), f32[32,2,512]{2,1,0:T(2,128)S(1)}, u32[]{:S(2)}, u32[]{:S(2)}) async-start(f32[32,2,512]{2,1,0:T(2,128)} %reduce_sum.90), calls=%async_computation.3 | async-start | bytes 262144 | tf_op jit(solution)/shard_map/all_to_all | solution.py:77
  184.8 9.1 %all-to-all-done.3 = f32[32,2,512]{2,1,0:T(2,128)S(1)} async-done(((f32[32,2,512]{2,1,0:T(2,128)}), f32[32,2,512]{2,1,0:T(2,128)S(1)}, u32[]{:S(2)}, u32[]{:S(2)}) %all-to-all-start.3) | async-done | bytes 131104 | tf_op jit(solution)/shard_map/all_to_all | solution.py:77
  199.0 8.8 %all-to-all-done.7 = f32[32,1,512]{2,1,0:T(1,128)S(1)} async-done(((f32[32,1,512]{2,1,0:T(1,128)}), f32[32,1,512]{2,1,0:T(1,128)S(1)}, u32[]{:S(2)}, u32[]{:S(2)}) %all-to-all-start.7) | async-done | bytes 65568 | tf_op jit(solution)/shard_map/all_to_all | solution.py:44
  207.9 12.3 %all_to_all.112 = f32[32,2,512]{2,1,0:T(2,128)S(1)} all-to-all(f32[32,2,512]{2,1,0:T(2,128)S(1)} %broadcast_in_dim.38), channel_id=1, replica_groups=mesh['brick_0'=4,'brick_1'=8,'brick_2'=2,'grp'=4] {'brick_0','brick_1'}, dimensions={0} | all-to-all | bytes 262144 | tf_op jit(solution)/shard_map/all_to_all | solution.py:44
  221.4 7.8 %all-to-all-start.5 = ((f32[8,32,2,512]{3,2,1,0:T(2,128)}), f32[8,32,2,512]{3,2,1,0:T(2,128)S(1)}, u32[]{:S(2)}, u32[]{:S(2)}) async-start(f32[8,32,2,512]{3,2,1,0:T(2,128)} %broadcast_in_dim.39), calls=%async_computation.5 | async-start | bytes 2097152 | tf_op jit(solution)/shard_map/all_to_all | solution.py:44
  229.4 14.5 %all-to-all-done.5 = f32[8,32,2,512]{3,2,1,0:T(2,128)S(1)} async-done(((f32[8,32,2,512]{3,2,1,0:T(2,128)}), f32[8,32,2,512]{3,2,1,0:T(2,128)S(1)}, u32[]{:S(2)}, u32[]{:S(2)}) %all-to-all-start.5) | async-done | bytes 1048608 | tf_op jit(solution)/shard_map/all_to_all | solution.py:44
  246.9 11.7 %cholesky.104 = f32[128,128]{1,0:T(8,128)S(1)} custom-call(f32[128,128]{1,0:T(8,128)S(1)} %cholesky.266), custom_call_target="Cholesky" | custom-call | tf_op jit(solution)/shard_map/jit(cholesky)/cholesky | solution.py:154
  258.8 9.8 %custom-call.32 = f32[1,128,128]{1,2,0:T(8,128)S(1)} custom-call(f32[1,128,128]{2,1,0:T(8,128)S(1)} %get-tuple-element.66), custom_call_target="InvertDiagBlocksLowerTriangular" | custom-call | tf_op jit(solution)/shard_map/jit(cholesky)/cholesky | solution.py:154
  269.2 11.8 %cholesky.217 = f32[128,128]{1,0:T(8,128)S(1)} custom-call(f32[128,128]{1,0:T(8,128)S(1)} %cholesky.270), custom_call_target="Cholesky" | custom-call | tf_op jit(solution)/shard_map/jit(cholesky)/cholesky | solution.py:154
  282.4 9.8 %custom-call.33 = f32[1,128,128]{1,2,0:T(8,128)S(1)} custom-call(f32[1,128,128]{2,1,0:T(8,128)S(1)} %get-tuple-element.63), custom_call_target="InvertDiagBlocksLowerTriangular" | custom-call | tf_op jit(solution)/shard_map/jit(cholesky)/cholesky | solution.py:154
  292.9 11.7 %cholesky.238 = f32[128,128]{1,0:T(8,128)S(1)} custom-call(f32[128,128]{1,0:T(8,128)S(1)} %cholesky.275), custom_call_target="Cholesky" | custom-call | tf_op jit(solution)/shard_map/jit(cholesky)/cholesky | solution.py:154
  305.3 9.8 %custom-call.34 = f32[1,128,128]{1,2,0:T(8,128)S(1)} custom-call(f32[1,128,128]{2,1,0:T(8,128)S(1)} %get-tuple-element.60), custom_call_target="InvertDiagBlocksLowerTriangular" | custom-call | tf_op jit(solution)/shard_map/jit(cholesky)/cholesky | solution.py:154
  315.7 11.9 %cholesky.255 = f32[128,128]{1,0:T(8,128)S(1)} custom-call(f32[128,128]{1,0:T(8,128)S(1)} %convolution_subtract_fusion.2), custom_call_target="Cholesky" | custom-call | tf_op jit(solution)/shard_map/jit(cholesky)/cholesky | solution.py:154
  331.1 7.9 %while.8 = (s32[]{:T(128)}, f32[512,512]{1,0:T(8,128)S(1)}, s32[4,2]{0,1:T(2,128)S(1)}, f32[4,128,128]{2,1,0:T(8,128)S(1)}, s32[]{:T(128)}) while((s32[]{:T(128)}, f32[512,512]{1,0:T(8,128)S(1)}, s32[4,2]{0,1:T(2,128)S(1)}, f32[4,128,128]{2,1,0:T(8,128)S(1)}, s32[]{:T(128)}) %tuple.45), condition=%wide.while_cond, body=%wide.while_body.sunk | while | flops 2 | bytes 131181 | solution.py:160
  339.0 39.3 %custom-call.38 = f32[4,128,128]{1,2,0:T(8,128)S(1)} custom-call(f32[4,128,128]{2,1,0:T(8,128)S(1)} %get-tuple-element.37), custom_call_target="InvertDiagBlocksLowerTriangular" | custom-call | tf_op jit(solution)/shard_map/jit(_cho_solve)/triangular_solve | solution.py:160
  386.9 8.1 %all_to_all.113 = f32[8,1,512]{2,1,0:T(1,128)S(1)} all-to-all(f32[8,1,512]{2,1,0:T(1,128)S(1)} %broadcast_in_dim.42), channel_id=1, replica_groups=mesh['brick_0'=4,'brick_1'=8,'brick_2'=2,'grp'=4] {'brick_2','grp'}, dimensions={0} | all-to-all | bytes 32768 | tf_op jit(solution)/shard_map/all_to_all | solution.py:44
  395.1 12.4 %all_to_all.114 = f32[32,1,512]{2,1,0:T(1,128)S(1)} all-to-all(f32[32,1,512]{2,1,0:T(1,128)S(1)} %broadcast_in_dim.43), channel_id=1, replica_groups=mesh['brick_0'=4,'brick_1'=8,'brick_2'=2,'grp'=4] {'brick_0','brick_1'}, dimensions={0} | all-to-all | bytes 131072 | tf_op jit(solution)/shard_map/all_to_all | solution.py:44
  416.1 9.1 %all_to_all.115 = f32[8,1,512]{2,1,0:T(1,128)S(1)} all-to-all(f32[8,1,512]{2,1,0:T(1,128)S(1)} %broadcast_in_dim.44), channel_id=1, replica_groups=mesh['brick_0'=4,'brick_1'=8,'brick_2'=2,'grp'=4] {'brick_2','grp'}, dimensions={0} | all-to-all | bytes 32768 | tf_op jit(solution)/shard_map/all_to_all | solution.py:44
  425.3 11.9 %all_to_all.116 = f32[32,1,512]{2,1,0:T(1,128)S(1)} all-to-all(f32[32,1,512]{2,1,0:T(1,128)S(1)} %broadcast_in_dim.45), channel_id=1, replica_groups=mesh['brick_0'=4,'brick_1'=8,'brick_2'=2,'grp'=4] {'brick_0','brick_1'}, dimensions={0} | all-to-all | bytes 131072 | tf_op jit(solution)/shard_map/all_to_all | solution.py:44
  445.8 8.9 %all_to_all.117 = f32[8,1,512]{2,1,0:T(1,128)S(1)} all-to-all(f32[8,1,512]{2,1,0:T(1,128)S(1)} %broadcast_in_dim.46), channel_id=1, replica_groups=mesh['brick_0'=4,'brick_1'=8,'brick_2'=2,'grp'=4] {'brick_2','grp'}, dimensions={0} | all-to-all | bytes 32768 | tf_op jit(solution)/shard_map/all_to_all | solution.py:44
  459.4 8.8 %all-to-all-done.13 = f32[32,1,512]{2,1,0:T(1,128)S(1)} async-done(((f32[32,1,512]{2,1,0:T(1,128)}), f32[32,1,512]{2,1,0:T(1,128)S(1)}, u32[]{:S(2)}, u32[]{:S(2)}) %all-to-all-start.13) | async-done | bytes 65568 | tf_op jit(solution)/shard_map/all_to_all | solution.py:44
  484.9 6.7 %all-to-all-start.15 = ((f32[64,2,128]{2,1,0:T(2,128)}), f32[64,2,128]{2,1,0:T(2,128)S(1)}, u32[]{:S(2)}, u32[]{:S(2)}) async-start(f32[64,2,128]{2,1,0:T(2,128)} %bitcast.185), calls=%async_computation.15 | async-start | bytes 131072 | tf_op jit(solution)/shard_map/all_to_all | solution.py:164
  491.7 9.9 %all-to-all-done.15 = f32[64,2,128]{2,1,0:T(2,128)S(1)} async-done(((f32[64,2,128]{2,1,0:T(2,128)}), f32[64,2,128]{2,1,0:T(2,128)S(1)}, u32[]{:S(2)}, u32[]{:S(2)}) %all-to-all-start.15) | async-done | bytes 65568 | tf_op jit(solution)/shard_map/all_to_all | solution.py:164
  (215 shorter events, 131.4 us)
Async XLA Ops:
  13.2 0.8 copy-start.5
  26.3 28.0 %all-to-all-start = ((f32[64,2,256]{2,1,0:T(2,128)}), f32[64,2,256]{2,1,0:T(2,128)S(1)}, u32[]{:S(2)}, u32[]{:S(2)}) async-start(f32[64,2,256]{2,1,0:T(2,128)} %all_to_all.74), calls=%async_computation | async-start | bytes 262144 | tf_op jit(solution)/shard_map/all_to_all | solution.py:30
  54.3 53.5 %all-to-all-start.1 = ((bf16[128,128,128]{2,0,1:T(8,128)(2,1)}), bf16[128,128,128]{2,0,1:T(8,128)(2,1)}, u32[]{:S(2)}, u32[]{:S(2)}) async-start(bf16[128,128,128]{2,0,1:T(8,128)(2,1)} %copy.43), calls=%async_computation.1 | async-start | bytes 8388608 | tf_op jit(solution)/shard_map/all_to_all | solution.py:144
  146.5 19.8 %all-to-all-start.2 = ((f32[8,32,2,512]{3,2,1,0:T(2,128)}), f32[8,32,2,512]{3,2,1,0:T(2,128)S(1)}, u32[]{:S(2)}, u32[]{:S(2)}) async-start(f32[8,32,2,512]{3,2,1,0:T(2,128)} %copy.48), calls=%async_computation.2 | async-start | bytes 2097152 | tf_op jit(solution)/shard_map/all_to_all | solution.py:70
  151.9 3.6 copy-start
  155.5 73.9 %copy-start.4 = (f32[512]{0:T(512)S(1)}, f32[512]{0:T(512)}, u32[]{:S(2)}) copy-start(f32[512]{0:T(512)} %param.11) | copy-start | bytes 6148
  166.8 8.4 %all-to-all-start.6 = ((f32[8,1,512]{2,1,0:T(1,128)}), f32[8,1,512]{2,1,0:T(1,128)S(1)}, u32[]{:S(2)}, u32[]{:S(2)}) async-start(f32[8,1,512]{2,1,0:T(1,128)} %broadcast_in_dim.40), calls=%async_computation.6 | async-start | bytes 32768 | tf_op jit(solution)/shard_map/all_to_all | solution.py:44
  175.3 18.6 %all-to-all-start.3 = ((f32[32,2,512]{2,1,0:T(2,128)}), f32[32,2,512]{2,1,0:T(2,128)S(1)}, u32[]{:S(2)}, u32[]{:S(2)}) async-start(f32[32,2,512]{2,1,0:T(2,128)} %reduce_sum.90), calls=%async_computation.3 | async-start | bytes 262144 | tf_op jit(solution)/shard_map/all_to_all | solution.py:77
  194.6 13.2 %all-to-all-start.7 = ((f32[32,1,512]{2,1,0:T(1,128)}), f32[32,1,512]{2,1,0:T(1,128)S(1)}, u32[]{:S(2)}, u32[]{:S(2)}) async-start(f32[32,1,512]{2,1,0:T(1,128)} %broadcast_in_dim.41), calls=%async_computation.7 | async-start | bytes 131072 | tf_op jit(solution)/shard_map/all_to_all | solution.py:44
  221.4 22.4 %all-to-all-start.5 = ((f32[8,32,2,512]{3,2,1,0:T(2,128)}), f32[8,32,2,512]{3,2,1,0:T(2,128)S(1)}, u32[]{:S(2)}, u32[]{:S(2)}) async-start(f32[8,32,2,512]{3,2,1,0:T(2,128)} %broadcast_in_dim.39), calls=%async_computation.5 | async-start | bytes 2097152 | tf_op jit(solution)/shard_map/all_to_all | solution.py:44
  378.3 6.4 %copy-start.1 = (bf16[4,128,32,128]{3,2,1,0:T(8,128)(2,1)S(1)}, bf16[4,128,32,128]{3,2,1,0:T(8,128)(2,1)}, u32[]{:S(2)}) copy-start(bf16[4,128,32,128]{3,2,1,0:T(8,128)(2,1)} %copy.46) | copy-start | bytes 12582916
  407.6 6.4 %copy-start.2 = (bf16[4,128,32,128]{3,2,1,0:T(8,128)(2,1)S(1)}, bf16[4,128,32,128]{3,2,1,0:T(8,128)(2,1)}, u32[]{:S(2)}) copy-start(bf16[4,128,32,128]{3,2,1,0:T(8,128)(2,1)} %copy.46) | copy-start | bytes 12582916
  437.2 6.4 %copy-start.3 = (bf16[4,128,32,128]{3,2,1,0:T(8,128)(2,1)S(1)}, bf16[4,128,32,128]{3,2,1,0:T(8,128)(2,1)}, u32[]{:S(2)}) copy-start(bf16[4,128,32,128]{3,2,1,0:T(8,128)(2,1)} %copy.46) | copy-start | bytes 12582916
  443.6 35.6 %copy-start.6 = (s32[128]{0:T(128)S(1)}, s32[128]{0:T(128)}, u32[]{:S(2)}) copy-start(s32[128]{0:T(128)} %copy-done.5) | copy-start | bytes 1540
  455.4 12.9 %all-to-all-start.13 = ((f32[32,1,512]{2,1,0:T(1,128)}), f32[32,1,512]{2,1,0:T(1,128)S(1)}, u32[]{:S(2)}, u32[]{:S(2)}) async-start(f32[32,1,512]{2,1,0:T(1,128)} %broadcast_in_dim.47), calls=%async_computation.13 | async-start | bytes 131072 | tf_op jit(solution)/shard_map/all_to_all | solution.py:44
  475.9 7.7 %all-to-all-start.14 = ((f32[4,32,128]{2,1,0:T(8,128)}), f32[4,32,128]{2,1,0:T(8,128)S(1)}, u32[]{:S(2)}, u32[]{:S(2)}) async-start(f32[4,32,128]{2,1,0:T(8,128)} %broadcast_in_dim.49), calls=%async_computation.14 | async-start | bytes 131072 | tf_op jit(solution)/shard_map/all_to_all | solution.py:44
  484.9 16.6 %all-to-all-start.15 = ((f32[64,2,128]{2,1,0:T(2,128)}), f32[64,2,128]{2,1,0:T(2,128)S(1)}, u32[]{:S(2)}, u32[]{:S(2)}) async-start(f32[64,2,128]{2,1,0:T(2,128)} %bitcast.185), calls=%async_computation.15 | async-start | bytes 131072 | tf_op jit(solution)/shard_map/all_to_all | solution.py:164
where the time goes:
time: 510 us; the launch traced here: 503 us
  other arithmetic  141 us (28%)
  waiting for transfers between devices  111 us (22%)
  blocking collectives  73 us (14%)
  local copies, waits for them, and re-layouts  65 us (13%)
  starting transfers between devices  64.3 us (13%)
  matrix products  45.3 us (9%)
    another operation x15, other arithmetic, on_device(): chol = jnp.linalg.cholesky(0.5 * (hessian + hessian.T))  79.4 us
    all_to_all x6, blocking collectives, from_everyone(): lax.all_to_all(jnp.broadcast_to(array[None], (devices, *array.shape)), ax...  62.7 us
    all_to_all x1, waiting for transfers between devices, on_device(): full = lax.all_to_all(tiles, 'grp', split_axis=1, concat_axis=0, tiled=True)  45.1 us
    another operation x8, other arithmetic, on_device(): jax.scipy.linalg.cho_solve((chol, True), product / ncols - bound)  39.5 us
    all_to_all x5, waiting for transfers between devices, from_everyone(): lax.all_to_all(jnp.broadcast_to(array[None], (devices, *array.shape)), ax...  37.8 us
    all_to_all x5, starting transfers between devices, from_everyone(): lax.all_to_all(jnp.broadcast_to(array[None], (devices, *array.shape)), ax...  23.1 us
    dot_general x5, matrix products, trial(): pushed = jnp.dot(lam_b, full, preferred_element_type=jnp.float32)  17.1 us
    all_to_all x1, starting transfers between devices, in_one_piece(): lax.all_to_all(both, axis, split_axis=split_dim, concat_axis=concat_dim,...  15.2 us
  transfers between devices with their start and end apart: 10, of which 9 were waited for; matrix products, arithmetic and copies ran while one was open for 5% of the time, Pallas kernels for 0%

commit v1 on v0

v1 whole, which is shorter than its diff:
```python
import functools

import jax
import jax.numpy as jnp
from jax import lax
from jax.experimental import pallas as pl
from jax.experimental.pallas import tpu as pltpu
from jax.sharding import Mesh
from jax.sharding import PartitionSpec as P

ITERS = 4
BRICK = ("brick_0", "brick_1", "brick_2")
BRICK_GRP = ("brick_0", "brick_1", "brick_2", "grp")
FAR = ("brick_0", "brick_1")
NEAR = ("brick_2", "grp")
PLANE = ("brick_0", "grp")
M = 512
ROWS = 128
NB = M // ROWS
COLS = 4096
BLKS = COLS // 128
NVAR = 1048576
PAIRS = [(i, j) for i in range(NB) for j in range(i + 1)]
SHARDS = 32
SHARD_G = len(PAIRS) * ROWS // SHARDS
SHARD = SHARD_G + 8
HALF = SHARDS // 2
DOUBLINGS = 5
MAX_CORRECT = 48
ACCEPT = 0.01

move_limit = 1.0
MIB = 1024 * 1024
BF = jnp.bfloat16
F32 = jnp.float32


def size_of(axis):
    return lax.axis_size(axis)


def from_everyone(array, axis):
    devices = size_of(axis)
    return lax.all_to_all(
        jnp.broadcast_to(array[None], (devices, *array.shape)), axis, 0, 0, tiled=True
    )


def layout_tables(perm, here, per_brick):
    total_blocks = perm.shape[0]
    index = jnp.arange(total_blocks, dtype=jnp.int32)
    owner = perm // per_brick
    keys = jnp.where(owner == here, index, index + total_blocks)
    chosen = jnp.argsort(keys)[:per_brick]
    outgoing = perm[chosen] % per_brick
    mine = lax.dynamic_slice_in_dim(perm, here * per_brick, per_brick)
    source = mine // per_brick
    arrival = jnp.argsort(source * per_brick + jnp.arange(per_brick, dtype=jnp.int32))
    place = jnp.argsort(arrival)
    return (outgoing, arrival, place)


def down(row):
    return jnp.broadcast_to(row, (128, 128)).T


def times(mat_ref, vec):
    total = [jnp.zeros((8, 128), F32) for _ in range(NB)]
    for i in range(NB):
        column = down(vec[i : i + 1, :])
        for j in range(NB):
            part = mat_ref[i * 128 : (i + 1) * 128, j * 128 : (j + 1) * 128] * column
            total[j] = total[j] + part.reshape(16, 8, 128).sum(axis=0)
    return jnp.concatenate([t.sum(axis=0, keepdims=True) for t in total], axis=0)


def flat_rows(ref, rows, first, count):
    return jnp.concatenate([ref[pl.ds(first + k, 1), :] for k in range(count)], axis=1)


def trial_chunk(full_ref, curv_ref, lin_ref, lam_b, chunk, width):
    count = width // 128
    start = pl.multiple_of(chunk * width, width)
    block = full_ref[:, :, pl.ds(start, width)].reshape(M, width)
    pushed = jnp.dot(lam_b, block, preferred_element_type=F32)
    curv = flat_rows(curv_ref, None, chunk * count, count)
    lin = flat_rows(lin_ref, None, chunk * count, count)
    return jnp.clip(-curv * (lin + pushed), -move_limit, move_limit), block


def as_rows(lam):
    flat = jnp.concatenate([lam[i : i + 1, :] for i in range(NB)], axis=1)
    return jnp.broadcast_to(flat, (16, M)).astype(BF)


def product_of_trial(full_ref, curv_ref, lin_ref, lam, acc_ref):
    width = 1024
    lam_b = as_rows(lam)
    acc_ref[...] = jnp.zeros_like(acc_ref)

    def step(chunk, carry):
        moved, block = trial_chunk(full_ref, curv_ref, lin_ref, lam_b, chunk, width)
        acc_ref[...] += lax.dot_general(
            moved.astype(BF), block, (((1,), (1,)), ((), ())), preferred_element_type=F32
        )
        return carry

    lax.fori_loop(0, COLS // width, step, 0)
    flat = acc_ref[0:1, :]
    return jnp.concatenate([flat[:, i * 128 : (i + 1) * 128] for i in range(NB)], axis=0)


def newton_update(lam, total, bound, hess_ref, inv_ref, scale):
    rhs = (total * (1.0 / NVAR) - bound) * scale
    step = times(inv_ref, rhs)
    for _ in range(2):
        step = step + times(inv_ref, rhs - times(hess_ref, step))
    return jnp.maximum(lam + step * scale, 0.0)


def gram_kernel(
    at_ref, own_hbm, one_hbm, two_hbm, three_hbm, curv_ref, lin_ref,
    full_ref, mine_ref, other_ref, top_ref, low_ref, prod_ref, half_ref, sems,
):
    quarter, core = at_ref[0], at_ref[1]
    start = pl.multiple_of(quarter * COLS, COLS)
    copies = [
        pltpu.make_async_copy(
            own_hbm.at[:, pl.ds(start, COLS)], full_ref.at[quarter], sems.at[0]
        )
    ]
    for k, piece in ((1, one_hbm), (2, two_hbm), (3, three_hbm)):
        copies.append(
            pltpu.make_async_copy(piece, full_ref.at[lax.rem(quarter + 4 - k, 4)], sems.at[k])
        )
    for copy in copies:
        copy.start()
    top_ref[...] = jnp.zeros_like(top_ref)
    low_ref[...] = jnp.zeros_like(low_ref)
    prod_ref[...] = jnp.zeros_like(prod_ref)
    for copy in copies:
        copy.wait()
    width = 1024
    count = width // 128
    nt = (((1,), (1,)), ((), ()))

    def step(chunk, carry):
        at = pl.multiple_of(chunk * width, width)
        block = full_ref[:, :, pl.ds(at, width)].reshape(M, width)
        curv = flat_rows(curv_ref, None, chunk * count, count)
        lin = flat_rows(lin_ref, None, chunk * count, count)
        weighted = (block.astype(F32) * curv).astype(BF)
        top_ref[...] += lax.dot_general(
            weighted[:256], block[:256], nt, preferred_element_type=F32
        )
        low_ref[...] += lax.dot_general(weighted[256:], block, nt, preferred_element_type=F32)
        moved = jnp.clip(-curv * lin, -move_limit, move_limit)
        moved = jnp.broadcast_to(moved, (16, width)).astype(BF)
        prod_ref[...] += lax.dot_general(moved, block, nt, preferred_element_type=F32)
        return carry

    lax.fori_loop(0, COLS // width, step, 0)
    for s in range(SHARDS):
        half_ref[s // HALF, s % HALF, SHARD_G:, :] = jnp.zeros((8, 128), F32)
    for j in range(NB):
        half_ref[0, j, SHARD_G : SHARD_G + 1, :] = prod_ref[0:1, j * 128 : (j + 1) * 128]
    for p, (i, j) in enumerate(PAIRS):
        for t in range(16):
            tile = p * 16 + t
            shard, row = tile // (SHARD_G // 8), tile % (SHARD_G // 8) * 8
            if i < 2:
                value = top_ref[i * 128 + t * 8 : i * 128 + t * 8 + 8, j * 128 : (j + 1) * 128]
            else:
                at = (i - 2) * 128 + t * 8
                value = low_ref[at : at + 8, j * 128 : (j + 1) * 128]
            half_ref[shard // HALF, shard % HALF, row : row + 8, :] = value
    mine_ref[...] = half_ref[core]
    other_ref[...] = half_ref[1 - core]


def split(value):
    high = value.astype(BF)
    return high, (value - high.astype(F32)).astype(BF)


def times_split(a_high, a_low, b_high, b_low):
    dot = functools.partial(jnp.dot, preferred_element_type=F32)
    return dot(a_high, b_high) + (dot(a_high, b_low) + dot(a_low, b_high))


def solve_kernel(
    at_ref, mine_ref, other_ref, full_ref, curv_ref, lin_ref, bound_ref,
    hess_ref, inv_ref, scale_ref, lam_ref, part_ref,
    half_ref, r_ref, prod_ref,
):
    core = at_ref[1]
    half_ref[core] = mine_ref[...]
    half_ref[1 - core] = other_ref[...]
    for p, (i, j) in enumerate(PAIRS):
        for t in range(16):
            tile = p * 16 + t
            shard, row = tile // (SHARD_G // 8), tile % (SHARD_G // 8) * 8
            hess_ref[i * 128 + t * 8 : i * 128 + t * 8 + 8, j * 128 : (j + 1) * 128] = (
                half_ref[shard // HALF, shard % HALF, row : row + 8, :] * (1.0 / NVAR)
            )
    row_id = lax.broadcasted_iota(jnp.int32, (128, 128), 0)
    col_id = lax.broadcasted_iota(jnp.int32, (128, 128), 1)
    diagonal = row_id == col_id
    for i in range(NB):
        at = slice(i * 128, (i + 1) * 128)
        for j in range(i):
            hess_ref[j * 128 : (j + 1) * 128, at] = hess_ref[at, j * 128 : (j + 1) * 128].T
        square = hess_ref[at, at]
        square = 0.5 * (square + square.T)
        hess_ref[at, at] = square
        values = jnp.sum(jnp.where(diagonal, square, 0.0), axis=0, keepdims=True)
        scale_ref[i : i + 1, :] = lax.rsqrt(values)
    scale = scale_ref[...]
    scale_row = jnp.concatenate([scale[i : i + 1, :] for i in range(NB)], axis=1)
    widest = jnp.zeros((1, M), F32)
    for i in range(NB):
        at = slice(i * 128, (i + 1) * 128)
        column = jnp.concatenate([down(scale[i : i + 1, :])] * NB, axis=1)
        rows = hess_ref[at, :] * column * scale_row
        hess_ref[at, :] = rows
        widest = widest + jnp.sum(jnp.abs(rows), axis=0, keepdims=True)
    alpha = 1.9 / jnp.max(widest)

    def eye():
        rid = lax.broadcasted_iota(jnp.int32, (M, M), 0)
        cid = lax.broadcasted_iota(jnp.int32, (M, M), 1)
        return (rid == cid).astype(F32)

    first = eye() - alpha * hess_ref[...]
    r_ref[...] = first
    inv_ref[...] = alpha * (eye() + first)

    def double(_, carry):
        r = r_ref[...].astype(BF)
        r2 = jnp.dot(r, r, preferred_element_type=F32)
        r_ref[...] = r2
        inv_ref[...] += jnp.dot(
            inv_ref[...].astype(BF), r2.astype(BF), preferred_element_type=F32
        )
        return carry

    lax.fori_loop(0, DOUBLINGS - 1, double, 0)

    def correct(state):
        count, _ = state
        x_high, x_low = split(inv_ref[...])
        h_high, h_low = split(hess_ref[...])
        residual = eye() - times_split(h_high, h_low, x_high, x_low)
        size = jnp.sum(residual * residual)
        good = size < M

        @pl.when(good)
        def _():
            r_high, r_low = split(residual)
            inv_ref[...] += times_split(x_high, x_low, r_high, r_low)

        @pl.when(jnp.logical_not(good))
        def _():
            inv_ref[...] = alpha * eye()

        return count + 1, size

    def unfinished(state):
        count, size = state
        return jnp.logical_and(jnp.logical_not(size < ACCEPT), count < MAX_CORRECT)

    _, size = lax.while_loop(unfinished, correct, (jnp.int32(0), jnp.float32(2.0 * M)))

    @pl.when(jnp.logical_not(size < ACCEPT))
    def _():
        inv_ref[...] = hess_ref[...]
        cid = lax.broadcasted_iota(jnp.int32, (8, M), 1)

        def pivot(k, carry):
            row = inv_ref[pl.ds(k, 1), :]
            here = lax.broadcasted_iota(jnp.int32, (1, M), 1) == k
            inverse = 1.0 / jnp.sum(jnp.where(here, row, 0.0))
            row = jnp.where(here, 1.0, row) * inverse

            def sweep(b, inner):
                at = pl.multiple_of(b * 8, 8)
                rows = inv_ref[pl.ds(at, 8), :]
                factor = jnp.sum(jnp.where(cid == k, rows, 0.0), axis=1, keepdims=True)
                rows = jnp.where(cid == k, 0.0, rows) - factor * row
                rid = lax.broadcasted_iota(jnp.int32, (8, M), 0) + at
                inv_ref[pl.ds(at, 8), :] = jnp.where(rid == k, row, rows)
                return inner

            lax.fori_loop(0, M // 8, sweep, 0)
            return carry

        lax.fori_loop(0, M, pivot, 0)

    total = jnp.concatenate(
        [half_ref[0, j, SHARD_G : SHARD_G + 1, :] for j in range(NB)], axis=0
    )
    zero = jnp.zeros((NB, 128), F32)
    lam = newton_update(zero, total, bound_ref[...], hess_ref, inv_ref, scale)
    lam_ref[...] = lam
    part_ref[...] = product_of_trial(full_ref, curv_ref, lin_ref, lam, prod_ref)


def step_kernel(
    gathered_ref, lam_in_ref, full_ref, curv_ref, lin_ref, bound_ref, hess_ref, inv_ref, scale_ref,
    lam_ref, part_ref, prod_ref,
):
    total = jnp.sum(gathered_ref[...], axis=0)
    lam = newton_update(
        lam_in_ref[...], total, bound_ref[...], hess_ref, inv_ref, scale_ref[...]
    )
    lam_ref[...] = lam
    part_ref[...] = product_of_trial(full_ref, curv_ref, lin_ref, lam, prod_ref)


def last_kernel(
    gathered_ref, lam_in_ref, full_ref, curv_ref, lin_ref, bound_ref, hess_ref, inv_ref, scale_ref,
    lam_ref, step_ref,
):
    total = jnp.sum(gathered_ref[...], axis=0)
    lam = newton_update(
        lam_in_ref[...], total, bound_ref[...], hess_ref, inv_ref, scale_ref[...]
    )
    lam_ref[...] = lam
    lam_b = as_rows(lam)
    width = 1024
    for chunk in range(COLS // width):
        moved, _ = trial_chunk(full_ref, curv_ref, lin_ref, lam_b, chunk, width)
        for k in range(width // 128):
            step_ref[chunk * (width // 128) + k : chunk * (width // 128) + k + 1, :] = moved[
                0:1, k * 128 : (k + 1) * 128
            ]


VM = pl.BlockSpec(memory_space=pltpu.VMEM)
SM = pl.BlockSpec(memory_space=pltpu.SMEM)
ANY = pl.BlockSpec(memory_space=pl.ANY)


def sds(shape, dtype=F32):
    return jax.ShapeDtypeStruct(shape, dtype)


def call(kernel, ins, outs, scratch, mib, name):
    return pl.pallas_call(
        kernel,
        in_specs=ins,
        out_specs=[VM] * len(outs),
        out_shape=outs,
        scratch_shapes=scratch,
        compiler_params=pltpu.CompilerParams(vmem_limit_bytes=mib * MIB),
        name=name,
    )


def summed(part):
    near = from_everyone(part, NEAR).sum(axis=0)
    return from_everyone(near, FAR)


def on_device(gradients, perm, weights, linear, bound):
    here = lax.axis_index(BRICK)
    quarter = lax.axis_index("grp")
    core = lax.axis_index("brick_2")
    per_brick = gradients.shape[1] // 128
    at = jnp.stack([quarter, core]).astype(jnp.int32)

    def toward(k):
        to = lax.rem(quarter + k, 4) * COLS
        piece = lax.dynamic_slice(gradients, (0, to), (ROWS, COLS))
        return lax.ppermute(piece, "grp", [(i, (i + k) % 4) for i in range(4)])

    two, one, three = toward(2), toward(1), toward(3)

    outgoing, arrival, place = layout_tables(perm, here, per_brick)
    inverse = lax.dynamic_slice_in_dim(jnp.argsort(outgoing), quarter * BLKS, BLKS)
    both = jnp.concatenate([weights.reshape(BLKS, 128), linear.reshape(BLKS, 128)], axis=1)
    both = from_everyone(both, "grp").reshape(per_brick, 256)
    back = lax.all_to_all(both[arrival], BRICK, 0, 0, tiled=True)[inverse]
    curv, lin = back[:, :128], back[:, 128:]

    packed = (HALF, SHARD, 128)
    full, mine, other = call(
        gram_kernel,
        [SM, ANY, ANY, ANY, ANY, VM, VM],
        [sds((NB, ROWS, COLS), BF), sds(packed), sds(packed)],
        [
            pltpu.VMEM((256, 256), F32),
            pltpu.VMEM((256, 512), F32),
            pltpu.VMEM((16, M), F32),
            pltpu.VMEM((2, *packed), F32),
            pltpu.SemaphoreType.DMA((4,)),
        ],
        24,
        "gram",
    )(at, gradients, one, two, three, curv, lin)

    swap = [(0, 1), (1, 0)]
    mine = mine + lax.ppermute(other, "brick_2", swap)
    shard = lax.all_to_all(mine, PLANE, 0, 0, tiled=True).sum(axis=0)
    shard = from_everyone(shard, "brick_1").sum(axis=0)
    mine = from_everyone(shard, PLANE)
    other = lax.ppermute(mine, "brick_2", swap)

    bound = bound.reshape(NB, 128)
    square = sds((M, M))
    vector = sds((NB, 128))
    hess, inv, scale, lam, part = call(
        solve_kernel,
        [SM, VM, VM, VM, VM, VM, VM],
        [square, square, vector, vector, vector],
        [pltpu.VMEM((2, *packed), F32), pltpu.VMEM((M, M), F32), pltpu.VMEM((16, M), F32)],
        32,
        "solve",
    )(at, mine, other, full, curv, lin, bound)
    for _ in range(ITERS - 2):
        lam, part = call(
            step_kernel, [VM] * 9, [vector, vector], [pltpu.VMEM((16, M), F32)], 24, "step"
        )(summed(part), lam, full, curv, lin, bound, hess, inv, scale)
    lam, result = call(
        last_kernel, [VM] * 9, [vector, sds((BLKS, 128))], [], 24, "last"
    )(summed(part), lam, full, curv, lin, bound, hess, inv, scale)

    whole = from_everyone(result, "grp").reshape(per_brick, 128)
    arrived = lax.all_to_all(whole[outgoing], BRICK, 0, 0, tiled=True)
    place = lax.dynamic_slice_in_dim(place, quarter * BLKS, BLKS)
    return (arrived[place].reshape(-1), lam.reshape(-1))


def solution(mesh):
    torus = Mesh(
        mesh.devices.reshape(4, 8, 2, mesh.shape["grp"]), ("brick_0", "brick_1", "brick_2", "grp")
    )
    placed = (P("grp", BRICK), P(), P(BRICK_GRP), P(BRICK_GRP), P())
    return jax.shard_map(
        on_device, mesh=torus, in_specs=placed, out_specs=(P(BRICK_GRP), P()), check_vma=False
    )
```

time: 510 us -> 252 us (0.49); the launches traced: 503 us -> 251 us
  other arithmetic: 141 us -> 14.9 us
  waiting for transfers between devices: 111 us -> 61.7 us
  matrix products: 45.3 us -> 0 us
  local copies, waits for them, and re-layouts: 65 us -> 24.3 us
  starting transfers between devices: 64.3 us -> 40.5 us
  Pallas kernels: 0 us -> 23.3 us
  blocking collectives: 73 us -> 85.4 us
    another operation x23 -> x1, other arithmetic: 119 us -> 0.07 us  [on_device(): at = jnp.stack([quarter, core]).astype(jnp.int32)]
    all_to_all x5 -> x2, waiting for transfers between devices: 72.8 us -> 20 us  [the longest x1 10.2 us: on_device(): back = lax.all_to_all(both[arrival], BRICK, 0, 0, tiled=True)[inverse]]
    dot_general x10 -> x0, matrix products: 31.8 us -> none  [the longest x5 17.1 us: trial(): pushed = jnp.dot(lam_b, full, preferred_element_type=jnp.float32)]
    pallas_call x0 -> x5, Pallas kernels: none -> 23.3 us  [the longest x1 11.8 us: on_device(): call(solve_kernel, [SM, VM, VM, VM, VM, VM, VM], [square, square, vector,...]
    all_to_all x5 -> x2, starting transfers between devices: 41.2 us -> 19.9 us  [the longest x1 13.2 us: on_device(): back = lax.all_to_all(both[arrival], BRICK, 0, 0, tiled=True)[inverse]]
    reshape x3 -> x0, local copies, waits for them, and re-layouts: 14.5 us -> none  [the longest x1 7.49 us: on_device(): full = full.reshape(full.shape[0], per_quarter * 128)]
    all_to_all x0 -> x1, blocking collectives: none -> 14.1 us  [on_device(): shard = lax.all_to_all(mine, PLANE, 0, 0, tiled=True).sum(axis=0)]
    another operation x62 -> x0, matrix products: 13.5 us -> none  [the longest x56 11.6 us: on_device(): jax.scipy.linalg.cho_solve((chol, True), product / ncols - bound)]
  transfers between devices with their start and end apart: 10 -> 10, of which waited for: 9 -> 7; matrix products, arithmetic and copies ran while one was open for 5% -> 7% of each run, Pallas kernels for 0% -> 0%
where the time goes in v1:
time: 252 us; the launch traced here: 251 us
  blocking collectives  85.4 us (34%)
  waiting for transfers between devices  61.7 us (24%)
  starting transfers between devices  40.5 us (16%)
  local copies, waits for them, and re-layouts  24.3 us (10%)
  Pallas kernels  23.3 us (9%)
  other arithmetic  14.9 us (6%)
    all_to_all x7, blocking collectives, from_everyone(): lax.all_to_all(jnp.broadcast_to(array[None], (devices, *array.shape)), ax...  71.3 us
    all_to_all x3, waiting for transfers between devices, from_everyone(): lax.all_to_all(jnp.broadcast_to(array[None], (devices, *array.shape)), ax...  39.1 us
    all_to_all x1, blocking collectives, on_device(): shard = lax.all_to_all(mine, PLANE, 0, 0, tiled=True).sum(axis=0)  14.1 us
    all_to_all x1, starting transfers between devices, on_device(): back = lax.all_to_all(both[arrival], BRICK, 0, 0, tiled=True)[inverse]  13.2 us
    unnamed x20, local copies, waits for them, and re-layouts  12.9 us
    pallas_call x1, Pallas kernels, on_device(): call(solve_kernel, [SM, VM, VM, VM, VM, VM, VM], [square, square, vector,...  11.8 us
    all_to_all x3, starting transfers between devices, from_everyone(): lax.all_to_all(jnp.broadcast_to(array[None], (devices, *array.shape)), ax...  10.5 us
    all_to_all x1, waiting for transfers between devices, on_device(): back = lax.all_to_all(both[arrival], BRICK, 0, 0, tiled=True)[inverse]  10.2 us
  transfers between devices with their start and end apart: 10, of which 7 were waited for; matrix products, arithmetic and copies ran while one was open for 7% of the time, Pallas kernels for 0%

profile of v1, /device:TPU:1, one launch (start us, length us, event | category | flops | bytes accessed | tf_op | source)
XLA Modules:
  0.0 251.0 jit_solution(8439199007835329448)
XLA Ops:
  0.7 3.6 %constant_dynamic-slice_fusion = (bf16[128,4096]{1,0:T(8,128)(2,1)}, bf16[128,4096]{1,0:T(8,128)(2,1)}, bf16[128,4096]{1,0:T(8,128)(2,1)}) fusion(bf16[128,16384]{1,0:T(8,128)(2,1)} %own_hbm.1, s32[]{:T(128)S(6)} %select_n.69, s32[]{:T(128)S(6)} %select_n.68, s32[]{:T(128)S(6)} %select_n.67), kind=kLoop, calls=%fused_computation.35 | loop fusion | bytes 6291468 | tf_op jit(solution)/shard_map/dynamic_slice | solution.py:374
  6.3 2.5 collective-permute-start.1
  10.6 3.3 %all-to-all-start = ((f32[4,32,256]{2,1,0:T(8,128)}), f32[4,32,256]{2,1,0:T(8,128)S(1)}, u32[]{:S(2)}, u32[]{:S(2)}) async-start(f32[4,32,256]{2,1,0:T(8,128)} %broadcast_in_dim.28), calls=%async_computation | async-start | bytes 262144 | tf_op jit(solution)/shard_map/all_to_all | solution.py:44
  14.0 6.8 %sort.63 = (s32[8192]{0:T(1024)}, s32[8192]{0:T(1024)S(1)}) sort(s32[8192]{0:T(1024)S(1)} %add_select_fusion.1, s32[8192]{0:T(1024)S(1)} %iota.26), dimensions={0}, to_apply=%region_1.2 | sort | flops 106496 | bytes 131072 | tf_op jit(solution)/shard_map/jit(argsort)/sort | solution.py:54
  22.0 2.5 %sort.64 = (s32[128]{0:T(128)}, s32[128]{0:T(128)S(1)}) sort(s32[128]{0:T(128)S(1)} %and_select_fusion.1, s32[128]{0:T(128)S(1)} %iota.27), dimensions={0}, to_apply=%region_2.3 | sort | flops 896 | bytes 2048 | tf_op jit(solution)/shard_map/jit(argsort)/sort | solution.py:380
  24.6 2.5 %sort.62 = (s32[128]{0:T(128)}, s32[128]{0:T(128)S(1)}) sort(s32[128]{0:T(128)S(1)} %get-tuple-element.44, s32[128]{0:T(128)S(1)} %iota.23), dimensions={0}, to_apply=%region_0.1 | sort | flops 896 | bytes 2048 | tf_op jit(solution)/shard_map/jit(argsort)/sort | solution.py:58
  27.1 28.3 %all-to-all-done = f32[4,32,256]{2,1,0:T(8,128)S(1)} async-done(((f32[4,32,256]{2,1,0:T(8,128)}), f32[4,32,256]{2,1,0:T(8,128)S(1)}, u32[]{:S(2)}, u32[]{:S(2)}) %all-to-all-start) | async-done | bytes 131104 | tf_op jit(solution)/shard_map/all_to_all | solution.py:44
  56.9 13.2 %all-to-all-start.1 = ((f32[64,2,256]{2,1,0:T(2,128)}), f32[64,2,256]{2,1,0:T(2,128)S(1)}, u32[]{:S(2)}, u32[]{:S(2)}) async-start(f32[64,2,256]{2,1,0:T(2,128)} %all_to_all.50), calls=%async_computation.1 | async-start | bytes 262144 | tf_op jit(solution)/shard_map/all_to_all | solution.py:383
  70.3 10.2 %all-to-all-done.1 = f32[64,2,256]{2,1,0:T(2,128)S(1)} async-done(((f32[64,2,256]{2,1,0:T(2,128)}), f32[64,2,256]{2,1,0:T(2,128)S(1)}, u32[]{:S(2)}, u32[]{:S(2)}) %all-to-all-start.1) | async-done | bytes 131104 | tf_op jit(solution)/shard_map/all_to_all | solution.py:383
  83.4 4.3 %gram.1 = (bf16[4,128,4096]{2,1,0:T(8,128)(2,1)S(1)}, f32[16,48,128]{2,1,0:T(8,128)S(1)}, f32[16,48,128]{2,1,0:T(8,128)S(1)}) custom-call(s32[2]{0:T(128)S(1)} %pad_add_fusion.at_ref, bf16[128,16384]{1,0:T(8,128)(2,1)S(1)} %copy-done.5, bf16[128,4096]{1,0:T(8,128)(2,1)S(1)} %collective-permute-done.one_hbm, ...), custom_call_target="tpu_custom_call" | custom-call | tf_op jit(solution)/shard_map/gram/pallas_call | solution.py:387
  91.4 14.1 %all_to_all.79 = f32[16,48,128]{2,1,0:T(8,128)S(1)} all-to-all(f32[16,48,128]{2,1,0:T(8,128)S(1)} %add.103), channel_id=1, replica_groups=mesh['brick_0'=4,'brick_1'=8,'brick_2'=2,'grp'=4] {'brick_0','grp'}, dimensions={0} | all-to-all | bytes 786432 | tf_op jit(solution)/shard_map/all_to_all | solution.py:404
  105.5 10.9 %all_to_all.80 = f32[8,48,128]{2,1,0:T(8,128)S(1)} all-to-all(f32[8,48,128]{2,1,0:T(8,128)S(1)} %broadcast_in_dim.32), channel_id=1, replica_groups=mesh['brick_0'=4,'brick_1'=8,'brick_2'=2,'grp'=4] {'brick_1'}, dimensions={0} | all-to-all | bytes 393216 | tf_op jit(solution)/shard_map/all_to_all | solution.py:44
  116.5 11.4 %all_to_all.81.mine_ref = f32[16,48,128]{2,1,0:T(8,128)S(1)} all-to-all(f32[16,48,128]{2,1,0:T(8,128)S(1)} %broadcast_in_dim.33), channel_id=1, replica_groups=mesh['brick_0'=4,'brick_1'=8,'brick_2'=2,'grp'=4] {'brick_0','grp'}, dimensions={0} | all-to-all | bytes 786432 | tf_op jit(solution)/shard_map/all_to_all | solution.py:44
  127.8 4.1 %collective-permute-start.4 = (f32[16,48,128]{2,1,0:T(8,128)S(1)}, f32[16,48,128]{2,1,0:T(8,128)S(1)}, u32[]{:S(2)}, u32[]{:S(2)}) collective-permute-start(f32[16,48,128]{2,1,0:T(8,128)S(1)} %all_to_all.81.mine_ref), channel_id=1, source_target_pairs={{0,4},{4,0},{1,5},{5,1},{2,6},{6,2},{3,7},{7,3},{8,12},{12,8},{9,1... | collective-permute-start | bytes 1179656 | tf_op jit(solution)/shard_map/ppermute | solution.py:407
  133.3 2.2 copy-done.1
  135.5 11.8 %solve.1 = (f32[512,512]{1,0:T(8,128)S(1)}, f32[512,512]{1,0:T(8,128)S(1)}, f32[4,128]{1,0:T(4,128)S(1)}, f32[4,128]{1,0:T(4,128)S(1)}, f32[4,128]{1,0:T(4,128)S(1)}) custom-call(s32[2]{0:T(128)S(1)} %pad_add_fusion.at_ref, f32[16,48,128]{2,1,0:T(8,128)S(1)} %all_to_all.81.mine_ref, f32[16,48,128]{2,1,0:T(8,128)S(1)} %collective-permute-done.4.other_ref, ...), custom_call_target="tpu_custom_call" | custom-call | tf_op jit(solution)/shard_map/solve/pallas_call | solution.py:412
  147.4 7.6 %all_to_all.82 = f32[8,4,128]{2,1,0:T(4,128)S(1)} all-to-all(f32[8,4,128]{2,1,0:T(4,128)S(1)} %broadcast_in_dim.34), channel_id=1, replica_groups=mesh['brick_0'=4,'brick_1'=8,'brick_2'=2,'grp'=4] {'brick_2','grp'}, dimensions={0} | all-to-all | bytes 32768 | tf_op jit(solution)/shard_map/all_to_all | solution.py:44
  155.0 11.8 %all_to_all.83.gathered_ref = f32[32,4,128]{2,1,0:T(4,128)S(1)} all-to-all(f32[32,4,128]{2,1,0:T(4,128)S(1)} %broadcast_in_dim.35), channel_id=1, replica_groups=mesh['brick_0'=4,'brick_1'=8,'brick_2'=2,'grp'=4] {'brick_0','brick_1'}, dimensions={0} | all-to-all | bytes 131072 | tf_op jit(solution)/shard_map/all_to_all | solution.py:44
  166.9 2.2 copy-done.2
  169.0 2.9 %step.2 = (f32[4,128]{1,0:T(4,128)S(1)}, f32[4,128]{1,0:T(4,128)S(1)}) custom-call(f32[32,4,128]{2,1,0:T(4,128)S(1)} %all_to_all.83.gathered_ref, f32[4,128]{1,0:T(4,128)S(1)} %get-tuple-element.27.lam_in_ref, bf16[4,128,4096]{2,1,0:T(8,128)(2,1)S(1)} %copy-done.2, f32[32,128]{1,0:T(8,128)S(1)} %get-tuple-element.42.curv_ref, ...), custom_call_target="tpu_custom_call" | custom-call | tf_op jit(solution)/shard_map/step/pallas_call | solution.py:421
  171.9 8.8 %all_to_all.84 = f32[8,4,128]{2,1,0:T(4,128)S(1)} all-to-all(f32[8,4,128]{2,1,0:T(4,128)S(1)} %broadcast_in_dim.36), channel_id=1, replica_groups=mesh['brick_0'=4,'brick_1'=8,'brick_2'=2,'grp'=4] {'brick_2','grp'}, dimensions={0} | all-to-all | bytes 32768 | tf_op jit(solution)/shard_map/all_to_all | solution.py:44
  180.8 11.9 %all_to_all.85.gathered_ref = f32[32,4,128]{2,1,0:T(4,128)S(1)} all-to-all(f32[32,4,128]{2,1,0:T(4,128)S(1)} %broadcast_in_dim.37), channel_id=1, replica_groups=mesh['brick_0'=4,'brick_1'=8,'brick_2'=2,'grp'=4] {'brick_0','brick_1'}, dimensions={0} | all-to-all | bytes 131072 | tf_op jit(solution)/shard_map/all_to_all | solution.py:44
  192.7 2.2 copy-done.3
  194.8 2.9 %step.3 = (f32[4,128]{1,0:T(4,128)S(1)}, f32[4,128]{1,0:T(4,128)S(1)}) custom-call(f32[32,4,128]{2,1,0:T(4,128)S(1)} %all_to_all.85.gathered_ref, f32[4,128]{1,0:T(4,128)S(1)} %get-tuple-element.32.lam_in_ref, bf16[4,128,4096]{2,1,0:T(8,128)(2,1)S(1)} %copy-done.3, f32[32,128]{1,0:T(8,128)S(1)} %get-tuple-element.42.curv_ref, ...), custom_call_target="tpu_custom_call" | custom-call | tf_op jit(solution)/shard_map/step/pallas_call | solution.py:421
  197.8 8.9 %all_to_all.86 = f32[8,4,128]{2,1,0:T(4,128)S(1)} all-to-all(f32[8,4,128]{2,1,0:T(4,128)S(1)} %broadcast_in_dim.38), channel_id=1, replica_groups=mesh['brick_0'=4,'brick_1'=8,'brick_2'=2,'grp'=4] {'brick_2','grp'}, dimensions={0} | all-to-all | bytes 32768 | tf_op jit(solution)/shard_map/all_to_all | solution.py:44
  207.3 3.8 %all-to-all-start.10 = ((f32[32,4,128]{2,1,0:T(4,128)}), f32[32,4,128]{2,1,0:T(4,128)S(1)}, u32[]{:S(2)}, u32[]{:S(2)}) async-start(f32[32,4,128]{2,1,0:T(4,128)} %broadcast_in_dim.39), calls=%async_computation.10 | async-start | bytes 131072 | tf_op jit(solution)/shard_map/all_to_all | solution.py:44
  211.2 8.9 %all-to-all-done.10.gathered_ref = f32[32,4,128]{2,1,0:T(4,128)S(1)} async-done(((f32[32,4,128]{2,1,0:T(4,128)}), f32[32,4,128]{2,1,0:T(4,128)S(1)}, u32[]{:S(2)}, u32[]{:S(2)}) %all-to-all-start.10) | async-done | bytes 65568 | tf_op jit(solution)/shard_map/all_to_all | solution.py:44
  220.1 2.2 copy-done.4
  224.3 3.3 %all-to-all-start.11 = ((f32[4,32,128]{2,1,0:T(8,128)}), f32[4,32,128]{2,1,0:T(8,128)S(1)}, u32[]{:S(2)}, u32[]{:S(2)}) async-start(f32[4,32,128]{2,1,0:T(8,128)} %broadcast_in_dim.40), calls=%async_computation.11 | async-start | bytes 131072 | tf_op jit(solution)/shard_map/all_to_all | solution.py:44
  227.6 2.5 %sort.65 = (s32[128]{0:T(128)}, s32[128]{0:T(128)S(1)}) sort(s32[128]{0:T(128)S(1)} %get-tuple-element.20, s32[128]{0:T(128)S(1)} %iota.28), dimensions={0}, to_apply=%region_8.9 | sort | flops 896 | bytes 2048 | tf_op jit(solution)/shard_map/jit(argsort)/sort | solution.py:59
  233.2 6.7 %all-to-all-start.12 = ((f32[64,2,128]{2,1,0:T(2,128)}), f32[64,2,128]{2,1,0:T(2,128)S(1)}, u32[]{:S(2)}, u32[]{:S(2)}) async-start(f32[64,2,128]{2,1,0:T(2,128)} %bitcast.9), calls=%async_computation.12 | async-start | bytes 131072 | tf_op jit(solution)/shard_map/all_to_all | solution.py:429
  240.1 9.8 %all-to-all-done.12 = f32[64,2,128]{2,1,0:T(2,128)S(1)} async-done(((f32[64,2,128]{2,1,0:T(2,128)}), f32[64,2,128]{2,1,0:T(2,128)S(1)}, u32[]{:S(2)}, u32[]{:S(2)}) %all-to-all-start.12) | async-done | bytes 65568 | tf_op jit(solution)/shard_map/all_to_all | solution.py:429
  (68 shorter events, 22.0 us)
Async XLA Ops:
  0.6 9.3 %copy-start.9 = (f32[4096]{0:T(1024)S(1)}, f32[4096]{0:T(1024)}, u32[]{:S(2)}) copy-start(f32[4096]{0:T(1024)} %param.7) | copy-start | bytes 49156
  0.6 9.3 %copy-start.8 = (f32[4096]{0:T(1024)S(1)}, f32[4096]{0:T(1024)}, u32[]{:S(2)}) copy-start(f32[4096]{0:T(1024)} %param.8) | copy-start | bytes 49156
  0.7 13.3 %copy-start.7 = (s32[8192]{0:T(1024)S(1)}, s32[8192]{0:T(1024)}, u32[]{:S(2)}) copy-start(s32[8192]{0:T(1024)} %param.6) | copy-start | bytes 98308
  4.3 76.9 %collective-permute-start = (bf16[128,4096]{1,0:T(8,128)(2,1)}, bf16[128,4096]{1,0:T(8,128)(2,1)S(1)}, u32[]{:S(2)}, u32[]{:S(2)}) collective-permute-start(bf16[128,4096]{1,0:T(8,128)(2,1)} %get-tuple-element.40), channel_id=1, source_target_pairs={{0,1},{1,2},{2,3},{3,0},{4,5},{5,6},{6,7},{7,4},{8,9},{9,10},{10,1... | collective-permute-start | bytes 3145736 | tf_op jit(solution)/shard_map/ppermute | solution.py:375
  6.3 74.8 %collective-permute-start.1 = (bf16[128,4096]{1,0:T(8,128)(2,1)}, bf16[128,4096]{1,0:T(8,128)(2,1)S(1)}, u32[]{:S(2)}, u32[]{:S(2)}) collective-permute-start(bf16[128,4096]{1,0:T(8,128)(2,1)} %get-tuple-element.39), channel_id=1, source_target_pairs={{0,2},{1,3},{2,0},{3,1},{4,6},{5,7},{6,4},{7,5},{8,10},{9,11},{10,... | collective-permute-start | bytes 3145736 | tf_op jit(solution)/shard_map/ppermute | solution.py:375
  8.8 72.4 %collective-permute-start.2 = (bf16[128,4096]{1,0:T(8,128)(2,1)}, bf16[128,4096]{1,0:T(8,128)(2,1)S(1)}, u32[]{:S(2)}, u32[]{:S(2)}) collective-permute-start(bf16[128,4096]{1,0:T(8,128)(2,1)} %get-tuple-element.38), channel_id=1, source_target_pairs={{0,3},{1,0},{2,1},{3,2},{4,7},{5,4},{6,5},{7,6},{8,11},{9,8},{10,9... | collective-permute-start | bytes 3145736 | tf_op jit(solution)/shard_map/ppermute | solution.py:375
  10.6 44.8 %all-to-all-start = ((f32[4,32,256]{2,1,0:T(8,128)}), f32[4,32,256]{2,1,0:T(8,128)S(1)}, u32[]{:S(2)}, u32[]{:S(2)}) async-start(f32[4,32,256]{2,1,0:T(8,128)} %broadcast_in_dim.28), calls=%async_computation | async-start | bytes 262144 | tf_op jit(solution)/shard_map/all_to_all | solution.py:44
  56.9 23.5 %all-to-all-start.1 = ((f32[64,2,256]{2,1,0:T(2,128)}), f32[64,2,256]{2,1,0:T(2,128)S(1)}, u32[]{:S(2)}, u32[]{:S(2)}) async-start(f32[64,2,256]{2,1,0:T(2,128)} %all_to_all.50), calls=%async_computation.1 | async-start | bytes 262144 | tf_op jit(solution)/shard_map/all_to_all | solution.py:383
  81.2 2.2 copy-start.5
  83.4 49.9 %copy-start.6 = (f32[512]{0:T(512)S(1)}, f32[512]{0:T(512)}, u32[]{:S(2)}) copy-start(f32[512]{0:T(512)} %param.9) | copy-start | bytes 6148
  87.7 1.9 copy-start
  89.6 1.7 collective-permute-start.3
  127.8 5.5 %collective-permute-start.4 = (f32[16,48,128]{2,1,0:T(8,128)S(1)}, f32[16,48,128]{2,1,0:T(8,128)S(1)}, u32[]{:S(2)}, u32[]{:S(2)}) collective-permute-start(f32[16,48,128]{2,1,0:T(8,128)S(1)} %all_to_all.81.mine_ref), channel_id=1, source_target_pairs={{0,4},{4,0},{1,5},{5,1},{2,6},{6,2},{3,7},{7,3},{8,12},{12,8},{9,1... | collective-permute-start | bytes 1179656 | tf_op jit(solution)/shard_map/ppermute | solution.py:407
  133.3 2.2 copy-start.1
  166.9 2.2 copy-start.2
  192.7 2.2 copy-start.3
  207.3 12.7 %all-to-all-start.10 = ((f32[32,4,128]{2,1,0:T(4,128)}), f32[32,4,128]{2,1,0:T(4,128)S(1)}, u32[]{:S(2)}, u32[]{:S(2)}) async-start(f32[32,4,128]{2,1,0:T(4,128)} %broadcast_in_dim.39), calls=%async_computation.10 | async-start | bytes 131072 | tf_op jit(solution)/shard_map/all_to_all | solution.py:44
  220.1 2.2 copy-start.4
  224.3 7.7 %all-to-all-start.11 = ((f32[4,32,128]{2,1,0:T(8,128)}), f32[4,32,128]{2,1,0:T(8,128)S(1)}, u32[]{:S(2)}, u32[]{:S(2)}) async-start(f32[4,32,128]{2,1,0:T(8,128)} %broadcast_in_dim.40), calls=%async_computation.11 | async-start | bytes 131072 | tf_op jit(solution)/shard_map/all_to_all | solution.py:44
  233.2 16.6 %all-to-all-start.12 = ((f32[64,2,128]{2,1,0:T(2,128)}), f32[64,2,128]{2,1,0:T(2,128)S(1)}, u32[]{:S(2)}, u32[]{:S(2)}) async-start(f32[64,2,128]{2,1,0:T(2,128)} %bitcast.9), calls=%async_computation.12 | async-start | bytes 131072 | tf_op jit(solution)/shard_map/all_to_all | solution.py:429

commit v2 on v1

v2 whole, which is shorter than its diff:
```python
import functools

import jax
import jax.numpy as jnp
from jax import lax
from jax.experimental import pallas as pl
from jax.experimental.pallas import tpu as pltpu
from jax.sharding import Mesh
from jax.sharding import PartitionSpec as P

ITERS = 4
BRICK = ("brick_0", "brick_1", "brick_2")
BRICK_GRP = ("brick_0", "brick_1", "brick_2", "grp")
FAR = ("brick_0", "brick_1")
NEAR = ("brick_2", "grp")
PLANE = ("brick_0", "grp")
M = 512
ROWS = 128
NB = M // ROWS
COLS = 4096
BLKS = COLS // 128
NVAR = 1048576
PAIRS = [(i, j) for i in range(NB) for j in range(i + 1)]
SHARDS = 32
SHARD_G = len(PAIRS) * ROWS // SHARDS
SHARD = SHARD_G + 8
HALF = SHARDS // 2
DOUBLINGS = 5
MAX_CORRECT = 48
ACCEPT = 1e-4

move_limit = 1.0
MIB = 1024 * 1024
BF = jnp.bfloat16
F32 = jnp.float32


def size_of(axis):
    return lax.axis_size(axis)


def from_everyone(array, axis):
    devices = size_of(axis)
    return lax.all_to_all(
        jnp.broadcast_to(array[None], (devices, *array.shape)), axis, 0, 0, tiled=True
    )


def first_of(mask, values, count):
    index = lax.broadcasted_iota(jnp.int32, values.shape, 1)
    _, kept = lax.sort_key_val(jnp.where(mask, index, index + values.shape[1]), values)
    return kept[:, :count]


def ranks(keys):
    return jnp.sum(keys[None, :] < keys[:, None], axis=1, dtype=jnp.int32)


def inverted(places, count):
    slots = jnp.arange(count, dtype=jnp.int32)
    index = jnp.arange(places.shape[0], dtype=jnp.int32)
    return jnp.sum(jnp.where(places[None, :] == slots[:, None], index[None, :], 0), axis=1)


def layout_tables(perm, here, per_brick):
    chip, core = here // 2, here % 2
    per_chip = 2 * per_brick
    grid = perm.reshape(-1, per_brick)
    incoming = first_of(grid // per_brick == here, grid, 2).reshape(-1) % per_brick
    local = lax.dynamic_slice_in_dim(perm, chip * per_chip, per_chip)
    index = jnp.arange(per_chip, dtype=jnp.int32)
    key = (local // per_chip) * per_chip + index
    key = jnp.where((local // per_brick) % 2 == core, key, key + perm.shape[0] * 2)
    leaving = inverted(ranks(key), per_brick)
    same = lax.dynamic_index_in_dim(grid.reshape(-1, 2, per_brick), core, 1, keepdims=False)
    back = first_of(same // per_chip == chip, same, 4).reshape(-1) % per_chip
    mine = lax.dynamic_slice_in_dim(perm, here * per_brick, per_brick)
    place = ranks((mine // per_chip) * per_brick + jnp.arange(per_brick, dtype=jnp.int32))
    return (inverted(incoming, per_brick), leaving, back, place)


def down(row):
    return jnp.broadcast_to(row, (128, 128)).T


def times(mat_ref, vec):
    total = [jnp.zeros((8, 128), F32) for _ in range(NB)]
    for i in range(NB):
        column = down(vec[i : i + 1, :])
        for j in range(NB):
            part = mat_ref[i * 128 : (i + 1) * 128, j * 128 : (j + 1) * 128] * column
            total[j] = total[j] + part.reshape(16, 8, 128).sum(axis=0)
    return jnp.concatenate([t.sum(axis=0, keepdims=True) for t in total], axis=0)


WIDTH = 1024
CHUNKS = COLS // WIDTH
NT = (((1,), (1,)), ((), ()))


def flat_rows(ref, chunk):
    count = WIDTH // 128
    rows = [ref[chunk * count + k : chunk * count + k + 1, :] for k in range(count)]
    return jnp.concatenate(rows, axis=1)


class Columns:
    def __init__(self, at_ref, pieces, full_ref, sems):
        quarter = at_ref[0]
        self.full_ref = full_ref
        self.copies = []
        for chunk in range(CHUNKS):
            to = pl.ds(chunk * WIDTH, WIDTH)
            own = pl.ds(pl.multiple_of(quarter * COLS + chunk * WIDTH, WIDTH), WIDTH)
            self.copies.append(
                [
                    pltpu.make_async_copy(
                        piece.at[:, own if k == 0 else to],
                        full_ref.at[lax.rem(quarter + 4 - k, 4), :, to],
                        sems.at[chunk, k],
                    )
                    for k, piece in enumerate(pieces)
                ]
            )

    def start(self):
        for group in self.copies:
            for copy in group:
                copy.start()

    def chunk(self, chunk):
        for copy in self.copies[chunk]:
            copy.wait()
        return self.full_ref[:, :, chunk * WIDTH : (chunk + 1) * WIDTH].reshape(M, WIDTH)


def as_rows(lam):
    flat = jnp.concatenate([lam[i : i + 1, :] for i in range(NB)], axis=1)
    return jnp.broadcast_to(flat, (16, M)).astype(BF)


def as_lines(flat):
    return jnp.concatenate([flat[:, i * 128 : (i + 1) * 128] for i in range(NB)], axis=0)


def trial_chunk(block, curv_ref, lin_ref, lam_b, chunk):
    pushed = jnp.dot(lam_b, block, preferred_element_type=F32)
    curv, lin = flat_rows(curv_ref, chunk), flat_rows(lin_ref, chunk)
    return jnp.clip(-curv * (lin + pushed), -move_limit, move_limit)


def product_of_trial(columns, curv_ref, lin_ref, lam):
    lam_b = as_rows(lam)
    total = jnp.zeros((16, M), F32)
    for chunk in range(CHUNKS):
        block = columns.chunk(chunk)
        moved = trial_chunk(block, curv_ref, lin_ref, lam_b, chunk).astype(BF)
        total += lax.dot_general(moved, block, NT, preferred_element_type=F32)
    return as_lines(total[0:1, :])


def newton_update(lam, total, bound, inv_ref, scale):
    rhs = (total * (1.0 / NVAR) - bound) * scale
    return jnp.maximum(lam + times(inv_ref, rhs) * scale, 0.0)


def packed_tile(p, t):
    tile = p * 16 + t
    shard, row = tile // (SHARD_G // 8), tile % (SHARD_G // 8) * 8
    return shard // HALF, shard % HALF, slice(row, row + 8)


def gram_kernel(
    at_ref, own_hbm, one_hbm, two_hbm, three_hbm, curv_ref, lin_ref,
    mine_ref, other_ref, full_ref, gram_ref, prod_ref, half_ref, sems,
):
    core = at_ref[1]
    columns = Columns(at_ref, (own_hbm, one_hbm, two_hbm, three_hbm), full_ref, sems)
    columns.start()
    gram_ref[...] = jnp.zeros_like(gram_ref)
    prod_ref[...] = jnp.zeros_like(prod_ref)
    for s in range(SHARDS):
        half_ref[s // HALF, s % HALF, SHARD_G:, :] = jnp.zeros((8, 128), F32)
    for chunk in range(CHUNKS):
        block = columns.chunk(chunk)
        curv, lin = flat_rows(curv_ref, chunk), flat_rows(lin_ref, chunk)
        weighted = (block.astype(F32) * curv).astype(BF)
        gram_ref[...] += lax.dot_general(weighted, block, NT, preferred_element_type=F32)
        moved = jnp.clip(-curv * lin, -move_limit, move_limit)
        moved = jnp.broadcast_to(moved, (16, WIDTH)).astype(BF)
        prod_ref[...] += lax.dot_general(moved, block, NT, preferred_element_type=F32)
    for j in range(NB):
        half_ref[0, j, SHARD_G : SHARD_G + 1, :] = prod_ref[0:1, j * 128 : (j + 1) * 128]
    for p, (i, j) in enumerate(PAIRS):
        rows, cols = slice(i * 128, (i + 1) * 128), slice(j * 128, (j + 1) * 128)
        value = 0.5 * (gram_ref[rows, cols] + gram_ref[cols, rows].T)
        for t in range(16):
            half_ref[packed_tile(p, t)] = value[t * 8 : t * 8 + 8]
    mine_ref[...] = half_ref[core]
    other_ref[...] = half_ref[1 - core]


def split(value):
    high = value.astype(BF)
    return high, (value - high.astype(F32)).astype(BF)


def times_split(a_high, a_low, b_high, b_low):
    dot = functools.partial(jnp.dot, preferred_element_type=F32)
    return dot(a_high, b_high) + (dot(a_high, b_low) + dot(a_low, b_high))


def solve_kernel(
    at_ref, own_hbm, one_hbm, two_hbm, three_hbm, mine_ref, other_ref, curv_ref, lin_ref, bound_ref,
    inv_ref, scale_ref, lam_ref, part_ref,
    full_ref, half_ref, hess_ref, r_ref, sems,
):
    columns = Columns(at_ref, (own_hbm, one_hbm, two_hbm, three_hbm), full_ref, sems)
    columns.start()
    core = at_ref[1]
    half_ref[core] = mine_ref[...]
    half_ref[1 - core] = other_ref[...]
    for p, (i, j) in enumerate(PAIRS):
        for t in range(16):
            at = i * 128 + t * 8
            hess_ref[at : at + 8, j * 128 : (j + 1) * 128] = half_ref[packed_tile(p, t)] * (
                1.0 / NVAR
            )
    row_id = lax.broadcasted_iota(jnp.int32, (128, 128), 0)
    col_id = lax.broadcasted_iota(jnp.int32, (128, 128), 1)
    diagonal = row_id == col_id
    for i in range(NB):
        at = slice(i * 128, (i + 1) * 128)
        for j in range(i):
            hess_ref[j * 128 : (j + 1) * 128, at] = hess_ref[at, j * 128 : (j + 1) * 128].T
        values = jnp.sum(jnp.where(diagonal, hess_ref[at, at], 0.0), axis=0, keepdims=True)
        scale_ref[i : i + 1, :] = lax.rsqrt(values)
    scale = scale_ref[...]
    scale_row = jnp.concatenate([scale[i : i + 1, :] for i in range(NB)], axis=1)
    widest = jnp.zeros((1, M), F32)
    for i in range(NB):
        at = slice(i * 128, (i + 1) * 128)
        column = jnp.concatenate([down(scale[i : i + 1, :])] * NB, axis=1)
        rows = hess_ref[at, :] * column * scale_row
        hess_ref[at, :] = rows
        widest = widest + jnp.sum(jnp.abs(rows), axis=0, keepdims=True)
    alpha = 1.9 / jnp.max(widest)

    def eye():
        rid = lax.broadcasted_iota(jnp.int32, (M, M), 0)
        cid = lax.broadcasted_iota(jnp.int32, (M, M), 1)
        return (rid == cid).astype(F32)

    first = eye() - alpha * hess_ref[...]
    r_ref[...] = first
    inv_ref[...] = alpha * (eye() + first)

    def double(_, carry):
        r = r_ref[...].astype(BF)
        r2 = jnp.dot(r, r, preferred_element_type=F32)
        r_ref[...] = r2
        inv_ref[...] += jnp.dot(
            inv_ref[...].astype(BF), r2.astype(BF), preferred_element_type=F32
        )
        return carry

    lax.fori_loop(0, DOUBLINGS - 1, double, 0)

    def correct(precise):
        x = inv_ref[...]
        x_high, x_low = split(x)
        if precise:
            product = jnp.dot(
                hess_ref[...], x, precision=lax.Precision.HIGHEST, preferred_element_type=F32
            )
        else:
            h_high, h_low = split(hess_ref[...])
            product = times_split(h_high, h_low, x_high, x_low)
        residual = eye() - product
        size = jnp.sum(residual * residual)
        good = size < M

        @pl.when(good)
        def _():
            r_high, r_low = split(residual)
            inv_ref[...] += times_split(x_high, x_low, r_high, r_low)

        @pl.when(jnp.logical_not(good))
        def _():
            inv_ref[...] = alpha * eye()

        return size

    def correct_again(state):
        return state[0] + 1, correct(True)

    def unfinished(state):
        count, size = state
        return jnp.logical_and(jnp.logical_not(size < ACCEPT), count < MAX_CORRECT)

    correct(False)
    _, size = lax.while_loop(unfinished, correct_again, (jnp.int32(0), jnp.float32(2.0 * M)))

    @pl.when(jnp.logical_not(size < ACCEPT))
    def _():
        inv_ref[...] = hess_ref[...]
        cid = lax.broadcasted_iota(jnp.int32, (8, M), 1)

        def pivot(k, carry):
            row = inv_ref[pl.ds(k, 1), :]
            here = lax.broadcasted_iota(jnp.int32, (1, M), 1) == k
            inverse = 1.0 / jnp.sum(jnp.where(here, row, 0.0))
            row = jnp.where(here, 1.0, row) * inverse

            def sweep(b, inner):
                at = pl.multiple_of(b * 8, 8)
                rows = inv_ref[pl.ds(at, 8), :]
                factor = jnp.sum(jnp.where(cid == k, rows, 0.0), axis=1, keepdims=True)
                rows = jnp.where(cid == k, 0.0, rows) - factor * row
                rid = lax.broadcasted_iota(jnp.int32, (8, M), 0) + at
                inv_ref[pl.ds(at, 8), :] = jnp.where(rid == k, row, rows)
                return inner

            lax.fori_loop(0, M // 8, sweep, 0)
            return carry

        lax.fori_loop(0, M, pivot, 0)

    total = jnp.concatenate(
        [half_ref[0, j, SHARD_G : SHARD_G + 1, :] for j in range(NB)], axis=0
    )
    zero = jnp.zeros((NB, 128), F32)
    lam = newton_update(zero, total, bound_ref[...], inv_ref, scale)
    lam_ref[...] = lam
    part_ref[...] = product_of_trial(columns, curv_ref, lin_ref, lam)


def updated(gathered_ref, lam_in_ref, bound_ref, inv_hbm, scale_ref, inv_ref, inv_sem):
    copy = pltpu.make_async_copy(inv_hbm, inv_ref, inv_sem)
    copy.start()
    return lambda: (
        copy.wait(),
        newton_update(
            lam_in_ref[...],
            jnp.sum(gathered_ref[...], axis=0),
            bound_ref[...],
            inv_ref,
            scale_ref[...],
        ),
    )[1]


def step_kernel(
    at_ref, own_hbm, one_hbm, two_hbm, three_hbm, inv_hbm,
    gathered_ref, lam_in_ref, curv_ref, lin_ref, bound_ref, scale_ref,
    lam_ref, part_ref, full_ref, inv_ref, sems, inv_sem,
):
    update = updated(gathered_ref, lam_in_ref, bound_ref, inv_hbm, scale_ref, inv_ref, inv_sem)
    columns = Columns(at_ref, (own_hbm, one_hbm, two_hbm, three_hbm), full_ref, sems)
    columns.start()
    lam = update()
    lam_ref[...] = lam
    part_ref[...] = product_of_trial(columns, curv_ref, lin_ref, lam)


def last_kernel(
    at_ref, own_hbm, one_hbm, two_hbm, three_hbm, inv_hbm,
    gathered_ref, lam_in_ref, curv_ref, lin_ref, bound_ref, scale_ref,
    lam_ref, step_ref, full_ref, inv_ref, sems, inv_sem,
):
    update = updated(gathered_ref, lam_in_ref, bound_ref, inv_hbm, scale_ref, inv_ref, inv_sem)
    columns = Columns(at_ref, (own_hbm, one_hbm, two_hbm, three_hbm), full_ref, sems)
    columns.start()
    lam = update()
    lam_ref[...] = lam
    lam_b = as_rows(lam)
    count = WIDTH // 128
    for chunk in range(CHUNKS):
        moved = trial_chunk(columns.chunk(chunk), curv_ref, lin_ref, lam_b, chunk)
        for k in range(count):
            at = chunk * count + k
            step_ref[at : at + 1, :] = moved[0:1, k * 128 : (k + 1) * 128]


VM = pl.BlockSpec(memory_space=pltpu.VMEM)
SM = pl.BlockSpec(memory_space=pltpu.SMEM)
ANY = pl.BlockSpec(memory_space=pl.ANY)


def sds(shape, dtype=F32):
    return jax.ShapeDtypeStruct(shape, dtype)


def call(kernel, ins, outs, scratch, mib, name):
    return pl.pallas_call(
        kernel,
        in_specs=ins,
        out_specs=[VM] * len(outs),
        out_shape=outs,
        scratch_shapes=scratch,
        compiler_params=pltpu.CompilerParams(vmem_limit_bytes=mib * MIB),
        name=name,
    )


def summed(part):
    near = from_everyone(part, NEAR).sum(axis=0)
    return from_everyone(near, FAR)


def on_device(gradients, perm, weights, linear, bound):
    here = lax.axis_index(BRICK)
    quarter = lax.axis_index("grp")
    core = lax.axis_index("brick_2")
    per_brick = gradients.shape[1] // 128
    at = jnp.stack([quarter, core]).astype(jnp.int32)

    both = jnp.concatenate([weights.reshape(BLKS, 128), linear.reshape(BLKS, 128)], axis=1)
    both = from_everyone(both, NEAR)

    slices = [
        lax.dynamic_slice(gradients, (0, lax.rem(quarter + k, 4) * COLS), (ROWS, COLS))
        for k in (1, 2, 3)
    ]
    *slices, both = lax.optimization_barrier((*slices, both))
    one, two, three = [
        lax.ppermute(piece, "grp", [(i, (i + k + 1) % 4) for i in range(4)])
        for k, piece in enumerate(slices)
    ]
    pieces = (gradients, one, two, three)

    incoming, leaving, back, place = layout_tables(perm, here, per_brick)
    incoming = lax.dynamic_slice_in_dim(incoming, quarter * BLKS, BLKS)
    place = lax.dynamic_slice_in_dim(place, quarter * BLKS, BLKS)
    both = lax.all_to_all(both.reshape(-1, 256)[leaving], FAR, 0, 0, tiled=True)[incoming]
    curv, lin, back, place = lax.optimization_barrier((both[:, :128], both[:, 128:], back, place))

    packed = (HALF, SHARD, 128)
    full = pltpu.VMEM((NB, ROWS, COLS), BF)
    sems = pltpu.SemaphoreType.DMA((CHUNKS, NB))
    mine, other = call(
        gram_kernel,
        [SM, ANY, ANY, ANY, ANY, VM, VM],
        [sds(packed), sds(packed)],
        [
            full,
            pltpu.VMEM((M, M), F32),
            pltpu.VMEM((16, M), F32),
            pltpu.VMEM((2, *packed), F32),
            sems,
        ],
        24,
        "gram",
    )(at, *pieces, curv, lin)

    swap = [(0, 1), (1, 0)]
    mine = mine + lax.ppermute(other, "brick_2", swap)
    shard = lax.all_to_all(mine, PLANE, 0, 0, tiled=True).sum(axis=0)
    shard = from_everyone(shard, "brick_1").sum(axis=0)
    mine = from_everyone(shard, PLANE)
    other = lax.ppermute(mine, "brick_2", swap)

    bound = bound.reshape(NB, 128)
    square = sds((M, M))
    vector = sds((NB, 128))
    inv, scale, lam, part = call(
        solve_kernel,
        [SM, ANY, ANY, ANY, ANY, VM, VM, VM, VM, VM],
        [square, vector, vector, vector],
        [
            full,
            pltpu.VMEM((2, *packed), F32),
            pltpu.VMEM((M, M), F32),
            pltpu.VMEM((M, M), F32),
            sems,
        ],
        32,
        "solve",
    )(at, *pieces, mine, other, curv, lin, bound)
    ins = [SM, ANY, ANY, ANY, ANY, ANY, VM, VM, VM, VM, VM, VM]
    scratch = [full, pltpu.VMEM((M, M), F32), sems, pltpu.SemaphoreType.DMA(())]
    for _ in range(ITERS - 2):
        lam, part = call(step_kernel, ins, [vector, vector], scratch, 24, "step")(
            at, *pieces, inv, summed(part), lam, curv, lin, bound, scale
        )
    lam, result = call(last_kernel, ins, [vector, sds((BLKS, 128))], scratch, 24, "last")(
        at, *pieces, inv, summed(part), lam, curv, lin, bound, scale
    )

    whole = from_everyone(result, NEAR).reshape(-1, 128)
    arrived = lax.all_to_all(whole[back], FAR, 0, 0, tiled=True)
    return (arrived[place].reshape(-1), lam.reshape(-1))


def solution(mesh):
    torus = Mesh(
        mesh.devices.reshape(4, 8, 2, mesh.shape["grp"]), ("brick_0", "brick_1", "brick_2", "grp")
    )
    placed = (P("grp", BRICK), P(), P(BRICK_GRP), P(BRICK_GRP), P())
    return jax.shard_map(
        on_device, mesh=torus, in_specs=placed, out_specs=(P(BRICK_GRP), P()), check_vma=False
    )
```

time: 252 us -> 263 us (1.044)
  blocking collectives: 85.4 us -> 104 us
  waiting for transfers between devices: 61.7 us -> 44.9 us
  between operations: 0.94 us -> 14.3 us
  other arithmetic: 14.9 us -> 7.17 us
  starting transfers between devices: 40.5 us -> 36.2 us
  local copies, waits for them, and re-layouts: 24.3 us -> 28.5 us
  Pallas kernels: 23.3 us -> 26 us
    all_to_all x3 -> x2, waiting for transfers between devices: 39.1 us -> 5.19 us  [from_everyone(): lax.all_to_all(jnp.broadcast_to(array[None], (devices, *array.shape)), ax...]
    ppermute x3, waiting for transfers between devices: 0.01 us -> 19.2 us  [on_device(): lax.ppermute(piece, 'grp', [(i, (i + k + 1) % 4) for i in range(4)])]
    all_to_all x7 -> x8, blocking collectives: 71.3 us -> 88.9 us  [from_everyone(): lax.all_to_all(jnp.broadcast_to(array[None], (devices, *array.shape)), ax...]
    sort x4 -> x0, other arithmetic: 14.4 us -> none  [the longest x1 6.76 us: layout_tables(): chosen = jnp.argsort(keys)[:per_brick]]
    all_to_all x2, starting transfers between devices: 19.9 us -> 14.3 us  [the longest x1 10.4 us: on_device(): lax.all_to_all(both.reshape(-1, 256)[leaving], FAR, 0, 0, tiled=True)]
    unnamed x20 -> x26, local copies, waits for them, and re-layouts: 12.9 us -> 15.6 us
    pallas_call x5, Pallas kernels: 23.3 us -> 26 us  [the longest x1 12.5 us: on_device(): call(solve_kernel, [SM, ANY, ANY, ANY, ANY, VM, VM, VM, VM, VM], [square,...]
    select_n x6 -> x7, other arithmetic: 0.22 us -> 2.9 us  [the longest x2 2.02 us: first_of(): jnp.where(mask, index, index + values.shape[1])]
  transfers between devices with their start and end apart: 10 -> 9, of which waited for: 7 -> 6; matrix products, arithmetic and copies ran while one was open for 7% -> 5% of each run, Pallas kernels for 0% -> 0%
where the time goes in v2:
time: 263 us; the launch traced here: 261 us
  blocking collectives  104 us (40%)
  waiting for transfers between devices  44.9 us (17%)
  starting transfers between devices  36.2 us (14%)
  local copies, waits for them, and re-layouts  28.5 us (11%)
  Pallas kernels  26 us (10%)
  between operations  14.3 us (5%)
  other arithmetic  7.17 us (3%)
    all_to_all x8, blocking collectives, from_everyone(): lax.all_to_all(jnp.broadcast_to(array[None], (devices, *array.shape)), ax...  88.9 us
    ppermute x3, waiting for transfers between devices, on_device(): lax.ppermute(piece, 'grp', [(i, (i + k + 1) % 4) for i in range(4)])  19.2 us
    unnamed x26, local copies, waits for them, and re-layouts  15.6 us
    all_to_all x1, blocking collectives, on_device(): shard = lax.all_to_all(mine, PLANE, 0, 0, tiled=True).sum(axis=0)  15.1 us
    pallas_call x1, Pallas kernels, on_device(): call(solve_kernel, [SM, ANY, ANY, ANY, ANY, VM, VM, VM, VM, VM], [square,...  12.5 us
    all_to_all x2, starting transfers between devices, from_everyone(): lax.all_to_all(jnp.broadcast_to(array[None], (devices, *array.shape)), ax...  11.5 us
    all_to_all x1, starting transfers between devices, on_device(): lax.all_to_all(both.reshape(-1, 256)[leaving], FAR, 0, 0, tiled=True)  10.4 us
    all_to_all x1, waiting for transfers between devices, on_device(): lax.all_to_all(both.reshape(-1, 256)[leaving], FAR, 0, 0, tiled=True)  8.98 us
  transfers between devices with their start and end apart: 9, of which 6 were waited for; matrix products, arithmetic and copies ran while one was open for 5% of the time, Pallas kernels for 0%

profile of v2, /device:TPU:1, one launch (start us, length us, event | category | flops | bytes accessed | tf_op | source)
XLA Modules:
  0.0 261.1 jit_solution(15099718037419208060)
XLA Ops:
  8.6 6.5 %all-to-all-start = ((f32[8,32,256]{2,1,0:T(8,128)}), f32[8,32,256]{2,1,0:T(8,128)S(1)}, u32[]{:S(2)}, u32[]{:S(2)}) async-start(f32[8,32,256]{2,1,0:T(8,128)} %broadcast_in_dim.50), calls=%async_computation | async-start | bytes 524288 | tf_op jit(solution)/shard_map/all_to_all | solution.py:44
  16.7 1.4 iota_select_fusion
  19.2 3.7 %constant_dynamic-slice_fusion.1 = (bf16[128,4096]{1,0:T(8,128)(2,1)}, bf16[128,4096]{1,0:T(8,128)(2,1)}, bf16[128,4096]{1,0:T(8,128)(2,1)}) fusion(bf16[128,16384]{1,0:T(8,128)(2,1)} %own_hbm.9, s32[]{:T(128)S(6)} %select_n.115, s32[]{:T(128)S(6)} %select_n.114, s32[]{:T(128)S(6)} %select_n.113), kind=kLoop, calls=%fused_computation.60 | loop fusion | bytes 6291468 | tf_op jit(solution)/shard_map/dynamic_slice | solution.py:422
  22.9 1.4 collective-permute-start
  24.3 2.4 collective-permute-start.1
  32.8 10.4 %all-to-all-start.1 = ((f32[32,4,256]{2,1,0:T(4,128)}), f32[32,4,256]{2,1,0:T(4,128)S(1)}, u32[]{:S(2)}, u32[]{:S(2)}) async-start(f32[32,4,256]{2,1,0:T(4,128)} %all_to_all.50), calls=%async_computation.1 | async-start | bytes 262144 | tf_op jit(solution)/shard_map/all_to_all | solution.py:435
  43.5 9.0 %all-to-all-done.1 = f32[32,4,256]{2,1,0:T(4,128)S(1)} async-done(((f32[32,4,256]{2,1,0:T(4,128)}), f32[32,4,256]{2,1,0:T(4,128)S(1)}, u32[]{:S(2)}, u32[]{:S(2)}) %all-to-all-start.1) | async-done | bytes 131104 | tf_op jit(solution)/shard_map/all_to_all | solution.py:435
  53.1 19.2 %collective-permute-done.1.two_hbm = bf16[128,4096]{1,0:T(8,128)(2,1)S(1)} collective-permute-done((bf16[128,4096]{1,0:T(8,128)(2,1)}, bf16[128,4096]{1,0:T(8,128)(2,1)S(1)}, u32[]{:S(2)}, u32[]{:S(2)}) %collective-permute-start.1) | collective-permute-done | bytes 1048608 | tf_op jit(solution)/shard_map/ppermute | solution.py:427
  72.3 2.2 copy-done
  74.5 4.5 %gram.1 = (f32[16,48,128]{2,1,0:T(8,128)S(1)}, f32[16,48,128]{2,1,0:T(8,128)S(1)}) custom-call(s32[2]{0:T(128)S(1)} %pad_add_fusion.at_ref, bf16[128,16384]{1,0:T(8,128)(2,1)S(1)} %copy-done, bf16[128,4096]{1,0:T(8,128)(2,1)S(1)} %collective-permute-done.one_hbm, bf16[128,4096]{1,0:T(8,128)(2,1)S(1)} %collective-permute-done.1.two_hbm, ...), custom_call_target="tpu_custom_call" | custom-call | tf_op jit(solution)/shard_map/gram/pallas_call | solution.py:441
  81.8 15.1 %all_to_all.79 = f32[16,48,128]{2,1,0:T(8,128)} all-to-all(f32[16,48,128]{2,1,0:T(8,128)S(1)} %add.135), channel_id=1, replica_groups=mesh['brick_0'=4,'brick_1'=8,'brick_2'=2,'grp'=4] {'brick_0','grp'}, dimensions={0} | all-to-all | bytes 786432 | tf_op jit(solution)/shard_map/all_to_all | solution.py:458
  97.9 16.8 %all_to_all.80 = f32[8,48,128]{2,1,0:T(8,128)} all-to-all(f32[8,48,128]{2,1,0:T(8,128)S(1)} %broadcast_in_dim.56), channel_id=1, replica_groups=mesh['brick_0'=4,'brick_1'=8,'brick_2'=2,'grp'=4] {'brick_1'}, dimensions={0} | all-to-all | bytes 393216 | tf_op jit(solution)/shard_map/all_to_all | solution.py:44
  115.7 11.1 %all_to_all.81.mine_ref = f32[16,48,128]{2,1,0:T(8,128)S(1)} all-to-all(f32[16,48,128]{2,1,0:T(8,128)S(1)} %broadcast_in_dim.57), channel_id=1, replica_groups=mesh['brick_0'=4,'brick_1'=8,'brick_2'=2,'grp'=4] {'brick_0','grp'}, dimensions={0} | all-to-all | bytes 786432 | tf_op jit(solution)/shard_map/all_to_all | solution.py:44
  126.8 4.1 %collective-permute-start.4 = (f32[16,48,128]{2,1,0:T(8,128)S(1)}, f32[16,48,128]{2,1,0:T(8,128)S(1)}, u32[]{:S(2)}, u32[]{:S(2)}) collective-permute-start(f32[16,48,128]{2,1,0:T(8,128)S(1)} %all_to_all.81.mine_ref), channel_id=1, source_target_pairs={{0,4},{4,0},{1,5},{5,1},{2,6},{6,2},{3,7},{7,3},{8,12},{12,8},{9,1... | collective-permute-start | bytes 1179656 | tf_op jit(solution)/shard_map/ppermute | solution.py:461
  132.3 2.2 copy-done.1
  134.5 12.5 %solve.1 = (f32[512,512]{1,0:T(8,128)S(1)}, f32[4,128]{1,0:T(4,128)S(1)}, f32[4,128]{1,0:T(4,128)S(1)}, f32[4,128]{1,0:T(4,128)S(1)}) custom-call(s32[2]{0:T(128)S(1)} %pad_add_fusion.at_ref, bf16[128,16384]{1,0:T(8,128)(2,1)S(1)} %copy-done.1, bf16[128,4096]{1,0:T(8,128)(2,1)S(1)} %collective-permute-done.one_hbm, ...), custom_call_target="tpu_custom_call" | custom-call | tf_op jit(solution)/shard_map/solve/pallas_call | solution.py:466
  148.0 7.6 %all_to_all.82 = f32[8,4,128]{2,1,0:T(4,128)S(1)} all-to-all(f32[8,4,128]{2,1,0:T(4,128)S(1)} %broadcast_in_dim.58), channel_id=1, replica_groups=mesh['brick_0'=4,'brick_1'=8,'brick_2'=2,'grp'=4] {'brick_2','grp'}, dimensions={0} | all-to-all | bytes 32768 | tf_op jit(solution)/shard_map/all_to_all | solution.py:44
  155.7 11.8 %all_to_all.83.gathered_ref = f32[32,4,128]{2,1,0:T(4,128)S(1)} all-to-all(f32[32,4,128]{2,1,0:T(4,128)S(1)} %broadcast_in_dim.59), channel_id=1, replica_groups=mesh['brick_0'=4,'brick_1'=8,'brick_2'=2,'grp'=4] {'brick_0','brick_1'}, dimensions={0} | all-to-all | bytes 131072 | tf_op jit(solution)/shard_map/all_to_all | solution.py:44
  167.5 2.2 copy-done.2
  170.9 3.2 %step.2 = (f32[4,128]{1,0:T(4,128)S(1)}, f32[4,128]{1,0:T(4,128)S(1)}) custom-call(s32[2]{0:T(128)S(1)} %pad_add_fusion.at_ref, bf16[128,16384]{1,0:T(8,128)(2,1)S(1)} %copy-done.2, bf16[128,4096]{1,0:T(8,128)(2,1)S(1)} %collective-permute-done.one_hbm, bf16[128,4096]{1,0:T(8,128)(2,1)S(1)} %collective-permute-done.1.two_hbm, ...), custom_call_target="tpu_custom_call" | custom-call | tf_op jit(solution)/shard_map/step/pallas_call | solution.py:483
  174.1 8.8 %all_to_all.84 = f32[8,4,128]{2,1,0:T(4,128)S(1)} all-to-all(f32[8,4,128]{2,1,0:T(4,128)S(1)} %broadcast_in_dim.60), channel_id=1, replica_groups=mesh['brick_0'=4,'brick_1'=8,'brick_2'=2,'grp'=4] {'brick_2','grp'}, dimensions={0} | all-to-all | bytes 32768 | tf_op jit(solution)/shard_map/all_to_all | solution.py:44
  182.9 11.9 %all_to_all.85.gathered_ref = f32[32,4,128]{2,1,0:T(4,128)S(1)} all-to-all(f32[32,4,128]{2,1,0:T(4,128)S(1)} %broadcast_in_dim.61), channel_id=1, replica_groups=mesh['brick_0'=4,'brick_1'=8,'brick_2'=2,'grp'=4] {'brick_0','brick_1'}, dimensions={0} | all-to-all | bytes 131072 | tf_op jit(solution)/shard_map/all_to_all | solution.py:44
  194.8 2.2 copy-done.3
  198.2 3.2 %step.3 = (f32[4,128]{1,0:T(4,128)S(1)}, f32[4,128]{1,0:T(4,128)S(1)}) custom-call(s32[2]{0:T(128)S(1)} %pad_add_fusion.at_ref, bf16[128,16384]{1,0:T(8,128)(2,1)S(1)} %copy-done.3, bf16[128,4096]{1,0:T(8,128)(2,1)S(1)} %collective-permute-done.one_hbm, bf16[128,4096]{1,0:T(8,128)(2,1)S(1)} %collective-permute-done.1.two_hbm, ...), custom_call_target="tpu_custom_call" | custom-call | tf_op jit(solution)/shard_map/step/pallas_call | solution.py:483
  201.4 8.9 %all_to_all.86 = f32[8,4,128]{2,1,0:T(4,128)S(1)} all-to-all(f32[8,4,128]{2,1,0:T(4,128)S(1)} %broadcast_in_dim.62), channel_id=1, replica_groups=mesh['brick_0'=4,'brick_1'=8,'brick_2'=2,'grp'=4] {'brick_2','grp'}, dimensions={0} | all-to-all | bytes 32768 | tf_op jit(solution)/shard_map/all_to_all | solution.py:44
  210.4 11.9 %all_to_all.87.gathered_ref = f32[32,4,128]{2,1,0:T(4,128)S(1)} all-to-all(f32[32,4,128]{2,1,0:T(4,128)S(1)} %broadcast_in_dim.63), channel_id=1, replica_groups=mesh['brick_0'=4,'brick_1'=8,'brick_2'=2,'grp'=4] {'brick_0','brick_1'}, dimensions={0} | all-to-all | bytes 131072 | tf_op jit(solution)/shard_map/all_to_all | solution.py:44
  222.3 2.2 copy-done.4
  225.7 2.6 %last.1 = (f32[4,128]{1,0:T(4,128)}, f32[32,128]{1,0:T(8,128)S(1)}) custom-call(s32[2]{0:T(128)S(1)} %pad_add_fusion.at_ref, bf16[128,16384]{1,0:T(8,128)(2,1)S(1)} %copy-done.4, bf16[128,4096]{1,0:T(8,128)(2,1)S(1)} %collective-permute-done.one_hbm, bf16[128,4096]{1,0:T(8,128)(2,1)S(1)} %collective-permute-done.1.two_hbm, ...), custom_call_target="tpu_custom_call" | custom-call | tf_op jit(solution)/shard_map/last/pallas_call | solution.py:486
  229.0 4.9 %all-to-all-start.11 = ((f32[8,32,128]{2,1,0:T(8,128)}), f32[8,32,128]{2,1,0:T(8,128)S(1)}, u32[]{:S(2)}, u32[]{:S(2)}) async-start(f32[8,32,128]{2,1,0:T(8,128)} %broadcast_in_dim.64), calls=%async_computation.11 | async-start | bytes 262144 | tf_op jit(solution)/shard_map/all_to_all | solution.py:44
  233.9 5.2 %all-to-all-done.11 = f32[8,32,128]{2,1,0:T(8,128)S(1)} async-done(((f32[8,32,128]{2,1,0:T(8,128)}), f32[8,32,128]{2,1,0:T(8,128)S(1)}, u32[]{:S(2)}, u32[]{:S(2)}) %all-to-all-start.11) | async-done | bytes 131104 | tf_op jit(solution)/shard_map/all_to_all | solution.py:44
  240.4 3.9 %all-to-all-start.12 = ((f32[32,4,128]{2,1,0:T(4,128)}), f32[32,4,128]{2,1,0:T(4,128)S(1)}, u32[]{:S(2)}, u32[]{:S(2)}) async-start(f32[32,4,128]{2,1,0:T(4,128)} %bitcast.12), calls=%async_computation.12 | async-start | bytes 131072 | tf_op jit(solution)/shard_map/all_to_all | solution.py:491
  244.3 8.8 %all-to-all-done.12 = f32[32,4,128]{2,1,0:T(4,128)S(1)} async-done(((f32[32,4,128]{2,1,0:T(4,128)}), f32[32,4,128]{2,1,0:T(4,128)S(1)}, u32[]{:S(2)}, u32[]{:S(2)}) %all-to-all-start.12) | async-done | bytes 65568 | tf_op jit(solution)/shard_map/all_to_all | solution.py:491
  (78 shorter events, 24.8 us)
Async XLA Ops:
  8.6 14.3 %all-to-all-start = ((f32[8,32,256]{2,1,0:T(8,128)}), f32[8,32,256]{2,1,0:T(8,128)S(1)}, u32[]{:S(2)}, u32[]{:S(2)}) async-start(f32[8,32,256]{2,1,0:T(8,128)} %broadcast_in_dim.50), calls=%async_computation | async-start | bytes 524288 | tf_op jit(solution)/shard_map/all_to_all | solution.py:44
  15.2 14.4 %sort.35.cloned.1.call-start = ((), (), s32[]{:S(2)}) async-start(), calls=%async_computation.14 | async-start | bytes 98336 | tf_op jit(solution)/shard_map/sort | solution.py:51
  16.0 0.6 copy-start.10
  16.6 13.8 %sort.33.cloned.1.call-start = ((), (), s32[]{:S(2)}) async-start(), calls=%async_computation.13 | async-start | bytes 196640 | tf_op jit(solution)/shard_map/sort | solution.py:51
  22.9 30.2 %collective-permute-start = (bf16[128,4096]{1,0:T(8,128)(2,1)}, bf16[128,4096]{1,0:T(8,128)(2,1)S(1)}, u32[]{:S(2)}, u32[]{:S(2)}) collective-permute-start(bf16[128,4096]{1,0:T(8,128)(2,1)} %get-tuple-element.24), channel_id=1, source_target_pairs={{0,1},{1,2},{2,3},{3,0},{4,5},{5,6},{6,7},{7,4},{8,9},{9,10},{10,1... | collective-permute-start | bytes 3145736 | tf_op jit(solution)/shard_map/ppermute | solution.py:427
  24.3 48.0 %collective-permute-start.1 = (bf16[128,4096]{1,0:T(8,128)(2,1)}, bf16[128,4096]{1,0:T(8,128)(2,1)S(1)}, u32[]{:S(2)}, u32[]{:S(2)}) collective-permute-start(bf16[128,4096]{1,0:T(8,128)(2,1)} %get-tuple-element.25), channel_id=1, source_target_pairs={{0,2},{1,3},{2,0},{3,1},{4,6},{5,7},{6,4},{7,5},{8,10},{9,11},{10,... | collective-permute-start | bytes 3145736 | tf_op jit(solution)/shard_map/ppermute | solution.py:427
  26.8 45.6 %collective-permute-start.2 = (bf16[128,4096]{1,0:T(8,128)(2,1)}, bf16[128,4096]{1,0:T(8,128)(2,1)S(1)}, u32[]{:S(2)}, u32[]{:S(2)}) collective-permute-start(bf16[128,4096]{1,0:T(8,128)(2,1)} %get-tuple-element.26), channel_id=1, source_target_pairs={{0,3},{1,0},{2,1},{3,2},{4,7},{5,4},{6,5},{7,6},{8,11},{9,8},{10,9... | collective-permute-start | bytes 3145736 | tf_op jit(solution)/shard_map/ppermute | solution.py:427
  32.8 19.6 %all-to-all-start.1 = ((f32[32,4,256]{2,1,0:T(4,128)}), f32[32,4,256]{2,1,0:T(4,128)S(1)}, u32[]{:S(2)}, u32[]{:S(2)}) async-start(f32[32,4,256]{2,1,0:T(4,128)} %all_to_all.50), calls=%async_computation.1 | async-start | bytes 262144 | tf_op jit(solution)/shard_map/all_to_all | solution.py:435
  53.1 79.2 %copy-start.9 = (f32[512]{0:T(512)S(1)}, f32[512]{0:T(512)}, u32[]{:S(2)}) copy-start(f32[512]{0:T(512)} %param.9) | copy-start | bytes 6148
  72.3 2.2 copy-start
  79.0 2.7 %collective-permute-start.3 = (f32[16,48,128]{2,1,0:T(8,128)S(1)}, f32[16,48,128]{2,1,0:T(8,128)S(1)}, u32[]{:S(2)}, u32[]{:S(2)}) collective-permute-start(f32[16,48,128]{2,1,0:T(8,128)S(1)} %get-tuple-element.33), channel_id=1, source_target_pairs={{0,4},{4,0},{1,5},{5,1},{2,6},{6,2},{3,7},{7,3},{8,12},{12,8},{9,1... | collective-permute-start | bytes 1179656 | tf_op jit(solution)/shard_map/ppermute | solution.py:457
  126.8 5.5 %collective-permute-start.4 = (f32[16,48,128]{2,1,0:T(8,128)S(1)}, f32[16,48,128]{2,1,0:T(8,128)S(1)}, u32[]{:S(2)}, u32[]{:S(2)}) collective-permute-start(f32[16,48,128]{2,1,0:T(8,128)S(1)} %all_to_all.81.mine_ref), channel_id=1, source_target_pairs={{0,4},{4,0},{1,5},{5,1},{2,6},{6,2},{3,7},{7,3},{8,12},{12,8},{9,1... | collective-permute-start | bytes 1179656 | tf_op jit(solution)/shard_map/ppermute | solution.py:461
  132.3 2.2 copy-start.1
  147.0 1.0 copy-start.5
  167.5 2.2 copy-start.2
  169.7 1.2 copy-start.6
  194.8 2.2 copy-start.3
  197.0 1.2 copy-start.7
  222.3 2.2 copy-start.4
  224.4 1.2 copy-start.8
  225.7 18.6 %copy-start.11 = (s32[32]{0:T(128)S(1)}, s32[32]{0:T(128)}, u32[]{:S(2)}) copy-start(s32[32]{0:T(128)} %dynamic_slice.32) | copy-start | bytes 388
  229.0 10.1 %all-to-all-start.11 = ((f32[8,32,128]{2,1,0:T(8,128)}), f32[8,32,128]{2,1,0:T(8,128)S(1)}, u32[]{:S(2)}, u32[]{:S(2)}) async-start(f32[8,32,128]{2,1,0:T(8,128)} %broadcast_in_dim.64), calls=%async_computation.11 | async-start | bytes 262144 | tf_op jit(solution)/shard_map/all_to_all | solution.py:44
  240.4 12.7 %all-to-all-start.12 = ((f32[32,4,128]{2,1,0:T(4,128)}), f32[32,4,128]{2,1,0:T(4,128)S(1)}, u32[]{:S(2)}, u32[]{:S(2)}) async-start(f32[32,4,128]{2,1,0:T(4,128)} %bitcast.12), calls=%async_computation.12 | async-start | bytes 131072 | tf_op jit(solution)/shard_map/all_to_all | solution.py:491
Sparse Core Ops, SparseCore 0:
  18.8 2.8 sort.39.cloned.1.call-done
  24.2 3.8 sort.37.cloned.1.call-done
  (2 shorter events, 0.0 us)

commit v3 on v2

--- a/solution.py
+++ b/solution.py
@@ -7,6 +7,7 @@
 from jax.experimental.pallas import tpu as pltpu
 from jax.sharding import Mesh
 from jax.sharding import PartitionSpec as P
+
 
 ITERS = 4
 BRICK = ("brick_0", "brick_1", "brick_2")
@@ -25,7 +26,7 @@
 SHARD_G = len(PAIRS) * ROWS // SHARDS
 SHARD = SHARD_G + 8
 HALF = SHARDS // 2
-DOUBLINGS = 5
+DOUBLINGS = 4
 MAX_CORRECT = 48
 ACCEPT = 1e-4
 
@@ -46,10 +47,12 @@
     )
 
 
-def first_of(mask, values, count):
+def two_of(mask, values):
     index = lax.broadcasted_iota(jnp.int32, values.shape, 1)
-    _, kept = lax.sort_key_val(jnp.where(mask, index, index + values.shape[1]), values)
-    return kept[:, :count]
+    first = jnp.min(jnp.where(mask, index, values.shape[1]), axis=1, keepdims=True)
+    second = jnp.max(jnp.where(mask, index, -1), axis=1, keepdims=True)
+    kept = [jnp.sum(jnp.where(index == at, values, 0), axis=1) for at in (first, second)]
+    return jnp.stack(kept, axis=1)
 
 
 def ranks(keys):
@@ -66,16 +69,22 @@
     chip, core = here // 2, here % 2
     per_chip = 2 * per_brick
     grid = perm.reshape(-1, per_brick)
-    incoming = first_of(grid // per_brick == here, grid, 2).reshape(-1) % per_brick
+    same = lax.dynamic_index_in_dim(grid.reshape(-1, 2, per_brick), core, 1, keepdims=False)
+    rows = jnp.concatenate([grid, same, same], axis=0)
+    bricks, chips = grid.shape[0], same.shape[0]
+    line = lax.broadcasted_iota(jnp.int32, rows.shape, 0)
+    wanted = jnp.where(line < bricks, here, chip * 2 + (line >= bricks + chips))
+    picked = two_of(rows // per_brick == wanted, rows)
+    incoming = picked[:bricks].reshape(-1) % per_brick
+    back = jnp.stack([picked[bricks : bricks + chips], picked[bricks + chips :]], axis=1)
+    back = back.reshape(-1) % per_chip
     local = lax.dynamic_slice_in_dim(perm, chip * per_chip, per_chip)
     index = jnp.arange(per_chip, dtype=jnp.int32)
     key = (local // per_chip) * per_chip + index
     key = jnp.where((local // per_brick) % 2 == core, key, key + perm.shape[0] * 2)
     leaving = inverted(ranks(key), per_brick)
-    same = lax.dynamic_index_in_dim(grid.reshape(-1, 2, per_brick), core, 1, keepdims=False)
-    back = first_of(same // per_chip == chip, same, 4).reshape(-1) % per_chip
     mine = lax.dynamic_slice_in_dim(perm, here * per_brick, per_brick)
-    place = ranks((mine // per_chip) * per_brick + jnp.arange(per_brick, dtype=jnp.int32))
+    place = ranks((mine // per_brick) * per_brick + jnp.arange(per_brick, dtype=jnp.int32))
     return (inverted(incoming, per_brick), leaving, back, place)
 
 
@@ -104,43 +113,18 @@
     return jnp.concatenate(rows, axis=1)
 
 
-class Columns:
-    def __init__(self, at_ref, pieces, full_ref, sems):
-        quarter = at_ref[0]
-        self.full_ref = full_ref
-        self.copies = []
-        for chunk in range(CHUNKS):
-            to = pl.ds(chunk * WIDTH, WIDTH)
-            own = pl.ds(pl.multiple_of(quarter * COLS + chunk * WIDTH, WIDTH), WIDTH)
-            self.copies.append(
-                [
-                    pltpu.make_async_copy(
-                        piece.at[:, own if k == 0 else to],
-                        full_ref.at[lax.rem(quarter + 4 - k, 4), :, to],
-                        sems.at[chunk, k],
-                    )
-                    for k, piece in enumerate(pieces)
-                ]
-            )
-
-    def start(self):
-        for group in self.copies:
-            for copy in group:
-                copy.start()
-
-    def chunk(self, chunk):
-        for copy in self.copies[chunk]:
-            copy.wait()
-        return self.full_ref[:, :, chunk * WIDTH : (chunk + 1) * WIDTH].reshape(M, WIDTH)
-
-
-def as_rows(lam):
-    flat = jnp.concatenate([lam[i : i + 1, :] for i in range(NB)], axis=1)
+def columns(pieces, chunk):
+    to = slice(chunk * WIDTH, (chunk + 1) * WIDTH)
+    return jnp.concatenate([piece[:, to] for piece in pieces], axis=0)
+
+
+def slots(at_ref):
+    return [lax.rem(at_ref[0] + NB - k, NB) for k in range(NB)]
+
+
+def as_rows(at_ref, lam_ref):
+    flat = jnp.concatenate([lam_ref[pl.ds(slot, 1), :] for slot in slots(at_ref)], axis=1)
     return jnp.broadcast_to(flat, (16, M)).astype(BF)
-
-
-def as_lines(flat):
-    return jnp.concatenate([flat[:, i * 128 : (i + 1) * 128] for i in range(NB)], axis=0)
 
 
 def trial_chunk(block, curv_ref, lin_ref, lam_b, chunk):
@@ -149,14 +133,15 @@
     return jnp.clip(-curv * (lin + pushed), -move_limit, move_limit)
 
 
-def product_of_trial(columns, curv_ref, lin_ref, lam):
-    lam_b = as_rows(lam)
+def product_of_trial(at_ref, pieces, curv_ref, lin_ref, lam_ref, part_ref):
+    lam_b = as_rows(at_ref, lam_ref)
     total = jnp.zeros((16, M), F32)
     for chunk in range(CHUNKS):
-        block = columns.chunk(chunk)
+        block = columns(pieces, chunk)
         moved = trial_chunk(block, curv_ref, lin_ref, lam_b, chunk).astype(BF)
         total += lax.dot_general(moved, block, NT, preferred_element_type=F32)
-    return as_lines(total[0:1, :])
+    for k, slot in enumerate(slots(at_ref)):
+        part_ref[pl.ds(slot, 1), :] = total[0:1, k * 128 : (k + 1) * 128]
 
 
 def newton_update(lam, total, bound, inv_ref, scale):
@@ -171,29 +156,32 @@
 
 
 def gram_kernel(
-    at_ref, own_hbm, one_hbm, two_hbm, three_hbm, curv_ref, lin_ref,
-    mine_ref, other_ref, full_ref, gram_ref, prod_ref, half_ref, sems,
+    at_ref, own_ref, one_ref, two_ref, three_ref, curv_ref, lin_ref,
+    mine_ref, other_ref, gram_ref, prod_ref, block_ref, half_ref,
 ):
     core = at_ref[1]
-    columns = Columns(at_ref, (own_hbm, one_hbm, two_hbm, three_hbm), full_ref, sems)
-    columns.start()
+    pieces = (own_ref, one_ref, two_ref, three_ref)
     gram_ref[...] = jnp.zeros_like(gram_ref)
     prod_ref[...] = jnp.zeros_like(prod_ref)
     for s in range(SHARDS):
         half_ref[s // HALF, s % HALF, SHARD_G:, :] = jnp.zeros((8, 128), F32)
     for chunk in range(CHUNKS):
-        block = columns.chunk(chunk)
+        block = columns(pieces, chunk)
         curv, lin = flat_rows(curv_ref, chunk), flat_rows(lin_ref, chunk)
         weighted = (block.astype(F32) * curv).astype(BF)
         gram_ref[...] += lax.dot_general(weighted, block, NT, preferred_element_type=F32)
         moved = jnp.clip(-curv * lin, -move_limit, move_limit)
         moved = jnp.broadcast_to(moved, (16, WIDTH)).astype(BF)
         prod_ref[...] += lax.dot_general(moved, block, NT, preferred_element_type=F32)
-    for j in range(NB):
-        half_ref[0, j, SHARD_G : SHARD_G + 1, :] = prod_ref[0:1, j * 128 : (j + 1) * 128]
+    where = slots(at_ref)
+    for a in range(NB):
+        half_ref[0, pl.ds(where[a], 1), SHARD_G, :] = prod_ref[0:1, a * 128 : (a + 1) * 128]
+        for b in range(NB):
+            block_ref[where[a], where[b]] = gram_ref[
+                a * 128 : (a + 1) * 128, b * 128 : (b + 1) * 128
+            ]
     for p, (i, j) in enumerate(PAIRS):
-        rows, cols = slice(i * 128, (i + 1) * 128), slice(j * 128, (j + 1) * 128)
-        value = 0.5 * (gram_ref[rows, cols] + gram_ref[cols, rows].T)
+        value = 0.5 * (block_ref[i, j] + block_ref[j, i].T)
         for t in range(16):
             half_ref[packed_tile(p, t)] = value[t * 8 : t * 8 + 8]
     mine_ref[...] = half_ref[core]
@@ -211,12 +199,11 @@
 
 
 def solve_kernel(
-    at_ref, own_hbm, one_hbm, two_hbm, three_hbm, mine_ref, other_ref, curv_ref, lin_ref, bound_ref,
+    at_ref, own_ref, one_ref, two_ref, three_ref, mine_ref, other_ref, curv_ref, lin_ref, bound_ref,
     inv_ref, scale_ref, lam_ref, part_ref,
-    full_ref, half_ref, hess_ref, r_ref, sems,
+    half_ref, hess_ref, r_ref,
 ):
-    columns = Columns(at_ref, (own_hbm, one_hbm, two_hbm, three_hbm), full_ref, sems)
-    columns.start()
+    pieces = (own_ref, one_ref, two_ref, three_ref)
     core = at_ref[1]
     half_ref[core] = mine_ref[...]
     half_ref[1 - core] = other_ref[...]
@@ -267,15 +254,18 @@
     lax.fori_loop(0, DOUBLINGS - 1, double, 0)
 
     def correct(precise):
-        x = inv_ref[...]
-        x_high, x_low = split(x)
         if precise:
+            x = inv_ref[...]
+            x_high, x_low = split(x)
             product = jnp.dot(
                 hess_ref[...], x, precision=lax.Precision.HIGHEST, preferred_element_type=F32
             )
         else:
+            x_high = inv_ref[...].astype(BF)
             h_high, h_low = split(hess_ref[...])
-            product = times_split(h_high, h_low, x_high, x_low)
+            product = jnp.dot(h_high, x_high, preferred_element_type=F32) + jnp.dot(
+                h_low, x_high, preferred_element_type=F32
+            )
         residual = eye() - product
         size = jnp.sum(residual * residual)
         good = size < M
@@ -283,7 +273,11 @@
         @pl.when(good)
         def _():
             r_high, r_low = split(residual)
-            inv_ref[...] += times_split(x_high, x_low, r_high, r_low)
+            if precise:
+                inv_ref[...] += times_split(x_high, x_low, r_high, r_low)
+            else:
+                step = jnp.dot(x_high, r_high, preferred_element_type=F32)
+                inv_ref[...] = x_high.astype(F32) + step
 
         @pl.when(jnp.logical_not(good))
         def _():
@@ -332,51 +326,35 @@
     zero = jnp.zeros((NB, 128), F32)
     lam = newton_update(zero, total, bound_ref[...], inv_ref, scale)
     lam_ref[...] = lam
-    part_ref[...] = product_of_trial(columns, curv_ref, lin_ref, lam)
-
-
-def updated(gathered_ref, lam_in_ref, bound_ref, inv_hbm, scale_ref, inv_ref, inv_sem):
-    copy = pltpu.make_async_copy(inv_hbm, inv_ref, inv_sem)
-    copy.start()
-    return lambda: (
-        copy.wait(),
-        newton_update(
-            lam_in_ref[...],
-            jnp.sum(gathered_ref[...], axis=0),
-            bound_ref[...],
-            inv_ref,
-            scale_ref[...],
-        ),
-    )[1]
+    product_of_trial(at_ref, pieces, curv_ref, lin_ref, lam_ref, part_ref)
+
+
+def updated(gathered_ref, lam_in_ref, bound_ref, inv_ref, scale_ref):
+    total = jnp.sum(gathered_ref[...], axis=0)
+    return newton_update(lam_in_ref[...], total, bound_ref[...], inv_ref, scale_ref[...])
 
 
 def step_kernel(
-    at_ref, own_hbm, one_hbm, two_hbm, three_hbm, inv_hbm,
+    at_ref, own_ref, one_ref, two_ref, three_ref, inv_ref,
     gathered_ref, lam_in_ref, curv_ref, lin_ref, bound_ref, scale_ref,
-    lam_ref, part_ref, full_ref, inv_ref, sems, inv_sem,
+    lam_ref, part_ref,
 ):
-    update = updated(gathered_ref, lam_in_ref, bound_ref, inv_hbm, scale_ref, inv_ref, inv_sem)
-    columns = Columns(at_ref, (own_hbm, one_hbm, two_hbm, three_hbm), full_ref, sems)
-    columns.start()
-    lam = update()
-    lam_ref[...] = lam
-    part_ref[...] = product_of_trial(columns, curv_ref, lin_ref, lam)
+    lam_ref[...] = updated(gathered_ref, lam_in_ref, bound_ref, inv_ref, scale_ref)
+    pieces = (own_ref, one_ref, two_ref, three_ref)
+    product_of_trial(at_ref, pieces, curv_ref, lin_ref, lam_ref, part_ref)
 
 
 def last_kernel(
-    at_ref, own_hbm, one_hbm, two_hbm, three_hbm, inv_hbm,
+    at_ref, own_ref, one_ref, two_ref, three_ref, inv_ref,
     gathered_ref, lam_in_ref, curv_ref, lin_ref, bound_ref, scale_ref,
-    lam_ref, step_ref, full_ref, inv_ref, sems, inv_sem,
+    lam_ref, step_ref,
 ):
-    update = updated(gathered_ref, lam_in_ref, bound_ref, inv_hbm, scale_ref, inv_ref, inv_sem)
-    columns = Columns(at_ref, (own_hbm, one_hbm, two_hbm, three_hbm), full_ref, sems)
-    columns.start()
-    lam = update()
-    lam_ref[...] = lam
-    lam_b = as_rows(lam)
+    lam_ref[...] = updated(gathered_ref, lam_in_ref, bound_ref, inv_ref, scale_ref)
+    lam_b = as_rows(at_ref, lam_ref)
+    pieces = (own_ref, one_ref, two_ref, three_ref)
     count = WIDTH // 128
     for chunk in range(CHUNKS):
-        moved = trial_chunk(columns.chunk(chunk), curv_ref, lin_ref, lam_b, chunk)
+        moved = trial_chunk(columns(pieces, chunk), curv_ref, lin_ref, lam_b, chunk)
         for k in range(count):
             at = chunk * count + k
             step_ref[at : at + 1, :] = moved[0:1, k * 128 : (k + 1) * 128]
@@ -384,14 +362,13 @@
 
 VM = pl.BlockSpec(memory_space=pltpu.VMEM)
 SM = pl.BlockSpec(memory_space=pltpu.SMEM)
-ANY = pl.BlockSpec(memory_space=pl.ANY)
 
 
 def sds(shape, dtype=F32):
     return jax.ShapeDtypeStruct(shape, dtype)
 
 
-def call(kernel, ins, outs, scratch, mib, name):
+def call(kernel, ins, outs, scratch, mib):
     return pl.pallas_call(
         kernel,
         in_specs=ins,
@@ -399,7 +376,6 @@
         out_shape=outs,
         scratch_shapes=scratch,
         compiler_params=pltpu.CompilerParams(vmem_limit_bytes=mib * MIB),
-        name=name,
     )
 
 
@@ -415,42 +391,48 @@
     per_brick = gradients.shape[1] // 128
     at = jnp.stack([quarter, core]).astype(jnp.int32)
 
-    both = jnp.concatenate([weights.reshape(BLKS, 128), linear.reshape(BLKS, 128)], axis=1)
-    both = from_everyone(both, NEAR)
+    near = size_of(NEAR)
+    both = lax.all_to_all(
+        jnp.concatenate(
+            [
+                jnp.broadcast_to(vector.reshape(1, BLKS, 128), (near, BLKS, 128))
+                for vector in (weights, linear)
+            ],
+            axis=2,
+        ),
+        NEAR, 0, 0, tiled=True,
+    )
 
     slices = [
         lax.dynamic_slice(gradients, (0, lax.rem(quarter + k, 4) * COLS), (ROWS, COLS))
-        for k in (1, 2, 3)
+        for k in range(NB)
     ]
-    *slices, both = lax.optimization_barrier((*slices, both))
-    one, two, three = [
-        lax.ppermute(piece, "grp", [(i, (i + k + 1) % 4) for i in range(4)])
-        for k, piece in enumerate(slices)
-    ]
-    pieces = (gradients, one, two, three)
+    *slices, both, perm = lax.optimization_barrier((*slices, both, perm))
+    pieces = [slices[0]]
+    for k in (1, 2, 3):
+        ring = [(i, (i + k) % 4) for i in range(4)]
+        pieces.append(lax.ppermute(slices[k], "grp", ring))
 
     incoming, leaving, back, place = layout_tables(perm, here, per_brick)
     incoming = lax.dynamic_slice_in_dim(incoming, quarter * BLKS, BLKS)
     place = lax.dynamic_slice_in_dim(place, quarter * BLKS, BLKS)
-    both = lax.all_to_all(both.reshape(-1, 256)[leaving], FAR, 0, 0, tiled=True)[incoming]
+    both = both.reshape(-1, 256)[leaving]
+    both = lax.all_to_all(both, FAR, 0, 0, tiled=True)
+    both = both[incoming]
     curv, lin, back, place = lax.optimization_barrier((both[:, :128], both[:, 128:], back, place))
 
     packed = (HALF, SHARD, 128)
-    full = pltpu.VMEM((NB, ROWS, COLS), BF)
-    sems = pltpu.SemaphoreType.DMA((CHUNKS, NB))
     mine, other = call(
         gram_kernel,
-        [SM, ANY, ANY, ANY, ANY, VM, VM],
+        [SM] + [VM] * 6,
         [sds(packed), sds(packed)],
         [
-            full,
             pltpu.VMEM((M, M), F32),
             pltpu.VMEM((16, M), F32),
+            pltpu.VMEM((NB, NB, 128, 128), F32),
             pltpu.VMEM((2, *packed), F32),
-            sems,
         ],
-        24,
-        "gram",
+        20,
     )(at, *pieces, curv, lin)
 
     swap = [(0, 1), (1, 0)]
@@ -465,25 +447,21 @@
     vector = sds((NB, 128))
     inv, scale, lam, part = call(
         solve_kernel,
-        [SM, ANY, ANY, ANY, ANY, VM, VM, VM, VM, VM],
+        [SM] + [VM] * 9,
         [square, vector, vector, vector],
         [
-            full,
             pltpu.VMEM((2, *packed), F32),
             pltpu.VMEM((M, M), F32),
             pltpu.VMEM((M, M), F32),
-            sems,
         ],
-        32,
-        "solve",
+        28,
     )(at, *pieces, mine, other, curv, lin, bound)
-    ins = [SM, ANY, ANY, ANY, ANY, ANY, VM, VM, VM, VM, VM, VM]
-    scratch = [full, pltpu.VMEM((M, M), F32), sems, pltpu.SemaphoreType.DMA(())]
+    ins = [SM] + [VM] * 11
     for _ in range(ITERS - 2):
-        lam, part = call(step_kernel, ins, [vector, vector], scratch, 24, "step")(
+        lam, part = call(step_kernel, ins, [vector, vector], [], 16)(
             at, *pieces, inv, summed(part), lam, curv, lin, bound, scale
         )
-    lam, result = call(last_kernel, ins, [vector, sds((BLKS, 128))], scratch, 24, "last")(
+    lam, result = call(last_kernel, ins, [vector, sds((BLKS, 128))], [], 16)(
         at, *pieces, inv, summed(part), lam, curv, lin, bound, scale
     )
 

time: 263 us -> 236 us (0.90)
  between operations: 14.3 us -> 0.82 us
  local copies, waits for them, and re-layouts: 28.5 us -> 16 us
  waiting for transfers between devices: 44.9 us -> 50.6 us
    unnamed x26 -> x12, local copies, waits for them, and re-layouts: 15.6 us -> 4.73 us
    all_to_all x2 -> x1, starting transfers between devices: 11.5 us -> 4.95 us  [from_everyone(): lax.all_to_all(jnp.broadcast_to(array[None], (devices, *array.shape)), ax...]
    all_to_all x1 -> x2, starting transfers between devices: 10.4 us -> 17 us  [the longest x1 10.4 us: on_device(): both = lax.all_to_all(both, FAR, 0, 0, tiled=True)]
    ppermute x3, waiting for transfers between devices: 19.2 us -> 23.4 us  [on_device(): pieces.append(lax.ppermute(slices[k], 'grp', ring))]
    all_to_all x1 -> x2, waiting for transfers between devices: 8.98 us -> 10.5 us  [the longest x1 7.91 us: on_device(): both = lax.all_to_all(both, FAR, 0, 0, tiled=True)]
  transfers between devices with their start and end apart: 9 -> 9, of which waited for: 6 -> 9; matrix products, arithmetic and copies ran while one was open for 5% -> 3% of each run, Pallas kernels for 0% -> 0%
where the time goes in v3:
time: 236 us; the launch traced here: 235 us
  blocking collectives  104 us (44%)
  waiting for transfers between devices  50.6 us (21%)
  starting transfers between devices  34.6 us (15%)
  Pallas kernels  24.1 us (10%)
  local copies, waits for them, and re-layouts  16 us (7%)
  other arithmetic  4.83 us (2%)
    all_to_all x8, blocking collectives, from_everyone(): lax.all_to_all(jnp.broadcast_to(array[None], (devices, *array.shape)), ax...  88.9 us
    ppermute x3, waiting for transfers between devices, on_device(): pieces.append(lax.ppermute(slices[k], 'grp', ring))  23.4 us
    all_to_all x1, blocking collectives, on_device(): shard = lax.all_to_all(mine, PLANE, 0, 0, tiled=True).sum(axis=0)  15 us
    pallas_call x1, Pallas kernels, on_device(): call(solve_kernel, [SM] + [VM] * 9, [square, vector, vector, vector], [pl...  11 us
    all_to_all x1, starting transfers between devices, on_device(): both = lax.all_to_all(both, FAR, 0, 0, tiled=True)  10.4 us
    all_to_all x1, waiting for transfers between devices, on_device(): arrived = lax.all_to_all(whole[back], FAR, 0, 0, tiled=True)  8.85 us
    all_to_all x1, waiting for transfers between devices, on_device(): both = lax.all_to_all(both, FAR, 0, 0, tiled=True)  7.91 us
    all_to_all x1, starting transfers between devices, on_device(): lax.all_to_all(jnp.concatenate([jnp.broadcast_to(vector.reshape(1, BLKS,...  6.53 us
  transfers between devices with their start and end apart: 9, of which 9 were waited for; matrix products, arithmetic and copies ran while one was open for 3% of the time, Pallas kernels for 0%

profile of v3, /device:TPU:1, one launch (start us, length us, event | category | flops | bytes accessed | tf_op | source)
XLA Modules:
  0.0 234.9 jit_solution(13939102380872379230)
XLA Ops:
  2.8 6.5 %all-to-all-start = ((f32[8,32,256]{2,1,0:T(8,128)}), f32[8,32,256]{2,1,0:T(8,128)S(1)}, u32[]{:S(2)}, u32[]{:S(2)}) async-start(f32[8,32,256]{2,1,0:T(8,128)} %pad_maximum_fusion), calls=%async_computation | async-start | bytes 524288 | tf_op jit(solution)/shard_map/all_to_all | solution.py:395
  9.3 3.9 %constant_dynamic-slice_fusion.1 = (bf16[128,4096]{1,0:T(8,128)(2,1)}, bf16[128,4096]{1,0:T(8,128)(2,1)}, bf16[128,4096]{1,0:T(8,128)(2,1)S(1)}, bf16[128,4096]{1,0:T(8,128)(2,1)}) fusion(bf16[128,16384]{1,0:T(8,128)(2,1)} %param.5, s32[]{:T(128)S(6)} %select_n.125, s32[]{:T(128)S(6)} %select_n.123, s32[]{:T(128)S(6)} %select_n.122, s32[]{:T(128)S(6)} %select_n.124), kind=kLoop, calls=%fused_computation.55 | loop fusion | bytes 8388624 | tf_op jit(solution)/shard_map/dynamic_slice | solution.py:407
  13.3 2.6 %all-to-all-done = f32[8,32,256]{2,1,0:T(8,128)S(1)} async-done(((f32[8,32,256]{2,1,0:T(8,128)}), f32[8,32,256]{2,1,0:T(8,128)S(1)}, u32[]{:S(2)}, u32[]{:S(2)}) %all-to-all-start) | async-done | bytes 262176 | tf_op jit(solution)/shard_map/all_to_all | solution.py:395
  17.4 1.4 collective-permute-start.1
  21.9 10.4 %all-to-all-start.1 = ((f32[32,4,256]{2,1,0:T(4,128)}), f32[32,4,256]{2,1,0:T(4,128)S(1)}, u32[]{:S(2)}, u32[]{:S(2)}) async-start(f32[32,4,256]{2,1,0:T(4,128)} %all_to_all.50), calls=%async_computation.1 | async-start | bytes 262144 | tf_op jit(solution)/shard_map/all_to_all | solution.py:420
  33.6 7.9 %all-to-all-done.1 = f32[32,4,256]{2,1,0:T(4,128)S(1)} async-done(((f32[32,4,256]{2,1,0:T(4,128)}), f32[32,4,256]{2,1,0:T(4,128)S(1)}, u32[]{:S(2)}, u32[]{:S(2)}) %all-to-all-start.1) | async-done | bytes 131104 | tf_op jit(solution)/shard_map/all_to_all | solution.py:420
  42.2 1.9 collective-permute-done.one_ref
  44.0 19.8 %collective-permute-done.1.two_ref = bf16[128,4096]{1,0:T(8,128)(2,1)S(1)} collective-permute-done((bf16[128,4096]{1,0:T(8,128)(2,1)}, bf16[128,4096]{1,0:T(8,128)(2,1)S(1)}, u32[]{:S(2)}, u32[]{:S(2)}) %collective-permute-start.1) | collective-permute-done | bytes 1048608 | tf_op jit(solution)/shard_map/ppermute | solution.py:414
  63.8 1.8 collective-permute-done.2.three_ref
  65.6 4.8 %shard_map.68 = (f32[16,48,128]{2,1,0:T(8,128)S(1)}, f32[16,48,128]{2,1,0:T(8,128)S(1)}) custom-call(s32[2]{0:T(128)S(1)} %pad_add_fusion.3.at_ref, bf16[128,4096]{1,0:T(8,128)(2,1)S(1)} %get-tuple-element.24.own_ref, bf16[128,4096]{1,0:T(8,128)(2,1)S(1)} %collective-permute-done.one_ref, bf16[128,4096]{1,0:T(8,128)(2,1)S(1)} %collective-permute-done.1.two_ref, ...), custom_call_target="tpu_custom_call" | custom-call | tf_op jit(solution)/shard_map/pallas_call | solution.py:425
  70.4 1.6 collective-permute-start.3
  72.0 1.3 collective-permute-done.3
  73.4 15.0 %all_to_all.79 = f32[16,48,128]{2,1,0:T(8,128)} all-to-all(f32[16,48,128]{2,1,0:T(8,128)S(1)} %add.136), channel_id=1, replica_groups=mesh['brick_0'=4,'brick_1'=8,'brick_2'=2,'grp'=4] {'brick_0','grp'}, dimensions={0} | all-to-all | bytes 786432 | tf_op jit(solution)/shard_map/all_to_all | solution.py:440
  89.4 16.8 %all_to_all.80 = f32[8,48,128]{2,1,0:T(8,128)} all-to-all(f32[8,48,128]{2,1,0:T(8,128)S(1)} %broadcast_in_dim.72), channel_id=1, replica_groups=mesh['brick_0'=4,'brick_1'=8,'brick_2'=2,'grp'=4] {'brick_1'}, dimensions={0} | all-to-all | bytes 393216 | tf_op jit(solution)/shard_map/all_to_all | solution.py:45
  107.2 11.1 %all_to_all.81.mine_ref = f32[16,48,128]{2,1,0:T(8,128)S(1)} all-to-all(f32[16,48,128]{2,1,0:T(8,128)S(1)} %broadcast_in_dim.73), channel_id=1, replica_groups=mesh['brick_0'=4,'brick_1'=8,'brick_2'=2,'grp'=4] {'brick_0','grp'}, dimensions={0} | all-to-all | bytes 786432 | tf_op jit(solution)/shard_map/all_to_all | solution.py:45
  118.4 4.1 %collective-permute-start.4 = (f32[16,48,128]{2,1,0:T(8,128)S(1)}, f32[16,48,128]{2,1,0:T(8,128)S(1)}, u32[]{:S(2)}, u32[]{:S(2)}) collective-permute-start(f32[16,48,128]{2,1,0:T(8,128)S(1)} %all_to_all.81.mine_ref), channel_id=1, source_target_pairs={{0,4},{4,0},{1,5},{5,1},{2,6},{6,2},{3,7},{7,3},{8,12},{12,8},{9,1... | collective-permute-start | bytes 1179656 | tf_op jit(solution)/shard_map/ppermute | solution.py:443
  122.5 1.3 collective-permute-done.4.other_ref
  123.8 11.0 %shard_map.69 = (f32[512,512]{1,0:T(8,128)S(1)}, f32[4,128]{1,0:T(4,128)S(1)}, f32[4,128]{1,0:T(4,128)S(1)}, f32[4,128]{1,0:T(4,128)S(1)}) custom-call(s32[2]{0:T(128)S(1)} %pad_add_fusion.3.at_ref, bf16[128,4096]{1,0:T(8,128)(2,1)S(1)} %get-tuple-element.24.own_ref, bf16[128,4096]{1,0:T(8,128)(2,1)S(1)} %collective-permute-done.one_ref, ...), custom_call_target="tpu_custom_call" | custom-call | tf_op jit(solution)/shard_map/pallas_call | solution.py:448
  135.9 7.6 %all_to_all.82 = f32[8,4,128]{2,1,0:T(4,128)S(1)} all-to-all(f32[8,4,128]{2,1,0:T(4,128)S(1)} %broadcast_in_dim.74), channel_id=1, replica_groups=mesh['brick_0'=4,'brick_1'=8,'brick_2'=2,'grp'=4] {'brick_2','grp'}, dimensions={0} | all-to-all | bytes 32768 | tf_op jit(solution)/shard_map/all_to_all | solution.py:45
  143.5 11.8 %all_to_all.83.gathered_ref = f32[32,4,128]{2,1,0:T(4,128)S(1)} all-to-all(f32[32,4,128]{2,1,0:T(4,128)S(1)} %broadcast_in_dim.75), channel_id=1, replica_groups=mesh['brick_0'=4,'brick_1'=8,'brick_2'=2,'grp'=4] {'brick_0','brick_1'}, dimensions={0} | all-to-all | bytes 131072 | tf_op jit(solution)/shard_map/all_to_all | solution.py:45
  156.6 3.1 %shard_map.70 = (f32[4,128]{1,0:T(4,128)S(1)}, f32[4,128]{1,0:T(4,128)S(1)}) custom-call(s32[2]{0:T(128)S(1)} %pad_add_fusion.3.at_ref, bf16[128,4096]{1,0:T(8,128)(2,1)S(1)} %get-tuple-element.24.own_ref, bf16[128,4096]{1,0:T(8,128)(2,1)S(1)} %collective-permute-done.one_ref, bf16[128,4096]{1,0:T(8,128)(2,1)S(1)} %collective-permute-done.1.two_ref, ...), custom_call_target="tpu_custom_call" | custom-call | tf_op jit(solution)/shard_map/pallas_call | solution.py:461
  159.7 8.8 %all_to_all.84 = f32[8,4,128]{2,1,0:T(4,128)S(1)} all-to-all(f32[8,4,128]{2,1,0:T(4,128)S(1)} %broadcast_in_dim.76), channel_id=1, replica_groups=mesh['brick_0'=4,'brick_1'=8,'brick_2'=2,'grp'=4] {'brick_2','grp'}, dimensions={0} | all-to-all | bytes 32768 | tf_op jit(solution)/shard_map/all_to_all | solution.py:45
  168.5 11.9 %all_to_all.85.gathered_ref = f32[32,4,128]{2,1,0:T(4,128)S(1)} all-to-all(f32[32,4,128]{2,1,0:T(4,128)S(1)} %broadcast_in_dim.77), channel_id=1, replica_groups=mesh['brick_0'=4,'brick_1'=8,'brick_2'=2,'grp'=4] {'brick_0','brick_1'}, dimensions={0} | all-to-all | bytes 131072 | tf_op jit(solution)/shard_map/all_to_all | solution.py:45
  181.7 3.1 %shard_map.71 = (f32[4,128]{1,0:T(4,128)S(1)}, f32[4,128]{1,0:T(4,128)S(1)}) custom-call(s32[2]{0:T(128)S(1)} %pad_add_fusion.3.at_ref, bf16[128,4096]{1,0:T(8,128)(2,1)S(1)} %get-tuple-element.24.own_ref, bf16[128,4096]{1,0:T(8,128)(2,1)S(1)} %collective-permute-done.one_ref, bf16[128,4096]{1,0:T(8,128)(2,1)S(1)} %collective-permute-done.1.two_ref, ...), custom_call_target="tpu_custom_call" | custom-call | tf_op jit(solution)/shard_map/pallas_call | solution.py:461
  184.8 8.9 %all_to_all.86 = f32[8,4,128]{2,1,0:T(4,128)S(1)} all-to-all(f32[8,4,128]{2,1,0:T(4,128)S(1)} %broadcast_in_dim.136), channel_id=1, replica_groups=mesh['brick_0'=4,'brick_1'=8,'brick_2'=2,'grp'=4] {'brick_2','grp'}, dimensions={0} | all-to-all | bytes 32768 | tf_op jit(solution)/shard_map/all_to_all | solution.py:45
  193.8 11.9 %all_to_all.87.gathered_ref = f32[32,4,128]{2,1,0:T(4,128)S(1)} all-to-all(f32[32,4,128]{2,1,0:T(4,128)S(1)} %broadcast_in_dim.137), channel_id=1, replica_groups=mesh['brick_0'=4,'brick_1'=8,'brick_2'=2,'grp'=4] {'brick_0','brick_1'}, dimensions={0} | all-to-all | bytes 131072 | tf_op jit(solution)/shard_map/all_to_all | solution.py:45
  206.9 2.1 shard_map.72
  209.6 4.9 %all-to-all-start.11 = ((f32[8,32,128]{2,1,0:T(8,128)}), f32[8,32,128]{2,1,0:T(8,128)S(1)}, u32[]{:S(2)}, u32[]{:S(2)}) async-start(f32[8,32,128]{2,1,0:T(8,128)} %broadcast_in_dim.138), calls=%async_computation.11 | async-start | bytes 262144 | tf_op jit(solution)/shard_map/all_to_all | solution.py:45
  214.5 5.2 %all-to-all-done.11 = f32[8,32,128]{2,1,0:T(8,128)S(1)} async-done(((f32[8,32,128]{2,1,0:T(8,128)}), f32[8,32,128]{2,1,0:T(8,128)S(1)}, u32[]{:S(2)}, u32[]{:S(2)}) %all-to-all-start.11) | async-done | bytes 131104 | tf_op jit(solution)/shard_map/all_to_all | solution.py:45
  219.7 1.2 gather_fusion.2
  221.0 3.9 %all-to-all-start.12 = ((f32[32,4,128]{2,1,0:T(4,128)}), f32[32,4,128]{2,1,0:T(4,128)S(1)}, u32[]{:S(2)}, u32[]{:S(2)}) async-start(f32[32,4,128]{2,1,0:T(4,128)} %bitcast.16), calls=%async_computation.12 | async-start | bytes 131072 | tf_op jit(solution)/shard_map/all_to_all | solution.py:469
  224.8 8.8 %all-to-all-done.12 = f32[32,4,128]{2,1,0:T(4,128)S(1)} async-done(((f32[32,4,128]{2,1,0:T(4,128)}), f32[32,4,128]{2,1,0:T(4,128)S(1)}, u32[]{:S(2)}, u32[]{:S(2)}) %all-to-all-start.12) | async-done | bytes 65568 | tf_op jit(solution)/shard_map/all_to_all | solution.py:469
  (67 shorter events, 17.4 us)
Async XLA Ops:
  2.8 13.1 %all-to-all-start = ((f32[8,32,256]{2,1,0:T(8,128)}), f32[8,32,256]{2,1,0:T(8,128)S(1)}, u32[]{:S(2)}, u32[]{:S(2)}) async-start(f32[8,32,256]{2,1,0:T(8,128)} %pad_maximum_fusion), calls=%async_computation | async-start | bytes 524288 | tf_op jit(solution)/shard_map/all_to_all | solution.py:395
  9.3 6.6 %copy-start.5 = (s32[8192]{0:T(1024)S(1)}, s32[8192]{0:T(1024)}, u32[]{:S(2)}) copy-start(s32[8192]{0:T(1024)} %param.6) | copy-start | bytes 98308
  16.8 27.2 %collective-permute-start = (bf16[128,4096]{1,0:T(8,128)(2,1)}, bf16[128,4096]{1,0:T(8,128)(2,1)S(1)}, u32[]{:S(2)}, u32[]{:S(2)}) collective-permute-start(bf16[128,4096]{1,0:T(8,128)(2,1)} %get-tuple-element.25), channel_id=1, source_target_pairs={{0,1},{1,2},{2,3},{3,0},{4,5},{5,6},{6,7},{7,4},{8,9},{9,10},{10,1... | collective-permute-start | bytes 3145736 | tf_op jit(solution)/shard_map/ppermute | solution.py:414
  17.4 46.4 %collective-permute-start.1 = (bf16[128,4096]{1,0:T(8,128)(2,1)}, bf16[128,4096]{1,0:T(8,128)(2,1)S(1)}, u32[]{:S(2)}, u32[]{:S(2)}) collective-permute-start(bf16[128,4096]{1,0:T(8,128)(2,1)} %get-tuple-element.26), channel_id=1, source_target_pairs={{0,2},{1,3},{2,0},{3,1},{4,6},{5,7},{6,4},{7,5},{8,10},{9,11},{10,... | collective-permute-start | bytes 3145736 | tf_op jit(solution)/shard_map/ppermute | solution.py:414
  18.9 46.7 %collective-permute-start.2 = (bf16[128,4096]{1,0:T(8,128)(2,1)}, bf16[128,4096]{1,0:T(8,128)(2,1)}, u32[]{:S(2)}, u32[]{:S(2)}) collective-permute-start(bf16[128,4096]{1,0:T(8,128)(2,1)} %get-tuple-element.27), channel_id=1, source_target_pairs={{0,3},{1,0},{2,1},{3,2},{4,7},{5,4},{6,5},{7,6},{8,11},{9,8},{10,9... | collective-permute-start | bytes 3145736 | tf_op jit(solution)/shard_map/ppermute | solution.py:414
  21.9 19.6 %all-to-all-start.1 = ((f32[32,4,256]{2,1,0:T(4,128)}), f32[32,4,256]{2,1,0:T(4,128)S(1)}, u32[]{:S(2)}, u32[]{:S(2)}) async-start(f32[32,4,256]{2,1,0:T(4,128)} %all_to_all.50), calls=%async_computation.1 | async-start | bytes 262144 | tf_op jit(solution)/shard_map/all_to_all | solution.py:420
  42.2 81.7 %copy-start.4 = (f32[512]{0:T(512)S(1)}, f32[512]{0:T(512)}, u32[]{:S(2)}) copy-start(f32[512]{0:T(512)} %param.9) | copy-start | bytes 6148
  70.4 2.9 %collective-permute-start.3 = (f32[16,48,128]{2,1,0:T(8,128)S(1)}, f32[16,48,128]{2,1,0:T(8,128)S(1)}, u32[]{:S(2)}, u32[]{:S(2)}) collective-permute-start(f32[16,48,128]{2,1,0:T(8,128)S(1)} %get-tuple-element.33), channel_id=1, source_target_pairs={{0,4},{4,0},{1,5},{5,1},{2,6},{6,2},{3,7},{7,3},{8,12},{12,8},{9,1... | collective-permute-start | bytes 1179656 | tf_op jit(solution)/shard_map/ppermute | solution.py:439
  118.4 5.5 %collective-permute-start.4 = (f32[16,48,128]{2,1,0:T(8,128)S(1)}, f32[16,48,128]{2,1,0:T(8,128)S(1)}, u32[]{:S(2)}, u32[]{:S(2)}) collective-permute-start(f32[16,48,128]{2,1,0:T(8,128)S(1)} %all_to_all.81.mine_ref), channel_id=1, source_target_pairs={{0,4},{4,0},{1,5},{5,1},{2,6},{6,2},{3,7},{7,3},{8,12},{12,8},{9,1... | collective-permute-start | bytes 1179656 | tf_op jit(solution)/shard_map/ppermute | solution.py:443
  134.8 1.1 copy-start
  155.4 1.2 copy-start.1
  180.4 1.2 copy-start.2
  205.6 1.2 copy-start.3
  209.6 10.1 %all-to-all-start.11 = ((f32[8,32,128]{2,1,0:T(8,128)}), f32[8,32,128]{2,1,0:T(8,128)S(1)}, u32[]{:S(2)}, u32[]{:S(2)}) async-start(f32[8,32,128]{2,1,0:T(8,128)} %broadcast_in_dim.138), calls=%async_computation.11 | async-start | bytes 262144 | tf_op jit(solution)/shard_map/all_to_all | solution.py:45
  221.0 12.7 %all-to-all-start.12 = ((f32[32,4,128]{2,1,0:T(4,128)}), f32[32,4,128]{2,1,0:T(4,128)S(1)}, u32[]{:S(2)}, u32[]{:S(2)}) async-start(f32[32,4,128]{2,1,0:T(4,128)} %bitcast.16), calls=%async_computation.12 | async-start | bytes 131072 | tf_op jit(solution)/shard_map/all_to_all | solution.py:469

commit v4 on v3

--- a/solution.py
+++ b/solution.py
@@ -29,6 +29,7 @@
 DOUBLINGS = 4
 MAX_CORRECT = 48
 ACCEPT = 1e-4
+TINY = 1e-5
 
 move_limit = 1.0
 MIB = 1024 * 1024
@@ -113,9 +114,28 @@
     return jnp.concatenate(rows, axis=1)
 
 
-def columns(pieces, chunk):
-    to = slice(chunk * WIDTH, (chunk + 1) * WIDTH)
-    return jnp.concatenate([piece[:, to] for piece in pieces], axis=0)
+class Columns:
+    def __init__(self, pieces, full_ref, sems):
+        self.full_ref = full_ref
+        self.copies = []
+        for chunk in range(CHUNKS):
+            to = pl.ds(chunk * WIDTH, WIDTH)
+            self.copies.append(
+                [
+                    pltpu.make_async_copy(
+                        piece.at[:, to], full_ref.at[k, :, to], sems.at[chunk, k]
+                    )
+                    for k, piece in enumerate(pieces)
+                ]
+            )
+        for group in self.copies:
+            for copy in group:
+                copy.start()
+
+    def chunk(self, chunk):
+        for copy in self.copies[chunk]:
+            copy.wait()
+        return self.full_ref[:, :, chunk * WIDTH : (chunk + 1) * WIDTH].reshape(M, WIDTH)
 
 
 def slots(at_ref):
@@ -133,11 +153,11 @@
     return jnp.clip(-curv * (lin + pushed), -move_limit, move_limit)
 
 
-def product_of_trial(at_ref, pieces, curv_ref, lin_ref, lam_ref, part_ref):
+def product_of_trial(at_ref, columns, curv_ref, lin_ref, lam_ref, part_ref):
     lam_b = as_rows(at_ref, lam_ref)
     total = jnp.zeros((16, M), F32)
     for chunk in range(CHUNKS):
-        block = columns(pieces, chunk)
+        block = columns.chunk(chunk)
         moved = trial_chunk(block, curv_ref, lin_ref, lam_b, chunk).astype(BF)
         total += lax.dot_general(moved, block, NT, preferred_element_type=F32)
     for k, slot in enumerate(slots(at_ref)):
@@ -156,17 +176,17 @@
 
 
 def gram_kernel(
-    at_ref, own_ref, one_ref, two_ref, three_ref, curv_ref, lin_ref,
-    mine_ref, other_ref, gram_ref, prod_ref, block_ref, half_ref,
+    at_ref, own_hbm, one_hbm, two_hbm, three_hbm, curv_ref, lin_ref,
+    mine_ref, other_ref, gram_ref, prod_ref, block_ref, half_ref, full_ref, sems,
 ):
     core = at_ref[1]
-    pieces = (own_ref, one_ref, two_ref, three_ref)
+    columns = Columns((own_hbm, one_hbm, two_hbm, three_hbm), full_ref, sems)
     gram_ref[...] = jnp.zeros_like(gram_ref)
     prod_ref[...] = jnp.zeros_like(prod_ref)
     for s in range(SHARDS):
         half_ref[s // HALF, s % HALF, SHARD_G:, :] = jnp.zeros((8, 128), F32)
     for chunk in range(CHUNKS):
-        block = columns(pieces, chunk)
+        block = columns.chunk(chunk)
         curv, lin = flat_rows(curv_ref, chunk), flat_rows(lin_ref, chunk)
         weighted = (block.astype(F32) * curv).astype(BF)
         gram_ref[...] += lax.dot_general(weighted, block, NT, preferred_element_type=F32)
@@ -193,17 +213,18 @@
     return high, (value - high.astype(F32)).astype(BF)
 
 
-def times_split(a_high, a_low, b_high, b_low):
-    dot = functools.partial(jnp.dot, preferred_element_type=F32)
-    return dot(a_high, b_high) + (dot(a_high, b_low) + dot(a_low, b_high))
+def split_in_three(value):
+    high = value.astype(BF)
+    middle, low = split(value - high.astype(F32))
+    return high, middle, low
 
 
 def solve_kernel(
-    at_ref, own_ref, one_ref, two_ref, three_ref, mine_ref, other_ref, curv_ref, lin_ref, bound_ref,
+    at_ref, own_hbm, one_hbm, two_hbm, three_hbm, mine_ref, other_ref, curv_ref, lin_ref, bound_ref,
     inv_ref, scale_ref, lam_ref, part_ref,
-    half_ref, hess_ref, r_ref,
+    half_ref, hess_ref, r_ref, full_ref, sems,
 ):
-    pieces = (own_ref, one_ref, two_ref, three_ref)
+    columns = Columns((own_hbm, one_hbm, two_hbm, three_hbm), full_ref, sems)
     core = at_ref[1]
     half_ref[core] = mine_ref[...]
     half_ref[1 - core] = other_ref[...]
@@ -254,18 +275,16 @@
     lax.fori_loop(0, DOUBLINGS - 1, double, 0)
 
     def correct(precise):
+        dot = functools.partial(jnp.dot, preferred_element_type=F32)
+        x_high, x_low = split(inv_ref[...])
+        h_high, h_low, h_rest = split_in_three(hess_ref[...])
+        product = dot(h_high, x_high)
         if precise:
-            x = inv_ref[...]
-            x_high, x_low = split(x)
-            product = jnp.dot(
-                hess_ref[...], x, precision=lax.Precision.HIGHEST, preferred_element_type=F32
+            product += dot(h_high, x_low) + (
+                dot(h_low, x_high) + (dot(h_low, x_low) + dot(h_rest, x_high))
             )
         else:
-            x_high = inv_ref[...].astype(BF)
-            h_high, h_low = split(hess_ref[...])
-            product = jnp.dot(h_high, x_high, preferred_element_type=F32) + jnp.dot(
-                h_low, x_high, preferred_element_type=F32
-            )
+            product += dot(h_low, x_high)
         residual = eye() - product
         size = jnp.sum(residual * residual)
         good = size < M
@@ -273,11 +292,16 @@
         @pl.when(good)
         def _():
             r_high, r_low = split(residual)
+            step = dot(x_high, r_high)
+            inv_ref[...] = x_high.astype(F32) + step
             if precise:
-                inv_ref[...] += times_split(x_high, x_low, r_high, r_low)
-            else:
-                step = jnp.dot(x_high, r_high, preferred_element_type=F32)
-                inv_ref[...] = x_high.astype(F32) + step
+                inv_ref[...] += x_low.astype(F32)
+
+            if precise:
+
+                @pl.when(size > TINY)
+                def _():
+                    inv_ref[...] += dot(x_high, r_low) + dot(x_low, r_high)
 
         @pl.when(jnp.logical_not(good))
         def _():
@@ -326,7 +350,7 @@
     zero = jnp.zeros((NB, 128), F32)
     lam = newton_update(zero, total, bound_ref[...], inv_ref, scale)
     lam_ref[...] = lam
-    product_of_trial(at_ref, pieces, curv_ref, lin_ref, lam_ref, part_ref)
+    product_of_trial(at_ref, columns, curv_ref, lin_ref, lam_ref, part_ref)
 
 
 def updated(gathered_ref, lam_in_ref, bound_ref, inv_ref, scale_ref):
@@ -335,32 +359,35 @@
 
 
 def step_kernel(
-    at_ref, own_ref, one_ref, two_ref, three_ref, inv_ref,
+    at_ref, own_hbm, one_hbm, two_hbm, three_hbm, inv_ref,
     gathered_ref, lam_in_ref, curv_ref, lin_ref, bound_ref, scale_ref,
-    lam_ref, part_ref,
+    lam_ref, part_ref, full_ref, sems,
 ):
+    columns = Columns((own_hbm, one_hbm, two_hbm, three_hbm), full_ref, sems)
     lam_ref[...] = updated(gathered_ref, lam_in_ref, bound_ref, inv_ref, scale_ref)
-    pieces = (own_ref, one_ref, two_ref, three_ref)
-    product_of_trial(at_ref, pieces, curv_ref, lin_ref, lam_ref, part_ref)
+    product_of_trial(at_ref, columns, curv_ref, lin_ref, lam_ref, part_ref)
 
 
 def last_kernel(
-    at_ref, own_ref, one_ref, two_ref, three_ref, inv_ref,
+    at_ref, own_hbm, one_hbm, two_hbm, three_hbm, inv_ref,
     gathered_ref, lam_in_ref, curv_ref, lin_ref, bound_ref, scale_ref,
-    lam_ref, step_ref,
+    lam_ref, step_ref, full_ref, sems,
 ):
+    columns = Columns((own_hbm, one_hbm, two_hbm, three_hbm), full_ref, sems)
     lam_ref[...] = updated(gathered_ref, lam_in_ref, bound_ref, inv_ref, scale_ref)
     lam_b = as_rows(at_ref, lam_ref)
-    pieces = (own_ref, one_ref, two_ref, three_ref)
     count = WIDTH // 128
     for chunk in range(CHUNKS):
-        moved = trial_chunk(columns(pieces, chunk), curv_ref, lin_ref, lam_b, chunk)
+        moved = trial_chunk(columns.chunk(chunk), curv_ref, lin_ref, lam_b, chunk)
         for k in range(count):
             at = chunk * count + k
-            step_ref[at : at + 1, :] = moved[0:1, k * 128 : (k + 1) * 128]
+            for copy in range(step_ref.shape[0]):
+                step_ref[copy, at : at + 1, :] = moved[0:1, k * 128 : (k + 1) * 128]
 
 
 VM = pl.BlockSpec(memory_space=pltpu.VMEM)
+HBM = pl.BlockSpec(memory_space=pltpu.HBM)
+FULL = [pltpu.VMEM((NB, ROWS, COLS), BF), pltpu.SemaphoreType.DMA((CHUNKS, NB))]
 SM = pl.BlockSpec(memory_space=pltpu.SMEM)
 
 
@@ -392,26 +419,19 @@
     at = jnp.stack([quarter, core]).astype(jnp.int32)
 
     near = size_of(NEAR)
-    both = lax.all_to_all(
-        jnp.concatenate(
-            [
-                jnp.broadcast_to(vector.reshape(1, BLKS, 128), (near, BLKS, 128))
-                for vector in (weights, linear)
-            ],
-            axis=2,
-        ),
-        NEAR, 0, 0, tiled=True,
-    )
-
-    slices = [
-        lax.dynamic_slice(gradients, (0, lax.rem(quarter + k, 4) * COLS), (ROWS, COLS))
-        for k in range(NB)
-    ]
-    *slices, both, perm = lax.optimization_barrier((*slices, both, perm))
-    pieces = [slices[0]]
-    for k in (1, 2, 3):
-        ring = [(i, (i + k) % 4) for i in range(4)]
-        pieces.append(lax.ppermute(slices[k], "grp", ring))
+    both = jnp.concatenate([weights.reshape(1, BLKS, 128), linear.reshape(1, BLKS, 128)], axis=2)
+    both = jnp.broadcast_to(both, (near, BLKS, 256))
+    both = lax.all_to_all(both, NEAR, 0, 0, tiled=True)
+
+    pieces, last = [None] * NB, gradients
+    for k in (1, 3, 2, 0):
+        to = lax.rem(quarter + k, NB) * COLS
+        piece = lax.dynamic_slice(last, (0, to), (ROWS, COLS))
+        piece, last = lax.optimization_barrier((piece, last))
+        if k:
+            piece = lax.ppermute(piece, "grp", [(i, (i + k) % NB) for i in range(NB)])
+        pieces[k] = piece
+    both, perm = lax.optimization_barrier((both, perm))
 
     incoming, leaving, back, place = layout_tables(perm, here, per_brick)
     incoming = lax.dynamic_slice_in_dim(incoming, quarter * BLKS, BLKS)
@@ -424,16 +444,19 @@
     packed = (HALF, SHARD, 128)
     mine, other = call(
         gram_kernel,
-        [SM] + [VM] * 6,
+        [SM] + [HBM] * NB + [VM] * 2,
         [sds(packed), sds(packed)],
         [
             pltpu.VMEM((M, M), F32),
             pltpu.VMEM((16, M), F32),
             pltpu.VMEM((NB, NB, 128, 128), F32),
             pltpu.VMEM((2, *packed), F32),
+            *FULL,
         ],
-        20,
+        24,
     )(at, *pieces, curv, lin)
+
+    pieces = [pltpu.with_memory_space_constraint(piece, pltpu.HBM) for piece in pieces]
 
     swap = [(0, 1), (1, 0)]
     mine = mine + lax.ppermute(other, "brick_2", swap)
@@ -447,25 +470,26 @@
     vector = sds((NB, 128))
     inv, scale, lam, part = call(
         solve_kernel,
-        [SM] + [VM] * 9,
+        [SM] + [HBM] * NB + [VM] * 5,
         [square, vector, vector, vector],
         [
             pltpu.VMEM((2, *packed), F32),
             pltpu.VMEM((M, M), F32),
             pltpu.VMEM((M, M), F32),
+            *FULL,
         ],
-        28,
+        32,
     )(at, *pieces, mine, other, curv, lin, bound)
-    ins = [SM] + [VM] * 11
+    ins = [SM] + [HBM] * NB + [VM] * 7
     for _ in range(ITERS - 2):
-        lam, part = call(step_kernel, ins, [vector, vector], [], 16)(
+        lam, part = call(step_kernel, ins, [vector, vector], FULL, 20)(
             at, *pieces, inv, summed(part), lam, curv, lin, bound, scale
         )
-    lam, result = call(last_kernel, ins, [vector, sds((BLKS, 128))], [], 16)(
+    lam, result = call(last_kernel, ins, [vector, sds((size_of(NEAR), BLKS, 128))], FULL, 20)(
         at, *pieces, inv, summed(part), lam, curv, lin, bound, scale
     )
 
-    whole = from_everyone(result, NEAR).reshape(-1, 128)
+    whole = lax.all_to_all(result, NEAR, 0, 0, tiled=True).reshape(-1, 128)
     arrived = lax.all_to_all(whole[back], FAR, 0, 0, tiled=True)
     return (arrived[place].reshape(-1), lam.reshape(-1))
 

time: 236 us -> 231 us (0.979)
  waiting for transfers between devices: 50.6 us -> 45.1 us
  Pallas kernels: 24.1 us -> 27.1 us
    unnamed x12 -> x10, local copies, waits for them, and re-layouts: 4.73 us -> 0.02 us
    dynamic_slice x1 -> x4, local copies, waits for them, and re-layouts: 3.9 us -> 8.19 us  [on_device(): piece = lax.dynamic_slice(last, (0, to), (ROWS, COLS))]
    ppermute x3, waiting for transfers between devices: 23.4 us -> 20.4 us  [on_device(): piece = lax.ppermute(piece, 'grp', [(i, (i + k) % NB) for i in range(NB)])]
    pallas_call x5, Pallas kernels: 24.1 us -> 27.1 us  [the longest x1 10.5 us: on_device(): call(solve_kernel, [SM] + [HBM] * NB + [VM] * 5, [square, vector, vector,...]
    all_to_all x2, waiting for transfers between devices: 7.74 us -> 5.19 us  [the longest x1 5.18 us: on_device(): whole = lax.all_to_all(result, NEAR, 0, 0, tiled=True).reshape(-1, 128)]
  transfers between devices with their start and end apart: 9 -> 9, of which waited for: 9 -> 7; matrix products, arithmetic and copies ran while one was open for 3% -> 5% of each run, Pallas kernels for 0% -> 0%
where the time goes in v4:
time: 231 us; the launch traced here: 230 us
  blocking collectives  104 us (45%)
  waiting for transfers between devices  45.1 us (20%)
  starting transfers between devices  35 us (15%)
  Pallas kernels  27.1 us (12%)
  local copies, waits for them, and re-layouts  14.2 us (6%)
  other arithmetic  3.93 us (2%)
    all_to_all x8, blocking collectives, from_everyone(): lax.all_to_all(jnp.broadcast_to(array[None], (devices, *array.shape)), ax...  88.8 us
    ppermute x3, waiting for transfers between devices, on_device(): piece = lax.ppermute(piece, 'grp', [(i, (i + k) % NB) for i in range(NB)])  20.4 us
    all_to_all x1, blocking collectives, on_device(): shard = lax.all_to_all(mine, PLANE, 0, 0, tiled=True).sum(axis=0)  15.4 us
    pallas_call x1, Pallas kernels, on_device(): call(solve_kernel, [SM] + [HBM] * NB + [VM] * 5, [square, vector, vector,...  10.5 us
    all_to_all x1, starting transfers between devices, on_device(): both = lax.all_to_all(both, FAR, 0, 0, tiled=True)  10.5 us
    all_to_all x1, waiting for transfers between devices, on_device(): arrived = lax.all_to_all(whole[back], FAR, 0, 0, tiled=True)  8.85 us
    dynamic_slice x4, local copies, waits for them, and re-layouts, on_device(): piece = lax.dynamic_slice(last, (0, to), (ROWS, COLS))  8.19 us
    all_to_all x1, waiting for transfers between devices, on_device(): both = lax.all_to_all(both, FAR, 0, 0, tiled=True)  7.93 us
  transfers between devices with their start and end apart: 9, of which 7 were waited for; matrix products, arithmetic and copies ran while one was open for 5% of the time, Pallas kernels for 0%

profile of v4, /device:TPU:1, one launch (start us, length us, event | category | flops | bytes accessed | tf_op | source)
XLA Modules:
  0.0 230.4 jit_solution(18175143730153370483)
XLA Ops:
  2.1 6.5 %all-to-all-start = ((f32[8,32,256]{2,1,0:T(8,128)}), f32[8,32,256]{2,1,0:T(8,128)S(1)}, u32[]{:S(2)}, u32[]{:S(2)}) async-start(f32[8,32,256]{2,1,0:T(8,128)} %broadcast_in_dim.58), calls=%async_computation | async-start | bytes 524288 | tf_op jit(solution)/shard_map/all_to_all | solution.py:424
  8.6 2.3 %constant_dynamic-slice_fusion.4 = bf16[128,4096]{1,0:T(8,128)(2,1)} fusion(bf16[128,16384]{1,0:T(8,128)(2,1)} %param.5, s32[]{:T(128)S(6)} %select_n.122), kind=kLoop, calls=%fused_computation.58 | loop fusion | bytes 2097156 | tf_op jit(solution)/shard_map/dynamic_slice | solution.py:429
  10.9 2.3 constant_dynamic-slice_fusion.3
  13.2 2.3 constant_dynamic-slice_fusion.2
  15.5 2.9 %collective-permute-start.1 = (bf16[128,4096]{1,0:T(8,128)(2,1)}, bf16[128,4096]{1,0:T(8,128)(2,1)S(1)}, u32[]{:S(2)}, u32[]{:S(2)}) collective-permute-start(bf16[128,4096]{1,0:T(8,128)(2,1)} %constant_dynamic-slice_fusion.2), channel_id=1, source_target_pairs={{0,2},{1,3},{2,0},{3,1},{4,6},{5,7},{6,4},{7,5},{8,10},{9,11},{10,... | collective-permute-start | bytes 3145736 | tf_op jit(solution)/shard_map/ppermute | solution.py:432
  19.9 1.3 constant_dynamic-slice_fusion.1.own_hbm
  24.2 10.5 %all-to-all-start.1 = ((f32[32,4,256]{2,1,0:T(4,128)}), f32[32,4,256]{2,1,0:T(4,128)S(1)}, u32[]{:S(2)}, u32[]{:S(2)}) async-start(f32[32,4,256]{2,1,0:T(4,128)} %all_to_all.50), calls=%async_computation.1 | async-start | bytes 262144 | tf_op jit(solution)/shard_map/all_to_all | solution.py:440
  35.9 7.9 %all-to-all-done.1 = f32[32,4,256]{2,1,0:T(4,128)S(1)} async-done(((f32[32,4,256]{2,1,0:T(4,128)}), f32[32,4,256]{2,1,0:T(4,128)S(1)}, u32[]{:S(2)}, u32[]{:S(2)}) %all-to-all-start.1) | async-done | bytes 131104 | tf_op jit(solution)/shard_map/all_to_all | solution.py:440
  44.5 19.9 %collective-permute-done.2.three_hbm = bf16[128,4096]{1,0:T(8,128)(2,1)S(1)} collective-permute-done((bf16[128,4096]{1,0:T(8,128)(2,1)}, bf16[128,4096]{1,0:T(8,128)(2,1)S(1)}, u32[]{:S(2)}, u32[]{:S(2)}) %collective-permute-start.2) | collective-permute-done | bytes 1048608 | tf_op jit(solution)/shard_map/ppermute | solution.py:432
  64.9 5.2 %shard_map.68 = (f32[16,48,128]{2,1,0:T(8,128)S(1)}, f32[16,48,128]{2,1,0:T(8,128)S(1)}) custom-call(s32[2]{0:T(128)S(1)} %pad_add_fusion.3.at_ref, bf16[128,4096]{1,0:T(8,128)(2,1)S(1)} %constant_dynamic-slice_fusion.1.own_hbm, bf16[128,4096]{1,0:T(8,128)(2,1)} %collective-permute-done.one_hbm, bf16[128,4096]{1,0:T(8,128)(2,1)S(1)} %collective-permute-done.1.two_hbm, ...), custom_call_target="tpu_custom_call" | custom-call | tf_op jit(solution)/shard_map/pallas_call | solution.py:445
  70.8 1.3 collective-permute-done.3
  72.2 15.4 %all_to_all.79 = f32[16,48,128]{2,1,0:T(8,128)} all-to-all(f32[16,48,128]{2,1,0:T(8,128)S(1)} %add.136), channel_id=1, replica_groups=mesh['brick_0'=4,'brick_1'=8,'brick_2'=2,'grp'=4] {'brick_0','grp'}, dimensions={0} | all-to-all | bytes 786432 | tf_op jit(solution)/shard_map/all_to_all | solution.py:463
  88.7 16.7 %all_to_all.80 = f32[8,48,128]{2,1,0:T(8,128)S(1)} all-to-all(f32[8,48,128]{2,1,0:T(8,128)S(1)} %broadcast_in_dim.64), channel_id=1, replica_groups=mesh['brick_0'=4,'brick_1'=8,'brick_2'=2,'grp'=4] {'brick_1'}, dimensions={0} | all-to-all | bytes 393216 | tf_op jit(solution)/shard_map/all_to_all | solution.py:46
  105.5 11.1 %all_to_all.81.mine_ref = f32[16,48,128]{2,1,0:T(8,128)S(1)} all-to-all(f32[16,48,128]{2,1,0:T(8,128)S(1)} %broadcast_in_dim.65), channel_id=1, replica_groups=mesh['brick_0'=4,'brick_1'=8,'brick_2'=2,'grp'=4] {'brick_0','grp'}, dimensions={0} | all-to-all | bytes 786432 | tf_op jit(solution)/shard_map/all_to_all | solution.py:46
  116.6 4.1 %collective-permute-start.4 = (f32[16,48,128]{2,1,0:T(8,128)S(1)}, f32[16,48,128]{2,1,0:T(8,128)S(1)}, u32[]{:S(2)}, u32[]{:S(2)}) collective-permute-start(f32[16,48,128]{2,1,0:T(8,128)S(1)} %all_to_all.81.mine_ref), channel_id=1, source_target_pairs={{0,4},{4,0},{1,5},{5,1},{2,6},{6,2},{3,7},{7,3},{8,12},{12,8},{9,1... | collective-permute-start | bytes 1179656 | tf_op jit(solution)/shard_map/ppermute | solution.py:466
  120.7 1.3 collective-permute-done.4.other_ref
  122.1 10.5 %shard_map.69 = (f32[512,512]{1,0:T(8,128)S(1)}, f32[4,128]{1,0:T(4,128)S(1)}, f32[4,128]{1,0:T(4,128)S(1)}, f32[4,128]{1,0:T(4,128)S(1)}) custom-call(s32[2]{0:T(128)S(1)} %pad_add_fusion.3.at_ref, bf16[128,4096]{1,0:T(8,128)(2,1)} %copy-done, bf16[128,4096]{1,0:T(8,128)(2,1)} %collective-permute-done.one_hbm, bf16[128,4096]{1,0:T(8,128)(2,1)} %copy-done.1, ...), custom_call_target="tpu_custom_call" | custom-call | tf_op jit(solution)/shard_map/pallas_call | solution.py:471
  132.6 7.6 %all_to_all.82 = f32[8,4,128]{2,1,0:T(4,128)S(1)} all-to-all(f32[8,4,128]{2,1,0:T(4,128)S(1)} %broadcast_in_dim.66), channel_id=1, replica_groups=mesh['brick_0'=4,'brick_1'=8,'brick_2'=2,'grp'=4] {'brick_2','grp'}, dimensions={0} | all-to-all | bytes 32768 | tf_op jit(solution)/shard_map/all_to_all | solution.py:46
  140.2 11.8 %all_to_all.83.gathered_ref = f32[32,4,128]{2,1,0:T(4,128)S(1)} all-to-all(f32[32,4,128]{2,1,0:T(4,128)S(1)} %broadcast_in_dim.67), channel_id=1, replica_groups=mesh['brick_0'=4,'brick_1'=8,'brick_2'=2,'grp'=4] {'brick_0','brick_1'}, dimensions={0} | all-to-all | bytes 131072 | tf_op jit(solution)/shard_map/all_to_all | solution.py:46
  152.1 3.8 %shard_map.70 = (f32[4,128]{1,0:T(4,128)S(1)}, f32[4,128]{1,0:T(4,128)S(1)}) custom-call(s32[2]{0:T(128)S(1)} %pad_add_fusion.3.at_ref, bf16[128,4096]{1,0:T(8,128)(2,1)} %copy-done, bf16[128,4096]{1,0:T(8,128)(2,1)} %collective-permute-done.one_hbm, bf16[128,4096]{1,0:T(8,128)(2,1)} %copy-done.1, bf16[128,4096]{1,0:T(8,128)(2,1)} %copy-done.2, ...), custom_call_target="tpu_custom_call" | custom-call | tf_op jit(solution)/shard_map/pallas_call | solution.py:485
  155.9 8.8 %all_to_all.84 = f32[8,4,128]{2,1,0:T(4,128)S(1)} all-to-all(f32[8,4,128]{2,1,0:T(4,128)S(1)} %broadcast_in_dim.68), channel_id=1, replica_groups=mesh['brick_0'=4,'brick_1'=8,'brick_2'=2,'grp'=4] {'brick_2','grp'}, dimensions={0} | all-to-all | bytes 32768 | tf_op jit(solution)/shard_map/all_to_all | solution.py:46
  164.7 11.9 %all_to_all.85.gathered_ref = f32[32,4,128]{2,1,0:T(4,128)S(1)} all-to-all(f32[32,4,128]{2,1,0:T(4,128)S(1)} %broadcast_in_dim.69), channel_id=1, replica_groups=mesh['brick_0'=4,'brick_1'=8,'brick_2'=2,'grp'=4] {'brick_0','brick_1'}, dimensions={0} | all-to-all | bytes 131072 | tf_op jit(solution)/shard_map/all_to_all | solution.py:46
  176.6 3.8 %shard_map.71 = (f32[4,128]{1,0:T(4,128)S(1)}, f32[4,128]{1,0:T(4,128)S(1)}) custom-call(s32[2]{0:T(128)S(1)} %pad_add_fusion.3.at_ref, bf16[128,4096]{1,0:T(8,128)(2,1)} %copy-done, bf16[128,4096]{1,0:T(8,128)(2,1)} %collective-permute-done.one_hbm, bf16[128,4096]{1,0:T(8,128)(2,1)} %copy-done.1, bf16[128,4096]{1,0:T(8,128)(2,1)} %copy-done.2, ...), custom_call_target="tpu_custom_call" | custom-call | tf_op jit(solution)/shard_map/pallas_call | solution.py:485
  180.5 8.9 %all_to_all.86 = f32[8,4,128]{2,1,0:T(4,128)S(1)} all-to-all(f32[8,4,128]{2,1,0:T(4,128)S(1)} %broadcast_in_dim.70), channel_id=1, replica_groups=mesh['brick_0'=4,'brick_1'=8,'brick_2'=2,'grp'=4] {'brick_2','grp'}, dimensions={0} | all-to-all | bytes 32768 | tf_op jit(solution)/shard_map/all_to_all | solution.py:46
  189.4 11.9 %all_to_all.87.gathered_ref = f32[32,4,128]{2,1,0:T(4,128)S(1)} all-to-all(f32[32,4,128]{2,1,0:T(4,128)S(1)} %broadcast_in_dim.122), channel_id=1, replica_groups=mesh['brick_0'=4,'brick_1'=8,'brick_2'=2,'grp'=4] {'brick_0','brick_1'}, dimensions={0} | all-to-all | bytes 131072 | tf_op jit(solution)/shard_map/all_to_all | solution.py:46
  201.3 3.8 %shard_map.72 = (f32[4,128]{1,0:T(4,128)}, f32[8,32,128]{2,1,0:T(8,128)}) custom-call(s32[2]{0:T(128)S(1)} %pad_add_fusion.3.at_ref, bf16[128,4096]{1,0:T(8,128)(2,1)} %copy-done, bf16[128,4096]{1,0:T(8,128)(2,1)} %collective-permute-done.one_hbm, bf16[128,4096]{1,0:T(8,128)(2,1)} %copy-done.1, bf16[128,4096]{1,0:T(8,128)(2,1)} %copy-done.2, ...), custom_call_target="tpu_custom_call" | custom-call | tf_op jit(solution)/shard_map/pallas_call | solution.py:488
  205.1 5.0 %all-to-all-start.11 = ((f32[8,32,128]{2,1,0:T(8,128)}), f32[8,32,128]{2,1,0:T(8,128)S(1)}, u32[]{:S(2)}, u32[]{:S(2)}) async-start(f32[8,32,128]{2,1,0:T(8,128)} %get-tuple-element.48), calls=%async_computation.11 | async-start | bytes 262144 | tf_op jit(solution)/shard_map/all_to_all | solution.py:492
  210.1 5.2 %all-to-all-done.11 = f32[8,32,128]{2,1,0:T(8,128)S(1)} async-done(((f32[8,32,128]{2,1,0:T(8,128)}), f32[8,32,128]{2,1,0:T(8,128)S(1)}, u32[]{:S(2)}, u32[]{:S(2)}) %all-to-all-start.11) | async-done | bytes 131104 | tf_op jit(solution)/shard_map/all_to_all | solution.py:492
  215.2 1.2 gather_fusion.2
  216.5 3.9 %all-to-all-start.12 = ((f32[32,4,128]{2,1,0:T(4,128)}), f32[32,4,128]{2,1,0:T(4,128)S(1)}, u32[]{:S(2)}, u32[]{:S(2)}) async-start(f32[32,4,128]{2,1,0:T(4,128)} %bitcast.17), calls=%async_computation.12 | async-start | bytes 131072 | tf_op jit(solution)/shard_map/all_to_all | solution.py:493
  220.4 8.8 %all-to-all-done.12 = f32[32,4,128]{2,1,0:T(4,128)S(1)} async-done(((f32[32,4,128]{2,1,0:T(4,128)}), f32[32,4,128]{2,1,0:T(4,128)S(1)}, u32[]{:S(2)}, u32[]{:S(2)}) %all-to-all-start.12) | async-done | bytes 65568 | tf_op jit(solution)/shard_map/all_to_all | solution.py:493
  229.2 1.2 gather_fusion.3
  (66 shorter events, 10.2 us)
Async XLA Ops:
  2.1 19.2 %all-to-all-start = ((f32[8,32,256]{2,1,0:T(8,128)}), f32[8,32,256]{2,1,0:T(8,128)S(1)}, u32[]{:S(2)}, u32[]{:S(2)}) async-start(f32[8,32,256]{2,1,0:T(8,128)} %broadcast_in_dim.58), calls=%async_computation | async-start | bytes 524288 | tf_op jit(solution)/shard_map/all_to_all | solution.py:424
  8.6 12.7 %copy-start.4 = (s32[8192]{0:T(1024)S(1)}, s32[8192]{0:T(1024)}, u32[]{:S(2)}) copy-start(s32[8192]{0:T(1024)} %param.6) | copy-start | bytes 98308
  15.5 29.0 %collective-permute-start.1 = (bf16[128,4096]{1,0:T(8,128)(2,1)}, bf16[128,4096]{1,0:T(8,128)(2,1)S(1)}, u32[]{:S(2)}, u32[]{:S(2)}) collective-permute-start(bf16[128,4096]{1,0:T(8,128)(2,1)} %constant_dynamic-slice_fusion.2), channel_id=1, source_target_pairs={{0,2},{1,3},{2,0},{3,1},{4,6},{5,7},{6,4},{7,5},{8,10},{9,11},{10,... | collective-permute-start | bytes 3145736 | tf_op jit(solution)/shard_map/ppermute | solution.py:432
  18.4 46.0 %collective-permute-start.2 = (bf16[128,4096]{1,0:T(8,128)(2,1)}, bf16[128,4096]{1,0:T(8,128)(2,1)S(1)}, u32[]{:S(2)}, u32[]{:S(2)}) collective-permute-start(bf16[128,4096]{1,0:T(8,128)(2,1)} %constant_dynamic-slice_fusion.3), channel_id=1, source_target_pairs={{0,3},{1,0},{2,1},{3,2},{4,7},{5,4},{6,5},{7,6},{8,11},{9,8},{10,9... | collective-permute-start | bytes 3145736 | tf_op jit(solution)/shard_map/ppermute | solution.py:432
  19.3 45.6 %collective-permute-start = (bf16[128,4096]{1,0:T(8,128)(2,1)}, bf16[128,4096]{1,0:T(8,128)(2,1)}, u32[]{:S(2)}, u32[]{:S(2)}) collective-permute-start(bf16[128,4096]{1,0:T(8,128)(2,1)} %constant_dynamic-slice_fusion.4), channel_id=1, source_target_pairs={{0,1},{1,2},{2,3},{3,0},{4,5},{5,6},{6,7},{7,4},{8,9},{9,10},{10,1... | collective-permute-start | bytes 3145736 | tf_op jit(solution)/shard_map/ppermute | solution.py:432
  21.2 66.5 %copy-start = (bf16[128,4096]{1,0:T(8,128)(2,1)}, bf16[128,4096]{1,0:T(8,128)(2,1)S(1)}, u32[]{:S(2)}) copy-start(bf16[128,4096]{1,0:T(8,128)(2,1)S(1)} %constant_dynamic-slice_fusion.1.own_hbm) | copy-start | bytes 3145732
  24.2 19.6 %all-to-all-start.1 = ((f32[32,4,256]{2,1,0:T(4,128)}), f32[32,4,256]{2,1,0:T(4,128)S(1)}, u32[]{:S(2)}, u32[]{:S(2)}) async-start(f32[32,4,256]{2,1,0:T(4,128)} %all_to_all.50), calls=%async_computation.1 | async-start | bytes 262144 | tf_op jit(solution)/shard_map/all_to_all | solution.py:440
  44.5 77.6 %copy-start.3 = (f32[512]{0:T(512)S(1)}, f32[512]{0:T(512)}, u32[]{:S(2)}) copy-start(f32[512]{0:T(512)} %param.9) | copy-start | bytes 6148
  44.5 72.1 %copy-start.1 = (bf16[128,4096]{1,0:T(8,128)(2,1)}, bf16[128,4096]{1,0:T(8,128)(2,1)S(1)}, u32[]{:S(2)}) copy-start(bf16[128,4096]{1,0:T(8,128)(2,1)S(1)} %collective-permute-done.1.two_hbm) | copy-start | bytes 3145732
  64.4 52.2 %copy-start.2 = (bf16[128,4096]{1,0:T(8,128)(2,1)}, bf16[128,4096]{1,0:T(8,128)(2,1)S(1)}, u32[]{:S(2)}) copy-start(bf16[128,4096]{1,0:T(8,128)(2,1)S(1)} %collective-permute-done.2.three_hbm) | copy-start | bytes 3145732
  70.1 2.1 collective-permute-start.3
  116.6 5.5 %collective-permute-start.4 = (f32[16,48,128]{2,1,0:T(8,128)S(1)}, f32[16,48,128]{2,1,0:T(8,128)S(1)}, u32[]{:S(2)}, u32[]{:S(2)}) collective-permute-start(f32[16,48,128]{2,1,0:T(8,128)S(1)} %all_to_all.81.mine_ref), channel_id=1, source_target_pairs={{0,4},{4,0},{1,5},{5,1},{2,6},{6,2},{3,7},{7,3},{8,12},{12,8},{9,1... | collective-permute-start | bytes 1179656 | tf_op jit(solution)/shard_map/ppermute | solution.py:466
  205.1 10.2 %all-to-all-start.11 = ((f32[8,32,128]{2,1,0:T(8,128)}), f32[8,32,128]{2,1,0:T(8,128)S(1)}, u32[]{:S(2)}, u32[]{:S(2)}) async-start(f32[8,32,128]{2,1,0:T(8,128)} %get-tuple-element.48), calls=%async_computation.11 | async-start | bytes 262144 | tf_op jit(solution)/shard_map/all_to_all | solution.py:492
  216.5 12.7 %all-to-all-start.12 = ((f32[32,4,128]{2,1,0:T(4,128)}), f32[32,4,128]{2,1,0:T(4,128)S(1)}, u32[]{:S(2)}, u32[]{:S(2)}) async-start(f32[32,4,128]{2,1,0:T(4,128)} %bitcast.17), calls=%async_computation.12 | async-start | bytes 131072 | tf_op jit(solution)/shard_map/all_to_all | solution.py:493

commit v5 on v4

--- a/solution.py
+++ b/solution.py
@@ -379,10 +379,10 @@
     count = WIDTH // 128
     for chunk in range(CHUNKS):
         moved = trial_chunk(columns.chunk(chunk), curv_ref, lin_ref, lam_b, chunk)
-        for k in range(count):
-            at = chunk * count + k
-            for copy in range(step_ref.shape[0]):
-                step_ref[copy, at : at + 1, :] = moved[0:1, k * 128 : (k + 1) * 128]
+        lines = [moved[0:1, k * 128 : (k + 1) * 128] for k in range(count)]
+        lines = jnp.concatenate(lines, axis=0)
+        for copy in range(step_ref.shape[0]):
+            step_ref[copy, chunk * count : (chunk + 1) * count, :] = lines
 
 
 VM = pl.BlockSpec(memory_space=pltpu.VMEM)
@@ -419,10 +419,6 @@
     at = jnp.stack([quarter, core]).astype(jnp.int32)
 
     near = size_of(NEAR)
-    both = jnp.concatenate([weights.reshape(1, BLKS, 128), linear.reshape(1, BLKS, 128)], axis=2)
-    both = jnp.broadcast_to(both, (near, BLKS, 256))
-    both = lax.all_to_all(both, NEAR, 0, 0, tiled=True)
-
     pieces, last = [None] * NB, gradients
     for k in (1, 3, 2, 0):
         to = lax.rem(quarter + k, NB) * COLS
@@ -431,7 +427,9 @@
         if k:
             piece = lax.ppermute(piece, "grp", [(i, (i + k) % NB) for i in range(NB)])
         pieces[k] = piece
-    both, perm = lax.optimization_barrier((both, perm))
+    both = jnp.concatenate([weights.reshape(1, BLKS, 128), linear.reshape(1, BLKS, 128)], axis=2)
+    both = jnp.broadcast_to(both, (near, BLKS, 256))
+    both = lax.all_to_all(both, NEAR, 0, 0, tiled=True)
 
     incoming, leaving, back, place = layout_tables(perm, here, per_brick)
     incoming = lax.dynamic_slice_in_dim(incoming, quarter * BLKS, BLKS)
@@ -456,7 +454,9 @@
         24,
     )(at, *pieces, curv, lin)
 
-    pieces = [pltpu.with_memory_space_constraint(piece, pltpu.HBM) for piece in pieces]
+    pieces = pieces[:2] + [
+        pltpu.with_memory_space_constraint(piece, pltpu.HBM) for piece in pieces[2:]
+    ]
 
     swap = [(0, 1), (1, 0)]
     mine = mine + lax.ppermute(other, "brick_2", swap)

time: 231 us -> 232 us (level)
  no operation moved by 1% of the time
where the time goes in v5:
time: 232 us; the launch traced here: 231 us
  blocking collectives  104 us (45%)
  waiting for transfers between devices  45.8 us (20%)
  starting transfers between devices  35 us (15%)
  Pallas kernels  26.7 us (12%)
  local copies, waits for them, and re-layouts  14.2 us (6%)
  other arithmetic  4.18 us (2%)
    all_to_all x8, blocking collectives, from_everyone(): lax.all_to_all(jnp.broadcast_to(array[None], (devices, *array.shape)), ax...  88.9 us
    ppermute x3, waiting for transfers between devices, on_device(): piece = lax.ppermute(piece, 'grp', [(i, (i + k) % NB) for i in range(NB)])  20.1 us
    all_to_all x1, blocking collectives, on_device(): shard = lax.all_to_all(mine, PLANE, 0, 0, tiled=True).sum(axis=0)  15.4 us
    pallas_call x1, Pallas kernels, on_device(): call(solve_kernel, [SM] + [HBM] * NB + [VM] * 5, [square, vector, vector,...  10.6 us
    all_to_all x1, starting transfers between devices, on_device(): both = lax.all_to_all(both, FAR, 0, 0, tiled=True)  10.5 us
    all_to_all x1, waiting for transfers between devices, on_device(): both = lax.all_to_all(both, FAR, 0, 0, tiled=True)  8.94 us
    all_to_all x1, waiting for transfers between devices, on_device(): arrived = lax.all_to_all(whole[back], FAR, 0, 0, tiled=True)  8.85 us
    dynamic_slice x4, local copies, waits for them, and re-layouts, on_device(): piece = lax.dynamic_slice(last, (0, to), (ROWS, COLS))  8.25 us
  transfers between devices with their start and end apart: 9, of which 7 were waited for; matrix products, arithmetic and copies ran while one was open for 5% of the time, Pallas kernels for 0%

profile of v5, /device:TPU:1, one launch (start us, length us, event | category | flops | bytes accessed | tf_op | source)
XLA Modules:
  0.0 231.1 jit_solution(5319142319396038655)
XLA Ops:
  2.1 6.5 %all-to-all-start = ((f32[8,32,256]{2,1,0:T(8,128)}), f32[8,32,256]{2,1,0:T(8,128)S(1)}, u32[]{:S(2)}, u32[]{:S(2)}) async-start(f32[8,32,256]{2,1,0:T(8,128)} %broadcast_in_dim.58), calls=%async_computation | async-start | bytes 524288 | tf_op jit(solution)/shard_map/all_to_all | solution.py:432
  8.6 2.4 %constant_dynamic-slice_fusion.4 = bf16[128,4096]{1,0:T(8,128)(2,1)} fusion(bf16[128,16384]{1,0:T(8,128)(2,1)} %param.5, s32[]{:T(128)S(6)} %select_n.122), kind=kLoop, calls=%fused_computation.58 | loop fusion | bytes 2097156 | tf_op jit(solution)/shard_map/dynamic_slice | solution.py:425
  11.0 2.3 constant_dynamic-slice_fusion.3
  13.3 2.3 constant_dynamic-slice_fusion.2
  15.6 2.9 %collective-permute-start.1 = (bf16[128,4096]{1,0:T(8,128)(2,1)}, bf16[128,4096]{1,0:T(8,128)(2,1)S(1)}, u32[]{:S(2)}, u32[]{:S(2)}) collective-permute-start(bf16[128,4096]{1,0:T(8,128)(2,1)} %constant_dynamic-slice_fusion.2), channel_id=1, source_target_pairs={{0,2},{1,3},{2,0},{3,1},{4,6},{5,7},{6,4},{7,5},{8,10},{9,11},{10,... | collective-permute-start | bytes 3145736 | tf_op jit(solution)/shard_map/ppermute | solution.py:428
  21.4 1.3 constant_dynamic-slice_fusion.1.own_hbm
  24.5 10.5 %all-to-all-start.1 = ((f32[32,4,256]{2,1,0:T(4,128)}), f32[32,4,256]{2,1,0:T(4,128)S(1)}, u32[]{:S(2)}, u32[]{:S(2)}) async-start(f32[32,4,256]{2,1,0:T(4,128)} %all_to_all.50), calls=%async_computation.1 | async-start | bytes 262144 | tf_op jit(solution)/shard_map/all_to_all | solution.py:438
  35.2 8.9 %all-to-all-done.1 = f32[32,4,256]{2,1,0:T(4,128)S(1)} async-done(((f32[32,4,256]{2,1,0:T(4,128)}), f32[32,4,256]{2,1,0:T(4,128)S(1)}, u32[]{:S(2)}, u32[]{:S(2)}) %all-to-all-start.1) | async-done | bytes 131104 | tf_op jit(solution)/shard_map/all_to_all | solution.py:438
  44.9 19.6 %collective-permute-done.2.three_hbm = bf16[128,4096]{1,0:T(8,128)(2,1)S(1)} collective-permute-done((bf16[128,4096]{1,0:T(8,128)(2,1)}, bf16[128,4096]{1,0:T(8,128)(2,1)S(1)}, u32[]{:S(2)}, u32[]{:S(2)}) %collective-permute-start.2) | collective-permute-done | bytes 1048608 | tf_op jit(solution)/shard_map/ppermute | solution.py:428
  64.9 5.2 %shard_map.68 = (f32[16,48,128]{2,1,0:T(8,128)S(1)}, f32[16,48,128]{2,1,0:T(8,128)S(1)}) custom-call(s32[2]{0:T(128)S(1)} %pad_add_fusion.3.at_ref, bf16[128,4096]{1,0:T(8,128)(2,1)S(1)} %constant_dynamic-slice_fusion.1.own_hbm, bf16[128,4096]{1,0:T(8,128)(2,1)} %collective-permute-done.one_hbm, bf16[128,4096]{1,0:T(8,128)(2,1)S(1)} %collective-permute-done.1.two_hbm, ...), custom_call_target="tpu_custom_call" | custom-call | tf_op jit(solution)/shard_map/pallas_call | solution.py:443
  70.9 1.3 collective-permute-done.3
  72.3 15.4 %all_to_all.79 = f32[16,48,128]{2,1,0:T(8,128)} all-to-all(f32[16,48,128]{2,1,0:T(8,128)S(1)} %add.136), channel_id=1, replica_groups=mesh['brick_0'=4,'brick_1'=8,'brick_2'=2,'grp'=4] {'brick_0','grp'}, dimensions={0} | all-to-all | bytes 786432 | tf_op jit(solution)/shard_map/all_to_all | solution.py:463
  88.8 16.8 %all_to_all.80 = f32[8,48,128]{2,1,0:T(8,128)} all-to-all(f32[8,48,128]{2,1,0:T(8,128)S(1)} %broadcast_in_dim.64), channel_id=1, replica_groups=mesh['brick_0'=4,'brick_1'=8,'brick_2'=2,'grp'=4] {'brick_1'}, dimensions={0} | all-to-all | bytes 393216 | tf_op jit(solution)/shard_map/all_to_all | solution.py:46
  106.5 11.1 %all_to_all.81.mine_ref = f32[16,48,128]{2,1,0:T(8,128)S(1)} all-to-all(f32[16,48,128]{2,1,0:T(8,128)S(1)} %broadcast_in_dim.65), channel_id=1, replica_groups=mesh['brick_0'=4,'brick_1'=8,'brick_2'=2,'grp'=4] {'brick_0','grp'}, dimensions={0} | all-to-all | bytes 786432 | tf_op jit(solution)/shard_map/all_to_all | solution.py:46
  117.7 4.1 %collective-permute-start.4 = (f32[16,48,128]{2,1,0:T(8,128)S(1)}, f32[16,48,128]{2,1,0:T(8,128)S(1)}, u32[]{:S(2)}, u32[]{:S(2)}) collective-permute-start(f32[16,48,128]{2,1,0:T(8,128)S(1)} %all_to_all.81.mine_ref), channel_id=1, source_target_pairs={{0,4},{4,0},{1,5},{5,1},{2,6},{6,2},{3,7},{7,3},{8,12},{12,8},{9,1... | collective-permute-start | bytes 1179656 | tf_op jit(solution)/shard_map/ppermute | solution.py:466
  121.8 1.3 collective-permute-done.4.other_ref
  123.2 10.6 %shard_map.69 = (f32[512,512]{1,0:T(8,128)S(1)}, f32[4,128]{1,0:T(4,128)S(1)}, f32[4,128]{1,0:T(4,128)S(1)}, f32[4,128]{1,0:T(4,128)S(1)}) custom-call(s32[2]{0:T(128)S(1)} %pad_add_fusion.3.at_ref, bf16[128,4096]{1,0:T(8,128)(2,1)S(1)} %constant_dynamic-slice_fusion.1.own_hbm, bf16[128,4096]{1,0:T(8,128)(2,1)} %collective-permute-done.one_hbm, ...), custom_call_target="tpu_custom_call" | custom-call | tf_op jit(solution)/shard_map/pallas_call | solution.py:471
  133.8 7.6 %all_to_all.82 = f32[8,4,128]{2,1,0:T(4,128)S(1)} all-to-all(f32[8,4,128]{2,1,0:T(4,128)S(1)} %broadcast_in_dim.66), channel_id=1, replica_groups=mesh['brick_0'=4,'brick_1'=8,'brick_2'=2,'grp'=4] {'brick_2','grp'}, dimensions={0} | all-to-all | bytes 32768 | tf_op jit(solution)/shard_map/all_to_all | solution.py:46
  141.4 11.8 %all_to_all.83.gathered_ref = f32[32,4,128]{2,1,0:T(4,128)S(1)} all-to-all(f32[32,4,128]{2,1,0:T(4,128)S(1)} %broadcast_in_dim.67), channel_id=1, replica_groups=mesh['brick_0'=4,'brick_1'=8,'brick_2'=2,'grp'=4] {'brick_0','brick_1'}, dimensions={0} | all-to-all | bytes 131072 | tf_op jit(solution)/shard_map/all_to_all | solution.py:46
  153.3 3.7 %shard_map.70 = (f32[4,128]{1,0:T(4,128)S(1)}, f32[4,128]{1,0:T(4,128)S(1)}) custom-call(s32[2]{0:T(128)S(1)} %pad_add_fusion.3.at_ref, bf16[128,4096]{1,0:T(8,128)(2,1)S(1)} %constant_dynamic-slice_fusion.1.own_hbm, bf16[128,4096]{1,0:T(8,128)(2,1)} %collective-permute-done.one_hbm, bf16[128,4096]{1,0:T(8,128)(2,1)} %copy-done, ...), custom_call_target="tpu_custom_call" | custom-call | tf_op jit(solution)/shard_map/pallas_call | solution.py:485
  157.0 8.8 %all_to_all.84 = f32[8,4,128]{2,1,0:T(4,128)S(1)} all-to-all(f32[8,4,128]{2,1,0:T(4,128)S(1)} %broadcast_in_dim.68), channel_id=1, replica_groups=mesh['brick_0'=4,'brick_1'=8,'brick_2'=2,'grp'=4] {'brick_2','grp'}, dimensions={0} | all-to-all | bytes 32768 | tf_op jit(solution)/shard_map/all_to_all | solution.py:46
  165.8 11.9 %all_to_all.85.gathered_ref = f32[32,4,128]{2,1,0:T(4,128)S(1)} all-to-all(f32[32,4,128]{2,1,0:T(4,128)S(1)} %broadcast_in_dim.69), channel_id=1, replica_groups=mesh['brick_0'=4,'brick_1'=8,'brick_2'=2,'grp'=4] {'brick_0','brick_1'}, dimensions={0} | all-to-all | bytes 131072 | tf_op jit(solution)/shard_map/all_to_all | solution.py:46
  177.7 3.7 %shard_map.71 = (f32[4,128]{1,0:T(4,128)S(1)}, f32[4,128]{1,0:T(4,128)S(1)}) custom-call(s32[2]{0:T(128)S(1)} %pad_add_fusion.3.at_ref, bf16[128,4096]{1,0:T(8,128)(2,1)S(1)} %constant_dynamic-slice_fusion.1.own_hbm, bf16[128,4096]{1,0:T(8,128)(2,1)} %collective-permute-done.one_hbm, bf16[128,4096]{1,0:T(8,128)(2,1)} %copy-done, ...), custom_call_target="tpu_custom_call" | custom-call | tf_op jit(solution)/shard_map/pallas_call | solution.py:485
  181.4 8.9 %all_to_all.86 = f32[8,4,128]{2,1,0:T(4,128)S(1)} all-to-all(f32[8,4,128]{2,1,0:T(4,128)S(1)} %broadcast_in_dim.70), channel_id=1, replica_groups=mesh['brick_0'=4,'brick_1'=8,'brick_2'=2,'grp'=4] {'brick_2','grp'}, dimensions={0} | all-to-all | bytes 32768 | tf_op jit(solution)/shard_map/all_to_all | solution.py:46
  190.4 11.9 %all_to_all.87.gathered_ref = f32[32,4,128]{2,1,0:T(4,128)S(1)} all-to-all(f32[32,4,128]{2,1,0:T(4,128)S(1)} %broadcast_in_dim.122), channel_id=1, replica_groups=mesh['brick_0'=4,'brick_1'=8,'brick_2'=2,'grp'=4] {'brick_0','brick_1'}, dimensions={0} | all-to-all | bytes 131072 | tf_op jit(solution)/shard_map/all_to_all | solution.py:46
  202.3 3.5 %shard_map.72 = (f32[4,128]{1,0:T(4,128)}, f32[8,32,128]{2,1,0:T(8,128)}) custom-call(s32[2]{0:T(128)S(1)} %pad_add_fusion.3.at_ref, bf16[128,4096]{1,0:T(8,128)(2,1)S(1)} %constant_dynamic-slice_fusion.1.own_hbm, bf16[128,4096]{1,0:T(8,128)(2,1)} %collective-permute-done.one_hbm, bf16[128,4096]{1,0:T(8,128)(2,1)} %copy-done, bf16[128,4096]{1,0:T(8,128)(2,1)} %copy-done.1, ...), custom_call_target="tpu_custom_call" | custom-call | tf_op jit(solution)/shard_map/pallas_call | solution.py:488
  205.8 5.0 %all-to-all-start.11 = ((f32[8,32,128]{2,1,0:T(8,128)}), f32[8,32,128]{2,1,0:T(8,128)S(1)}, u32[]{:S(2)}, u32[]{:S(2)}) async-start(f32[8,32,128]{2,1,0:T(8,128)} %get-tuple-element.44), calls=%async_computation.11 | async-start | bytes 262144 | tf_op jit(solution)/shard_map/all_to_all | solution.py:492
  210.8 5.2 %all-to-all-done.11 = f32[8,32,128]{2,1,0:T(8,128)S(1)} async-done(((f32[8,32,128]{2,1,0:T(8,128)}), f32[8,32,128]{2,1,0:T(8,128)S(1)}, u32[]{:S(2)}, u32[]{:S(2)}) %all-to-all-start.11) | async-done | bytes 131104 | tf_op jit(solution)/shard_map/all_to_all | solution.py:492
  216.0 1.2 gather_fusion.2
  217.2 3.9 %all-to-all-start.12 = ((f32[32,4,128]{2,1,0:T(4,128)}), f32[32,4,128]{2,1,0:T(4,128)S(1)}, u32[]{:S(2)}, u32[]{:S(2)}) async-start(f32[32,4,128]{2,1,0:T(4,128)} %bitcast.17), calls=%async_computation.12 | async-start | bytes 131072 | tf_op jit(solution)/shard_map/all_to_all | solution.py:493
  221.1 8.8 %all-to-all-done.12 = f32[32,4,128]{2,1,0:T(4,128)S(1)} async-done(((f32[32,4,128]{2,1,0:T(4,128)}), f32[32,4,128]{2,1,0:T(4,128)S(1)}, u32[]{:S(2)}, u32[]{:S(2)}) %all-to-all-start.12) | async-done | bytes 65568 | tf_op jit(solution)/shard_map/all_to_all | solution.py:493
  229.9 1.2 gather_fusion.3
  (64 shorter events, 10.4 us)
Async XLA Ops:
  0.6 19.3 %copy-start.3 = (s32[8192]{0:T(1024)S(1)}, s32[8192]{0:T(1024)}, u32[]{:S(2)}) copy-start(s32[8192]{0:T(1024)} %param.6) | copy-start | bytes 98308
  2.1 21.0 %all-to-all-start = ((f32[8,32,256]{2,1,0:T(8,128)}), f32[8,32,256]{2,1,0:T(8,128)S(1)}, u32[]{:S(2)}, u32[]{:S(2)}) async-start(f32[8,32,256]{2,1,0:T(8,128)} %broadcast_in_dim.58), calls=%async_computation | async-start | bytes 524288 | tf_op jit(solution)/shard_map/all_to_all | solution.py:432
  15.6 29.3 %collective-permute-start.1 = (bf16[128,4096]{1,0:T(8,128)(2,1)}, bf16[128,4096]{1,0:T(8,128)(2,1)S(1)}, u32[]{:S(2)}, u32[]{:S(2)}) collective-permute-start(bf16[128,4096]{1,0:T(8,128)(2,1)} %constant_dynamic-slice_fusion.2), channel_id=1, source_target_pairs={{0,2},{1,3},{2,0},{3,1},{4,6},{5,7},{6,4},{7,5},{8,10},{9,11},{10,... | collective-permute-start | bytes 3145736 | tf_op jit(solution)/shard_map/ppermute | solution.py:428
  18.4 46.0 %collective-permute-start.2 = (bf16[128,4096]{1,0:T(8,128)(2,1)}, bf16[128,4096]{1,0:T(8,128)(2,1)S(1)}, u32[]{:S(2)}, u32[]{:S(2)}) collective-permute-start(bf16[128,4096]{1,0:T(8,128)(2,1)} %constant_dynamic-slice_fusion.3), channel_id=1, source_target_pairs={{0,3},{1,0},{2,1},{3,2},{4,7},{5,4},{6,5},{7,6},{8,11},{9,8},{10,9... | collective-permute-start | bytes 3145736 | tf_op jit(solution)/shard_map/ppermute | solution.py:428
  19.3 45.6 %collective-permute-start = (bf16[128,4096]{1,0:T(8,128)(2,1)}, bf16[128,4096]{1,0:T(8,128)(2,1)}, u32[]{:S(2)}, u32[]{:S(2)}) collective-permute-start(bf16[128,4096]{1,0:T(8,128)(2,1)} %constant_dynamic-slice_fusion.4), channel_id=1, source_target_pairs={{0,1},{1,2},{2,3},{3,0},{4,5},{5,6},{6,7},{7,4},{8,9},{9,10},{10,1... | collective-permute-start | bytes 3145736 | tf_op jit(solution)/shard_map/ppermute | solution.py:428
  24.5 19.6 %all-to-all-start.1 = ((f32[32,4,256]{2,1,0:T(4,128)}), f32[32,4,256]{2,1,0:T(4,128)S(1)}, u32[]{:S(2)}, u32[]{:S(2)}) async-start(f32[32,4,256]{2,1,0:T(4,128)} %all_to_all.50), calls=%async_computation.1 | async-start | bytes 262144 | tf_op jit(solution)/shard_map/all_to_all | solution.py:438
  44.8 78.4 %copy-start.2 = (f32[512]{0:T(512)S(1)}, f32[512]{0:T(512)}, u32[]{:S(2)}) copy-start(f32[512]{0:T(512)} %param.9) | copy-start | bytes 6148
  44.8 72.8 %copy-start = (bf16[128,4096]{1,0:T(8,128)(2,1)}, bf16[128,4096]{1,0:T(8,128)(2,1)S(1)}, u32[]{:S(2)}) copy-start(bf16[128,4096]{1,0:T(8,128)(2,1)S(1)} %collective-permute-done.1.two_hbm) | copy-start | bytes 3145732
  64.5 53.2 %copy-start.1 = (bf16[128,4096]{1,0:T(8,128)(2,1)}, bf16[128,4096]{1,0:T(8,128)(2,1)S(1)}, u32[]{:S(2)}) copy-start(bf16[128,4096]{1,0:T(8,128)(2,1)S(1)} %collective-permute-done.2.three_hbm) | copy-start | bytes 3145732
  70.2 2.1 collective-permute-start.3
  117.7 5.5 %collective-permute-start.4 = (f32[16,48,128]{2,1,0:T(8,128)S(1)}, f32[16,48,128]{2,1,0:T(8,128)S(1)}, u32[]{:S(2)}, u32[]{:S(2)}) collective-permute-start(f32[16,48,128]{2,1,0:T(8,128)S(1)} %all_to_all.81.mine_ref), channel_id=1, source_target_pairs={{0,4},{4,0},{1,5},{5,1},{2,6},{6,2},{3,7},{7,3},{8,12},{12,8},{9,1... | collective-permute-start | bytes 1179656 | tf_op jit(solution)/shard_map/ppermute | solution.py:466
  205.8 10.2 %all-to-all-start.11 = ((f32[8,32,128]{2,1,0:T(8,128)}), f32[8,32,128]{2,1,0:T(8,128)S(1)}, u32[]{:S(2)}, u32[]{:S(2)}) async-start(f32[8,32,128]{2,1,0:T(8,128)} %get-tuple-element.44), calls=%async_computation.11 | async-start | bytes 262144 | tf_op jit(solution)/shard_map/all_to_all | solution.py:492
  217.2 12.7 %all-to-all-start.12 = ((f32[32,4,128]{2,1,0:T(4,128)}), f32[32,4,128]{2,1,0:T(4,128)S(1)}, u32[]{:S(2)}, u32[]{:S(2)}) async-start(f32[32,4,128]{2,1,0:T(4,128)} %bitcast.17), calls=%async_computation.12 | async-start | bytes 131072 | tf_op jit(solution)/shard_map/all_to_all | solution.py:493

commit v6 on v5

--- a/solution.py
+++ b/solution.py
@@ -418,18 +418,18 @@
     per_brick = gradients.shape[1] // 128
     at = jnp.stack([quarter, core]).astype(jnp.int32)
 
-    near = size_of(NEAR)
-    pieces, last = [None] * NB, gradients
-    for k in (1, 3, 2, 0):
-        to = lax.rem(quarter + k, NB) * COLS
-        piece = lax.dynamic_slice(last, (0, to), (ROWS, COLS))
-        piece, last = lax.optimization_barrier((piece, last))
-        if k:
-            piece = lax.ppermute(piece, "grp", [(i, (i + k) % NB) for i in range(NB)])
-        pieces[k] = piece
     both = jnp.concatenate([weights.reshape(1, BLKS, 128), linear.reshape(1, BLKS, 128)], axis=2)
-    both = jnp.broadcast_to(both, (near, BLKS, 256))
+    both = jnp.broadcast_to(both, (size_of(NEAR), BLKS, 256))
     both = lax.all_to_all(both, NEAR, 0, 0, tiled=True)
+
+    pieces = [
+        lax.dynamic_slice(gradients, (0, lax.rem(quarter + k, NB) * COLS), (ROWS, COLS))
+        for k in range(NB)
+    ]
+    pieces = list(lax.optimization_barrier(tuple(pieces)))
+    for k in (1, 3, 2):
+        ring = [(i, (i + k) % NB) for i in range(NB)]
+        pieces[k] = lax.ppermute(pieces[k], "grp", ring)
 
     incoming, leaving, back, place = layout_tables(perm, here, per_brick)
     incoming = lax.dynamic_slice_in_dim(incoming, quarter * BLKS, BLKS)
@@ -454,9 +454,7 @@
         24,
     )(at, *pieces, curv, lin)
 
-    pieces = pieces[:2] + [
-        pltpu.with_memory_space_constraint(piece, pltpu.HBM) for piece in pieces[2:]
-    ]
+    pieces = [pltpu.with_memory_space_constraint(piece, pltpu.HBM) for piece in pieces]
 
     swap = [(0, 1), (1, 0)]
     mine = mine + lax.ppermute(other, "brick_2", swap)

time: 232 us -> 229 us (0.987)
  local copies, waits for them, and re-layouts: 14.2 us -> 9.93 us
    dynamic_slice x4 -> x1, local copies, waits for them, and re-layouts: 8.25 us -> 3.94 us  [on_device(): lax.dynamic_slice(gradients, (0, lax.rem(quarter + k, NB) * COLS), (ROWS,...]
  transfers between devices with their start and end apart: 9 -> 9, of which waited for: 7 -> 6; matrix products, arithmetic and copies ran while one was open for 5% -> 3% of each run, Pallas kernels for 0% -> 0%
where the time goes in v6:
time: 229 us; the launch traced here: 228 us
  blocking collectives  104 us (45%)
  waiting for transfers between devices  46.4 us (20%)
  starting transfers between devices  36.2 us (16%)
  Pallas kernels  27.2 us (12%)
  local copies, waits for them, and re-layouts  9.93 us (4%)
  other arithmetic  3.25 us (1%)
    all_to_all x8, blocking collectives, from_everyone(): lax.all_to_all(jnp.broadcast_to(array[None], (devices, *array.shape)), ax...  88.8 us
    ppermute x3, waiting for transfers between devices, on_device(): pieces[k] = lax.ppermute(pieces[k], 'grp', ring)  20.8 us
    all_to_all x1, blocking collectives, on_device(): shard = lax.all_to_all(mine, PLANE, 0, 0, tiled=True).sum(axis=0)  15.2 us
    pallas_call x1, Pallas kernels, on_device(): call(solve_kernel, [SM] + [HBM] * NB + [VM] * 5, [square, vector, vector,...  10.5 us
    all_to_all x1, starting transfers between devices, on_device(): both = lax.all_to_all(both, FAR, 0, 0, tiled=True)  10.4 us
    all_to_all x1, waiting for transfers between devices, on_device(): both = lax.all_to_all(both, FAR, 0, 0, tiled=True)  8.94 us
    all_to_all x1, waiting for transfers between devices, on_device(): arrived = lax.all_to_all(whole[back], FAR, 0, 0, tiled=True)  8.85 us
    pallas_call x2, Pallas kernels, on_device(): call(step_kernel, ins, [vector, vector], FULL, 20)  7.67 us
  transfers between devices with their start and end apart: 9, of which 6 were waited for; matrix products, arithmetic and copies ran while one was open for 3% of the time, Pallas kernels for 0%

profile of v6, /device:TPU:1, one launch (start us, length us, event | category | flops | bytes accessed | tf_op | source)
XLA Modules:
  0.0 227.8 jit_solution(7900025071585534814)
XLA Ops:
  2.1 6.5 %all-to-all-start = ((f32[8,32,256]{2,1,0:T(8,128)}), f32[8,32,256]{2,1,0:T(8,128)S(1)}, u32[]{:S(2)}, u32[]{:S(2)}) async-start(f32[8,32,256]{2,1,0:T(8,128)} %broadcast_in_dim.58), calls=%async_computation | async-start | bytes 524288 | tf_op jit(solution)/shard_map/all_to_all | solution.py:423
  8.6 3.9 %constant_dynamic-slice_fusion.1 = (bf16[128,4096]{1,0:T(8,128)(2,1)}, bf16[128,4096]{1,0:T(8,128)(2,1)}, bf16[128,4096]{1,0:T(8,128)(2,1)S(1)}, bf16[128,4096]{1,0:T(8,128)(2,1)}) fusion(bf16[128,16384]{1,0:T(8,128)(2,1)} %param.5, s32[]{:T(128)S(6)} %select_n.125, s32[]{:T(128)S(6)} %select_n.123, s32[]{:T(128)S(6)} %select_n.122, s32[]{:T(128)S(6)} %select_n.124), kind=kLoop, calls=%fused_computation.55 | loop fusion | bytes 8388624 | tf_op jit(solution)/shard_map/dynamic_slice | solution.py:426
  12.6 1.4 collective-permute-start
  13.9 2.4 %collective-permute-start.1 = (bf16[128,4096]{1,0:T(8,128)(2,1)}, bf16[128,4096]{1,0:T(8,128)(2,1)S(1)}, u32[]{:S(2)}, u32[]{:S(2)}) collective-permute-start(bf16[128,4096]{1,0:T(8,128)(2,1)} %get-tuple-element.24), channel_id=1, source_target_pairs={{0,2},{1,3},{2,0},{3,1},{4,6},{5,7},{6,4},{7,5},{8,10},{9,11},{10,... | collective-permute-start | bytes 3145736 | tf_op jit(solution)/shard_map/ppermute | solution.py:432
  16.3 1.2 collective-permute-start.2
  20.8 10.4 %all-to-all-start.1 = ((f32[32,4,256]{2,1,0:T(4,128)}), f32[32,4,256]{2,1,0:T(4,128)S(1)}, u32[]{:S(2)}, u32[]{:S(2)}) async-start(f32[32,4,256]{2,1,0:T(4,128)} %all_to_all.50), calls=%async_computation.1 | async-start | bytes 262144 | tf_op jit(solution)/shard_map/all_to_all | solution.py:438
  31.5 8.9 %all-to-all-done.1 = f32[32,4,256]{2,1,0:T(4,128)S(1)} async-done(((f32[32,4,256]{2,1,0:T(4,128)}), f32[32,4,256]{2,1,0:T(4,128)S(1)}, u32[]{:S(2)}, u32[]{:S(2)}) %all-to-all-start.1) | async-done | bytes 131104 | tf_op jit(solution)/shard_map/all_to_all | solution.py:438
  41.2 20.8 %collective-permute-done.1.two_hbm = bf16[128,4096]{1,0:T(8,128)(2,1)S(1)} collective-permute-done((bf16[128,4096]{1,0:T(8,128)(2,1)}, bf16[128,4096]{1,0:T(8,128)(2,1)S(1)}, u32[]{:S(2)}, u32[]{:S(2)}) %collective-permute-start.1) | collective-permute-done | bytes 1048608 | tf_op jit(solution)/shard_map/ppermute | solution.py:432
  61.9 5.3 %shard_map.68 = (f32[16,48,128]{2,1,0:T(8,128)S(1)}, f32[16,48,128]{2,1,0:T(8,128)S(1)}) custom-call(s32[2]{0:T(128)S(1)} %pad_add_fusion.3.at_ref, bf16[128,4096]{1,0:T(8,128)(2,1)S(1)} %get-tuple-element.22.own_hbm, bf16[128,4096]{1,0:T(8,128)(2,1)S(1)} %collective-permute-done.one_hbm, bf16[128,4096]{1,0:T(8,128)(2,1)S(1)} %collective-permute-done.1.two_hbm, ...), custom_call_target="tpu_custom_call" | custom-call | tf_op jit(solution)/shard_map/pallas_call | solution.py:443
  67.2 1.3 collective-permute-start.3
  68.5 1.3 collective-permute-done.3
  69.9 15.2 %all_to_all.79 = f32[16,48,128]{2,1,0:T(8,128)} all-to-all(f32[16,48,128]{2,1,0:T(8,128)S(1)} %add.136), channel_id=1, replica_groups=mesh['brick_0'=4,'brick_1'=8,'brick_2'=2,'grp'=4] {'brick_0','grp'}, dimensions={0} | all-to-all | bytes 786432 | tf_op jit(solution)/shard_map/all_to_all | solution.py:461
  86.1 16.7 %all_to_all.80 = f32[8,48,128]{2,1,0:T(8,128)S(1)} all-to-all(f32[8,48,128]{2,1,0:T(8,128)S(1)} %broadcast_in_dim.64), channel_id=1, replica_groups=mesh['brick_0'=4,'brick_1'=8,'brick_2'=2,'grp'=4] {'brick_1'}, dimensions={0} | all-to-all | bytes 393216 | tf_op jit(solution)/shard_map/all_to_all | solution.py:46
  102.9 11.1 %all_to_all.81.mine_ref = f32[16,48,128]{2,1,0:T(8,128)S(1)} all-to-all(f32[16,48,128]{2,1,0:T(8,128)S(1)} %broadcast_in_dim.65), channel_id=1, replica_groups=mesh['brick_0'=4,'brick_1'=8,'brick_2'=2,'grp'=4] {'brick_0','grp'}, dimensions={0} | all-to-all | bytes 786432 | tf_op jit(solution)/shard_map/all_to_all | solution.py:46
  114.0 4.1 %collective-permute-start.4 = (f32[16,48,128]{2,1,0:T(8,128)S(1)}, f32[16,48,128]{2,1,0:T(8,128)S(1)}, u32[]{:S(2)}, u32[]{:S(2)}) collective-permute-start(f32[16,48,128]{2,1,0:T(8,128)S(1)} %all_to_all.81.mine_ref), channel_id=1, source_target_pairs={{0,4},{4,0},{1,5},{5,1},{2,6},{6,2},{3,7},{7,3},{8,12},{12,8},{9,1... | collective-permute-start | bytes 1179656 | tf_op jit(solution)/shard_map/ppermute | solution.py:464
  118.2 1.3 collective-permute-done.4.other_ref
  119.5 10.5 %shard_map.69 = (f32[512,512]{1,0:T(8,128)S(1)}, f32[4,128]{1,0:T(4,128)S(1)}, f32[4,128]{1,0:T(4,128)S(1)}, f32[4,128]{1,0:T(4,128)S(1)}) custom-call(s32[2]{0:T(128)S(1)} %pad_add_fusion.3.at_ref, bf16[128,4096]{1,0:T(8,128)(2,1)} %copy-done, bf16[128,4096]{1,0:T(8,128)(2,1)} %copy-done.1, bf16[128,4096]{1,0:T(8,128)(2,1)} %copy-done.2, ...), custom_call_target="tpu_custom_call" | custom-call | tf_op jit(solution)/shard_map/pallas_call | solution.py:469
  130.0 7.6 %all_to_all.82 = f32[8,4,128]{2,1,0:T(4,128)S(1)} all-to-all(f32[8,4,128]{2,1,0:T(4,128)S(1)} %broadcast_in_dim.66), channel_id=1, replica_groups=mesh['brick_0'=4,'brick_1'=8,'brick_2'=2,'grp'=4] {'brick_2','grp'}, dimensions={0} | all-to-all | bytes 32768 | tf_op jit(solution)/shard_map/all_to_all | solution.py:46
  137.7 11.8 %all_to_all.83.gathered_ref = f32[32,4,128]{2,1,0:T(4,128)S(1)} all-to-all(f32[32,4,128]{2,1,0:T(4,128)S(1)} %broadcast_in_dim.67), channel_id=1, replica_groups=mesh['brick_0'=4,'brick_1'=8,'brick_2'=2,'grp'=4] {'brick_0','brick_1'}, dimensions={0} | all-to-all | bytes 131072 | tf_op jit(solution)/shard_map/all_to_all | solution.py:46
  149.5 3.8 %shard_map.70 = (f32[4,128]{1,0:T(4,128)S(1)}, f32[4,128]{1,0:T(4,128)S(1)}) custom-call(s32[2]{0:T(128)S(1)} %pad_add_fusion.3.at_ref, bf16[128,4096]{1,0:T(8,128)(2,1)} %copy-done, bf16[128,4096]{1,0:T(8,128)(2,1)} %copy-done.1, bf16[128,4096]{1,0:T(8,128)(2,1)} %copy-done.2, bf16[128,4096]{1,0:T(8,128)(2,1)} %collective-permute-done.2.three_hbm, ...), custom_call_target="tpu_custom_call" | custom-call | tf_op jit(solution)/shard_map/pallas_call | solution.py:483
  153.4 8.8 %all_to_all.84 = f32[8,4,128]{2,1,0:T(4,128)S(1)} all-to-all(f32[8,4,128]{2,1,0:T(4,128)S(1)} %broadcast_in_dim.68), channel_id=1, replica_groups=mesh['brick_0'=4,'brick_1'=8,'brick_2'=2,'grp'=4] {'brick_2','grp'}, dimensions={0} | all-to-all | bytes 32768 | tf_op jit(solution)/shard_map/all_to_all | solution.py:46
  162.2 11.9 %all_to_all.85.gathered_ref = f32[32,4,128]{2,1,0:T(4,128)S(1)} all-to-all(f32[32,4,128]{2,1,0:T(4,128)S(1)} %broadcast_in_dim.69), channel_id=1, replica_groups=mesh['brick_0'=4,'brick_1'=8,'brick_2'=2,'grp'=4] {'brick_0','brick_1'}, dimensions={0} | all-to-all | bytes 131072 | tf_op jit(solution)/shard_map/all_to_all | solution.py:46
  174.1 3.8 %shard_map.71 = (f32[4,128]{1,0:T(4,128)S(1)}, f32[4,128]{1,0:T(4,128)S(1)}) custom-call(s32[2]{0:T(128)S(1)} %pad_add_fusion.3.at_ref, bf16[128,4096]{1,0:T(8,128)(2,1)} %copy-done, bf16[128,4096]{1,0:T(8,128)(2,1)} %copy-done.1, bf16[128,4096]{1,0:T(8,128)(2,1)} %copy-done.2, bf16[128,4096]{1,0:T(8,128)(2,1)} %collective-permute-done.2.three_hbm, ...), custom_call_target="tpu_custom_call" | custom-call | tf_op jit(solution)/shard_map/pallas_call | solution.py:483
  178.0 8.9 %all_to_all.86 = f32[8,4,128]{2,1,0:T(4,128)S(1)} all-to-all(f32[8,4,128]{2,1,0:T(4,128)S(1)} %broadcast_in_dim.70), channel_id=1, replica_groups=mesh['brick_0'=4,'brick_1'=8,'brick_2'=2,'grp'=4] {'brick_2','grp'}, dimensions={0} | all-to-all | bytes 32768 | tf_op jit(solution)/shard_map/all_to_all | solution.py:46
  186.9 11.9 %all_to_all.87.gathered_ref = f32[32,4,128]{2,1,0:T(4,128)S(1)} all-to-all(f32[32,4,128]{2,1,0:T(4,128)S(1)} %broadcast_in_dim.122), channel_id=1, replica_groups=mesh['brick_0'=4,'brick_1'=8,'brick_2'=2,'grp'=4] {'brick_0','brick_1'}, dimensions={0} | all-to-all | bytes 131072 | tf_op jit(solution)/shard_map/all_to_all | solution.py:46
  198.8 3.8 %shard_map.72 = (f32[4,128]{1,0:T(4,128)}, f32[8,32,128]{2,1,0:T(8,128)}) custom-call(s32[2]{0:T(128)S(1)} %pad_add_fusion.3.at_ref, bf16[128,4096]{1,0:T(8,128)(2,1)} %copy-done, bf16[128,4096]{1,0:T(8,128)(2,1)} %copy-done.1, bf16[128,4096]{1,0:T(8,128)(2,1)} %copy-done.2, bf16[128,4096]{1,0:T(8,128)(2,1)} %collective-permute-done.2.three_hbm, ...), custom_call_target="tpu_custom_call" | custom-call | tf_op jit(solution)/shard_map/pallas_call | solution.py:486
  202.6 5.0 %all-to-all-start.11 = ((f32[8,32,128]{2,1,0:T(8,128)}), f32[8,32,128]{2,1,0:T(8,128)S(1)}, u32[]{:S(2)}, u32[]{:S(2)}) async-start(f32[8,32,128]{2,1,0:T(8,128)} %get-tuple-element.38), calls=%async_computation.11 | async-start | bytes 262144 | tf_op jit(solution)/shard_map/all_to_all | solution.py:490
  207.5 5.2 %all-to-all-done.11 = f32[8,32,128]{2,1,0:T(8,128)S(1)} async-done(((f32[8,32,128]{2,1,0:T(8,128)}), f32[8,32,128]{2,1,0:T(8,128)S(1)}, u32[]{:S(2)}, u32[]{:S(2)}) %all-to-all-start.11) | async-done | bytes 131104 | tf_op jit(solution)/shard_map/all_to_all | solution.py:490
  212.7 1.2 gather_fusion.2
  213.9 3.9 %all-to-all-start.12 = ((f32[32,4,128]{2,1,0:T(4,128)}), f32[32,4,128]{2,1,0:T(4,128)S(1)}, u32[]{:S(2)}, u32[]{:S(2)}) async-start(f32[32,4,128]{2,1,0:T(4,128)} %bitcast.17), calls=%async_computation.12 | async-start | bytes 131072 | tf_op jit(solution)/shard_map/all_to_all | solution.py:491
  217.8 8.8 %all-to-all-done.12 = f32[32,4,128]{2,1,0:T(4,128)S(1)} async-done(((f32[32,4,128]{2,1,0:T(4,128)}), f32[32,4,128]{2,1,0:T(4,128)S(1)}, u32[]{:S(2)}, u32[]{:S(2)}) %all-to-all-start.12) | async-done | bytes 65568 | tf_op jit(solution)/shard_map/all_to_all | solution.py:491
  226.7 1.2 gather_fusion.3
  (63 shorter events, 6.9 us)
Async XLA Ops:
  2.1 17.3 %all-to-all-start = ((f32[8,32,256]{2,1,0:T(8,128)}), f32[8,32,256]{2,1,0:T(8,128)S(1)}, u32[]{:S(2)}, u32[]{:S(2)}) async-start(f32[8,32,256]{2,1,0:T(8,128)} %broadcast_in_dim.58), calls=%async_computation | async-start | bytes 524288 | tf_op jit(solution)/shard_map/all_to_all | solution.py:423
  8.6 8.9 %copy-start.4 = (s32[8192]{0:T(1024)S(1)}, s32[8192]{0:T(1024)}, u32[]{:S(2)}) copy-start(s32[8192]{0:T(1024)} %param.6) | copy-start | bytes 98308
  12.6 72.5 %copy-start = (bf16[128,4096]{1,0:T(8,128)(2,1)}, bf16[128,4096]{1,0:T(8,128)(2,1)S(1)}, u32[]{:S(2)}) copy-start(bf16[128,4096]{1,0:T(8,128)(2,1)S(1)} %get-tuple-element.22.own_hbm) | copy-start | bytes 3145732
  12.6 28.6 %collective-permute-start = (bf16[128,4096]{1,0:T(8,128)(2,1)}, bf16[128,4096]{1,0:T(8,128)(2,1)S(1)}, u32[]{:S(2)}, u32[]{:S(2)}) collective-permute-start(bf16[128,4096]{1,0:T(8,128)(2,1)} %get-tuple-element.23), channel_id=1, source_target_pairs={{0,1},{1,2},{2,3},{3,0},{4,5},{5,6},{6,7},{7,4},{8,9},{9,10},{10,1... | collective-permute-start | bytes 3145736 | tf_op jit(solution)/shard_map/ppermute | solution.py:432
  13.9 48.0 %collective-permute-start.1 = (bf16[128,4096]{1,0:T(8,128)(2,1)}, bf16[128,4096]{1,0:T(8,128)(2,1)S(1)}, u32[]{:S(2)}, u32[]{:S(2)}) collective-permute-start(bf16[128,4096]{1,0:T(8,128)(2,1)} %get-tuple-element.24), channel_id=1, source_target_pairs={{0,2},{1,3},{2,0},{3,1},{4,6},{5,7},{6,4},{7,5},{8,10},{9,11},{10,... | collective-permute-start | bytes 3145736 | tf_op jit(solution)/shard_map/ppermute | solution.py:432
  16.3 45.6 %collective-permute-start.2 = (bf16[128,4096]{1,0:T(8,128)(2,1)}, bf16[128,4096]{1,0:T(8,128)(2,1)}, u32[]{:S(2)}, u32[]{:S(2)}) collective-permute-start(bf16[128,4096]{1,0:T(8,128)(2,1)} %get-tuple-element.25), channel_id=1, source_target_pairs={{0,3},{1,0},{2,1},{3,2},{4,7},{5,4},{6,5},{7,6},{8,11},{9,8},{10,9... | collective-permute-start | bytes 3145736 | tf_op jit(solution)/shard_map/ppermute | solution.py:432
  20.8 19.6 %all-to-all-start.1 = ((f32[32,4,256]{2,1,0:T(4,128)}), f32[32,4,256]{2,1,0:T(4,128)S(1)}, u32[]{:S(2)}, u32[]{:S(2)}) async-start(f32[32,4,256]{2,1,0:T(4,128)} %all_to_all.50), calls=%async_computation.1 | async-start | bytes 262144 | tf_op jit(solution)/shard_map/all_to_all | solution.py:438
  41.1 78.4 %copy-start.3 = (f32[512]{0:T(512)S(1)}, f32[512]{0:T(512)}, u32[]{:S(2)}) copy-start(f32[512]{0:T(512)} %param.9) | copy-start | bytes 6148
  41.1 72.9 %copy-start.1 = (bf16[128,4096]{1,0:T(8,128)(2,1)}, bf16[128,4096]{1,0:T(8,128)(2,1)S(1)}, u32[]{:S(2)}) copy-start(bf16[128,4096]{1,0:T(8,128)(2,1)S(1)} %collective-permute-done.one_hbm) | copy-start | bytes 3145732
  61.9 52.1 %copy-start.2 = (bf16[128,4096]{1,0:T(8,128)(2,1)}, bf16[128,4096]{1,0:T(8,128)(2,1)S(1)}, u32[]{:S(2)}) copy-start(bf16[128,4096]{1,0:T(8,128)(2,1)S(1)} %collective-permute-done.1.two_hbm) | copy-start | bytes 3145732
  67.2 2.7 %collective-permute-start.3 = (f32[16,48,128]{2,1,0:T(8,128)S(1)}, f32[16,48,128]{2,1,0:T(8,128)S(1)}, u32[]{:S(2)}, u32[]{:S(2)}) collective-permute-start(f32[16,48,128]{2,1,0:T(8,128)S(1)} %get-tuple-element.29), channel_id=1, source_target_pairs={{0,4},{4,0},{1,5},{5,1},{2,6},{6,2},{3,7},{7,3},{8,12},{12,8},{9,1... | collective-permute-start | bytes 1179656 | tf_op jit(solution)/shard_map/ppermute | solution.py:460
  114.0 5.5 %collective-permute-start.4 = (f32[16,48,128]{2,1,0:T(8,128)S(1)}, f32[16,48,128]{2,1,0:T(8,128)S(1)}, u32[]{:S(2)}, u32[]{:S(2)}) collective-permute-start(f32[16,48,128]{2,1,0:T(8,128)S(1)} %all_to_all.81.mine_ref), channel_id=1, source_target_pairs={{0,4},{4,0},{1,5},{5,1},{2,6},{6,2},{3,7},{7,3},{8,12},{12,8},{9,1... | collective-permute-start | bytes 1179656 | tf_op jit(solution)/shard_map/ppermute | solution.py:464
  202.6 10.2 %all-to-all-start.11 = ((f32[8,32,128]{2,1,0:T(8,128)}), f32[8,32,128]{2,1,0:T(8,128)S(1)}, u32[]{:S(2)}, u32[]{:S(2)}) async-start(f32[8,32,128]{2,1,0:T(8,128)} %get-tuple-element.38), calls=%async_computation.11 | async-start | bytes 262144 | tf_op jit(solution)/shard_map/all_to_all | solution.py:490
  213.9 12.7 %all-to-all-start.12 = ((f32[32,4,128]{2,1,0:T(4,128)}), f32[32,4,128]{2,1,0:T(4,128)S(1)}, u32[]{:S(2)}, u32[]{:S(2)}) async-start(f32[32,4,128]{2,1,0:T(4,128)} %bitcast.17), calls=%async_computation.12 | async-start | bytes 131072 | tf_op jit(solution)/shard_map/all_to_all | solution.py:491

commit v7 on v6

--- a/solution.py
+++ b/solution.py
@@ -153,15 +153,19 @@
     return jnp.clip(-curv * (lin + pushed), -move_limit, move_limit)
 
 
+def product_chunk(block, moved):
+    moved = jnp.concatenate([moved.astype(BF)] * 8, axis=0)
+    return lax.dot_general(block, moved, NT, preferred_element_type=F32)
+
+
 def product_of_trial(at_ref, columns, curv_ref, lin_ref, lam_ref, part_ref):
     lam_b = as_rows(at_ref, lam_ref)
-    total = jnp.zeros((16, M), F32)
+    total = jnp.zeros((M, 128), F32)
     for chunk in range(CHUNKS):
         block = columns.chunk(chunk)
-        moved = trial_chunk(block, curv_ref, lin_ref, lam_b, chunk).astype(BF)
-        total += lax.dot_general(moved, block, NT, preferred_element_type=F32)
+        total += product_chunk(block, trial_chunk(block, curv_ref, lin_ref, lam_b, chunk))
     for k, slot in enumerate(slots(at_ref)):
-        part_ref[pl.ds(slot, 1), :] = total[0:1, k * 128 : (k + 1) * 128]
+        part_ref[pl.ds(slot, 1), :] = total[k * 128 : (k + 1) * 128, :].T[0:1, :]
 
 
 def newton_update(lam, total, bound, inv_ref, scale):
@@ -191,11 +195,11 @@
         weighted = (block.astype(F32) * curv).astype(BF)
         gram_ref[...] += lax.dot_general(weighted, block, NT, preferred_element_type=F32)
         moved = jnp.clip(-curv * lin, -move_limit, move_limit)
-        moved = jnp.broadcast_to(moved, (16, WIDTH)).astype(BF)
-        prod_ref[...] += lax.dot_general(moved, block, NT, preferred_element_type=F32)
+        prod_ref[...] += product_chunk(block, jnp.broadcast_to(moved, (16, WIDTH)))
     where = slots(at_ref)
     for a in range(NB):
-        half_ref[0, pl.ds(where[a], 1), SHARD_G, :] = prod_ref[0:1, a * 128 : (a + 1) * 128]
+        line = prod_ref[a * 128 : (a + 1) * 128, :].T[0:1, :]
+        half_ref[0, pl.ds(where[a], 1), SHARD_G, :] = line
         for b in range(NB):
             block_ref[where[a], where[b]] = gram_ref[
                 a * 128 : (a + 1) * 128, b * 128 : (b + 1) * 128
@@ -446,7 +450,7 @@
         [sds(packed), sds(packed)],
         [
             pltpu.VMEM((M, M), F32),
-            pltpu.VMEM((16, M), F32),
+            pltpu.VMEM((M, 128), F32),
             pltpu.VMEM((NB, NB, 128, 128), F32),
             pltpu.VMEM((2, *packed), F32),
             *FULL,
@@ -455,6 +459,7 @@
     )(at, *pieces, curv, lin)
 
     pieces = [pltpu.with_memory_space_constraint(piece, pltpu.HBM) for piece in pieces]
+    *pieces, mine, other = lax.optimization_barrier((*pieces, mine, other))
 
     swap = [(0, 1), (1, 0)]
     mine = mine + lax.ppermute(other, "brick_2", swap)

time: 229 us -> 234 us (1.022)
  Pallas kernels: 27.2 us -> 32.4 us
    pallas_call x2, Pallas kernels: 7.67 us -> 10.1 us  [on_device(): call(step_kernel, ins, [vector, vector], FULL, 20)]
where the time goes in v7:
time: 234 us; the launch traced here: 233 us
  blocking collectives  104 us (44%)
  waiting for transfers between devices  46.4 us (20%)
  starting transfers between devices  36.2 us (15%)
  Pallas kernels  32.4 us (14%)
  local copies, waits for them, and re-layouts  9.93 us (4%)
  other arithmetic  3.25 us (1%)
    all_to_all x8, blocking collectives, from_everyone(): lax.all_to_all(jnp.broadcast_to(array[None], (devices, *array.shape)), ax...  88.8 us
    ppermute x3, waiting for transfers between devices, on_device(): pieces[k] = lax.ppermute(pieces[k], 'grp', ring)  20.8 us
    all_to_all x1, blocking collectives, on_device(): shard = lax.all_to_all(mine, PLANE, 0, 0, tiled=True).sum(axis=0)  15.2 us
    pallas_call x1, Pallas kernels, on_device(): call(solve_kernel, [SM] + [HBM] * NB + [VM] * 5, [square, vector, vector,...  11.5 us
    all_to_all x1, starting transfers between devices, on_device(): both = lax.all_to_all(both, FAR, 0, 0, tiled=True)  10.4 us
    pallas_call x2, Pallas kernels, on_device(): call(step_kernel, ins, [vector, vector], FULL, 20)  10.1 us
    all_to_all x1, waiting for transfers between devices, on_device(): both = lax.all_to_all(both, FAR, 0, 0, tiled=True)  8.94 us
    all_to_all x1, waiting for transfers between devices, on_device(): arrived = lax.all_to_all(whole[back], FAR, 0, 0, tiled=True)  8.85 us
  transfers between devices with their start and end apart: 9, of which 6 were waited for; matrix products, arithmetic and copies ran while one was open for 3% of the time, Pallas kernels for 0%

profile of v7, /device:TPU:1, one launch (start us, length us, event | category | flops | bytes accessed | tf_op | source)
XLA Modules:
  0.0 233.0 jit_solution(10054471303875318628)
XLA Ops:
  2.1 6.5 %all-to-all-start = ((f32[8,32,256]{2,1,0:T(8,128)}), f32[8,32,256]{2,1,0:T(8,128)S(1)}, u32[]{:S(2)}, u32[]{:S(2)}) async-start(f32[8,32,256]{2,1,0:T(8,128)} %broadcast_in_dim.58), calls=%async_computation | async-start | bytes 524288 | tf_op jit(solution)/shard_map/all_to_all | solution.py:427
  8.6 3.9 %constant_dynamic-slice_fusion.1 = (bf16[128,4096]{1,0:T(8,128)(2,1)}, bf16[128,4096]{1,0:T(8,128)(2,1)}, bf16[128,4096]{1,0:T(8,128)(2,1)S(1)}, bf16[128,4096]{1,0:T(8,128)(2,1)}) fusion(bf16[128,16384]{1,0:T(8,128)(2,1)} %param.5, s32[]{:T(128)S(6)} %select_n.125, s32[]{:T(128)S(6)} %select_n.123, s32[]{:T(128)S(6)} %select_n.122, s32[]{:T(128)S(6)} %select_n.124), kind=kLoop, calls=%fused_computation.55 | loop fusion | bytes 8388624 | tf_op jit(solution)/shard_map/dynamic_slice | solution.py:430
  12.6 1.4 collective-permute-start
  13.9 2.4 %collective-permute-start.1 = (bf16[128,4096]{1,0:T(8,128)(2,1)}, bf16[128,4096]{1,0:T(8,128)(2,1)S(1)}, u32[]{:S(2)}, u32[]{:S(2)}) collective-permute-start(bf16[128,4096]{1,0:T(8,128)(2,1)} %get-tuple-element.30), channel_id=1, source_target_pairs={{0,2},{1,3},{2,0},{3,1},{4,6},{5,7},{6,4},{7,5},{8,10},{9,11},{10,... | collective-permute-start | bytes 3145736 | tf_op jit(solution)/shard_map/ppermute | solution.py:436
  16.3 1.2 collective-permute-start.2
  20.8 10.4 %all-to-all-start.1 = ((f32[32,4,256]{2,1,0:T(4,128)}), f32[32,4,256]{2,1,0:T(4,128)S(1)}, u32[]{:S(2)}, u32[]{:S(2)}) async-start(f32[32,4,256]{2,1,0:T(4,128)} %all_to_all.50), calls=%async_computation.1 | async-start | bytes 262144 | tf_op jit(solution)/shard_map/all_to_all | solution.py:442
  31.5 8.9 %all-to-all-done.1 = f32[32,4,256]{2,1,0:T(4,128)S(1)} async-done(((f32[32,4,256]{2,1,0:T(4,128)}), f32[32,4,256]{2,1,0:T(4,128)S(1)}, u32[]{:S(2)}, u32[]{:S(2)}) %all-to-all-start.1) | async-done | bytes 131104 | tf_op jit(solution)/shard_map/all_to_all | solution.py:442
  41.2 20.8 %collective-permute-done.1.two_hbm = bf16[128,4096]{1,0:T(8,128)(2,1)S(1)} collective-permute-done((bf16[128,4096]{1,0:T(8,128)(2,1)}, bf16[128,4096]{1,0:T(8,128)(2,1)S(1)}, u32[]{:S(2)}, u32[]{:S(2)}) %collective-permute-start.1) | collective-permute-done | bytes 1048608 | tf_op jit(solution)/shard_map/ppermute | solution.py:436
  61.9 7.1 %shard_map.68 = (f32[16,48,128]{2,1,0:T(8,128)S(1)}, f32[16,48,128]{2,1,0:T(8,128)S(1)}) custom-call(s32[2]{0:T(128)S(1)} %pad_add_fusion.3.at_ref, bf16[128,4096]{1,0:T(8,128)(2,1)S(1)} %get-tuple-element.36.own_hbm, bf16[128,4096]{1,0:T(8,128)(2,1)S(1)} %collective-permute-done.one_hbm, bf16[128,4096]{1,0:T(8,128)(2,1)S(1)} %collective-permute-done.1.two_hbm, ...), custom_call_target="tpu_custom_call" | custom-call | tf_op jit(solution)/shard_map/pallas_call | solution.py:447
  69.0 1.3 collective-permute-start.3
  70.3 1.3 collective-permute-done.3
  71.7 15.2 %all_to_all.79 = f32[16,48,128]{2,1,0:T(8,128)} all-to-all(f32[16,48,128]{2,1,0:T(8,128)S(1)} %add.136), channel_id=1, replica_groups=mesh['brick_0'=4,'brick_1'=8,'brick_2'=2,'grp'=4] {'brick_0','grp'}, dimensions={0} | all-to-all | bytes 786432 | tf_op jit(solution)/shard_map/all_to_all | solution.py:466
  88.0 16.7 %all_to_all.80 = f32[8,48,128]{2,1,0:T(8,128)S(1)} all-to-all(f32[8,48,128]{2,1,0:T(8,128)S(1)} %broadcast_in_dim.64), channel_id=1, replica_groups=mesh['brick_0'=4,'brick_1'=8,'brick_2'=2,'grp'=4] {'brick_1'}, dimensions={0} | all-to-all | bytes 393216 | tf_op jit(solution)/shard_map/all_to_all | solution.py:46
  104.7 11.1 %all_to_all.81.mine_ref = f32[16,48,128]{2,1,0:T(8,128)S(1)} all-to-all(f32[16,48,128]{2,1,0:T(8,128)S(1)} %broadcast_in_dim.65), channel_id=1, replica_groups=mesh['brick_0'=4,'brick_1'=8,'brick_2'=2,'grp'=4] {'brick_0','grp'}, dimensions={0} | all-to-all | bytes 786432 | tf_op jit(solution)/shard_map/all_to_all | solution.py:46
  115.8 4.1 %collective-permute-start.4 = (f32[16,48,128]{2,1,0:T(8,128)S(1)}, f32[16,48,128]{2,1,0:T(8,128)S(1)}, u32[]{:S(2)}, u32[]{:S(2)}) collective-permute-start(f32[16,48,128]{2,1,0:T(8,128)S(1)} %all_to_all.81.mine_ref), channel_id=1, source_target_pairs={{0,4},{4,0},{1,5},{5,1},{2,6},{6,2},{3,7},{7,3},{8,12},{12,8},{9,1... | collective-permute-start | bytes 1179656 | tf_op jit(solution)/shard_map/ppermute | solution.py:469
  120.0 1.3 collective-permute-done.4.other_ref
  121.3 11.5 %shard_map.69 = (f32[512,512]{1,0:T(8,128)S(1)}, f32[4,128]{1,0:T(4,128)S(1)}, f32[4,128]{1,0:T(4,128)S(1)}, f32[4,128]{1,0:T(4,128)S(1)}) custom-call(s32[2]{0:T(128)S(1)} %pad_add_fusion.3.at_ref, bf16[128,4096]{1,0:T(8,128)(2,1)} %copy-done, bf16[128,4096]{1,0:T(8,128)(2,1)} %copy-done.1, bf16[128,4096]{1,0:T(8,128)(2,1)} %copy-done.2, ...), custom_call_target="tpu_custom_call" | custom-call | tf_op jit(solution)/shard_map/pallas_call | solution.py:474
  132.9 7.6 %all_to_all.82 = f32[8,4,128]{2,1,0:T(4,128)S(1)} all-to-all(f32[8,4,128]{2,1,0:T(4,128)S(1)} %broadcast_in_dim.66), channel_id=1, replica_groups=mesh['brick_0'=4,'brick_1'=8,'brick_2'=2,'grp'=4] {'brick_2','grp'}, dimensions={0} | all-to-all | bytes 32768 | tf_op jit(solution)/shard_map/all_to_all | solution.py:46
  140.5 11.8 %all_to_all.83.gathered_ref = f32[32,4,128]{2,1,0:T(4,128)S(1)} all-to-all(f32[32,4,128]{2,1,0:T(4,128)S(1)} %broadcast_in_dim.67), channel_id=1, replica_groups=mesh['brick_0'=4,'brick_1'=8,'brick_2'=2,'grp'=4] {'brick_0','brick_1'}, dimensions={0} | all-to-all | bytes 131072 | tf_op jit(solution)/shard_map/all_to_all | solution.py:46
  152.4 5.0 %shard_map.70 = (f32[4,128]{1,0:T(4,128)S(1)}, f32[4,128]{1,0:T(4,128)S(1)}) custom-call(s32[2]{0:T(128)S(1)} %pad_add_fusion.3.at_ref, bf16[128,4096]{1,0:T(8,128)(2,1)} %copy-done, bf16[128,4096]{1,0:T(8,128)(2,1)} %copy-done.1, bf16[128,4096]{1,0:T(8,128)(2,1)} %copy-done.2, bf16[128,4096]{1,0:T(8,128)(2,1)} %collective-permute-done.2.three_hbm, ...), custom_call_target="tpu_custom_call" | custom-call | tf_op jit(solution)/shard_map/pallas_call | solution.py:488
  157.4 8.8 %all_to_all.84 = f32[8,4,128]{2,1,0:T(4,128)S(1)} all-to-all(f32[8,4,128]{2,1,0:T(4,128)S(1)} %broadcast_in_dim.68), channel_id=1, replica_groups=mesh['brick_0'=4,'brick_1'=8,'brick_2'=2,'grp'=4] {'brick_2','grp'}, dimensions={0} | all-to-all | bytes 32768 | tf_op jit(solution)/shard_map/all_to_all | solution.py:46
  166.2 11.9 %all_to_all.85.gathered_ref = f32[32,4,128]{2,1,0:T(4,128)S(1)} all-to-all(f32[32,4,128]{2,1,0:T(4,128)S(1)} %broadcast_in_dim.69), channel_id=1, replica_groups=mesh['brick_0'=4,'brick_1'=8,'brick_2'=2,'grp'=4] {'brick_0','brick_1'}, dimensions={0} | all-to-all | bytes 131072 | tf_op jit(solution)/shard_map/all_to_all | solution.py:46
  178.1 5.0 %shard_map.71 = (f32[4,128]{1,0:T(4,128)S(1)}, f32[4,128]{1,0:T(4,128)S(1)}) custom-call(s32[2]{0:T(128)S(1)} %pad_add_fusion.3.at_ref, bf16[128,4096]{1,0:T(8,128)(2,1)} %copy-done, bf16[128,4096]{1,0:T(8,128)(2,1)} %copy-done.1, bf16[128,4096]{1,0:T(8,128)(2,1)} %copy-done.2, bf16[128,4096]{1,0:T(8,128)(2,1)} %collective-permute-done.2.three_hbm, ...), custom_call_target="tpu_custom_call" | custom-call | tf_op jit(solution)/shard_map/pallas_call | solution.py:488
  183.2 8.9 %all_to_all.86 = f32[8,4,128]{2,1,0:T(4,128)S(1)} all-to-all(f32[8,4,128]{2,1,0:T(4,128)S(1)} %broadcast_in_dim.70), channel_id=1, replica_groups=mesh['brick_0'=4,'brick_1'=8,'brick_2'=2,'grp'=4] {'brick_2','grp'}, dimensions={0} | all-to-all | bytes 32768 | tf_op jit(solution)/shard_map/all_to_all | solution.py:46
  192.1 11.9 %all_to_all.87.gathered_ref = f32[32,4,128]{2,1,0:T(4,128)S(1)} all-to-all(f32[32,4,128]{2,1,0:T(4,128)S(1)} %broadcast_in_dim.122), channel_id=1, replica_groups=mesh['brick_0'=4,'brick_1'=8,'brick_2'=2,'grp'=4] {'brick_0','brick_1'}, dimensions={0} | all-to-all | bytes 131072 | tf_op jit(solution)/shard_map/all_to_all | solution.py:46
  204.0 3.8 %shard_map.72 = (f32[4,128]{1,0:T(4,128)}, f32[8,32,128]{2,1,0:T(8,128)}) custom-call(s32[2]{0:T(128)S(1)} %pad_add_fusion.3.at_ref, bf16[128,4096]{1,0:T(8,128)(2,1)} %copy-done, bf16[128,4096]{1,0:T(8,128)(2,1)} %copy-done.1, bf16[128,4096]{1,0:T(8,128)(2,1)} %copy-done.2, bf16[128,4096]{1,0:T(8,128)(2,1)} %collective-permute-done.2.three_hbm, ...), custom_call_target="tpu_custom_call" | custom-call | tf_op jit(solution)/shard_map/pallas_call | solution.py:491
  207.8 5.0 %all-to-all-start.11 = ((f32[8,32,128]{2,1,0:T(8,128)}), f32[8,32,128]{2,1,0:T(8,128)S(1)}, u32[]{:S(2)}, u32[]{:S(2)}) async-start(f32[8,32,128]{2,1,0:T(8,128)} %get-tuple-element.50), calls=%async_computation.11 | async-start | bytes 262144 | tf_op jit(solution)/shard_map/all_to_all | solution.py:495
  212.7 5.2 %all-to-all-done.11 = f32[8,32,128]{2,1,0:T(8,128)S(1)} async-done(((f32[8,32,128]{2,1,0:T(8,128)}), f32[8,32,128]{2,1,0:T(8,128)S(1)}, u32[]{:S(2)}, u32[]{:S(2)}) %all-to-all-start.11) | async-done | bytes 131104 | tf_op jit(solution)/shard_map/all_to_all | solution.py:495
  217.9 1.2 gather_fusion.2
  219.1 3.9 %all-to-all-start.12 = ((f32[32,4,128]{2,1,0:T(4,128)}), f32[32,4,128]{2,1,0:T(4,128)S(1)}, u32[]{:S(2)}, u32[]{:S(2)}) async-start(f32[32,4,128]{2,1,0:T(4,128)} %bitcast.17), calls=%async_computation.12 | async-start | bytes 131072 | tf_op jit(solution)/shard_map/all_to_all | solution.py:496
  223.0 8.8 %all-to-all-done.12 = f32[32,4,128]{2,1,0:T(4,128)S(1)} async-done(((f32[32,4,128]{2,1,0:T(4,128)}), f32[32,4,128]{2,1,0:T(4,128)S(1)}, u32[]{:S(2)}, u32[]{:S(2)}) %all-to-all-start.12) | async-done | bytes 65568 | tf_op jit(solution)/shard_map/all_to_all | solution.py:496
  231.9 1.2 gather_fusion.3
  (63 shorter events, 6.9 us)
Async XLA Ops:
  2.1 17.3 %all-to-all-start = ((f32[8,32,256]{2,1,0:T(8,128)}), f32[8,32,256]{2,1,0:T(8,128)S(1)}, u32[]{:S(2)}, u32[]{:S(2)}) async-start(f32[8,32,256]{2,1,0:T(8,128)} %broadcast_in_dim.58), calls=%async_computation | async-start | bytes 524288 | tf_op jit(solution)/shard_map/all_to_all | solution.py:427
  8.6 8.9 %copy-start.4 = (s32[8192]{0:T(1024)S(1)}, s32[8192]{0:T(1024)}, u32[]{:S(2)}) copy-start(s32[8192]{0:T(1024)} %param.6) | copy-start | bytes 98308
  12.6 74.3 %copy-start = (bf16[128,4096]{1,0:T(8,128)(2,1)}, bf16[128,4096]{1,0:T(8,128)(2,1)S(1)}, u32[]{:S(2)}) copy-start(bf16[128,4096]{1,0:T(8,128)(2,1)S(1)} %get-tuple-element.36.own_hbm) | copy-start | bytes 3145732
  12.6 28.6 %collective-permute-start = (bf16[128,4096]{1,0:T(8,128)(2,1)}, bf16[128,4096]{1,0:T(8,128)(2,1)S(1)}, u32[]{:S(2)}, u32[]{:S(2)}) collective-permute-start(bf16[128,4096]{1,0:T(8,128)(2,1)} %get-tuple-element.29), channel_id=1, source_target_pairs={{0,1},{1,2},{2,3},{3,0},{4,5},{5,6},{6,7},{7,4},{8,9},{9,10},{10,1... | collective-permute-start | bytes 3145736 | tf_op jit(solution)/shard_map/ppermute | solution.py:436
  13.9 48.0 %collective-permute-start.1 = (bf16[128,4096]{1,0:T(8,128)(2,1)}, bf16[128,4096]{1,0:T(8,128)(2,1)S(1)}, u32[]{:S(2)}, u32[]{:S(2)}) collective-permute-start(bf16[128,4096]{1,0:T(8,128)(2,1)} %get-tuple-element.30), channel_id=1, source_target_pairs={{0,2},{1,3},{2,0},{3,1},{4,6},{5,7},{6,4},{7,5},{8,10},{9,11},{10,... | collective-permute-start | bytes 3145736 | tf_op jit(solution)/shard_map/ppermute | solution.py:436
  16.3 45.6 %collective-permute-start.2 = (bf16[128,4096]{1,0:T(8,128)(2,1)}, bf16[128,4096]{1,0:T(8,128)(2,1)}, u32[]{:S(2)}, u32[]{:S(2)}) collective-permute-start(bf16[128,4096]{1,0:T(8,128)(2,1)} %get-tuple-element.31), channel_id=1, source_target_pairs={{0,3},{1,0},{2,1},{3,2},{4,7},{5,4},{6,5},{7,6},{8,11},{9,8},{10,9... | collective-permute-start | bytes 3145736 | tf_op jit(solution)/shard_map/ppermute | solution.py:436
  20.8 19.6 %all-to-all-start.1 = ((f32[32,4,256]{2,1,0:T(4,128)}), f32[32,4,256]{2,1,0:T(4,128)S(1)}, u32[]{:S(2)}, u32[]{:S(2)}) async-start(f32[32,4,256]{2,1,0:T(4,128)} %all_to_all.50), calls=%async_computation.1 | async-start | bytes 262144 | tf_op jit(solution)/shard_map/all_to_all | solution.py:442
  41.1 80.2 %copy-start.3 = (f32[512]{0:T(512)S(1)}, f32[512]{0:T(512)}, u32[]{:S(2)}) copy-start(f32[512]{0:T(512)} %param.9) | copy-start | bytes 6148
  41.1 74.7 %copy-start.1 = (bf16[128,4096]{1,0:T(8,128)(2,1)}, bf16[128,4096]{1,0:T(8,128)(2,1)S(1)}, u32[]{:S(2)}) copy-start(bf16[128,4096]{1,0:T(8,128)(2,1)S(1)} %collective-permute-done.one_hbm) | copy-start | bytes 3145732
  61.9 53.9 %copy-start.2 = (bf16[128,4096]{1,0:T(8,128)(2,1)}, bf16[128,4096]{1,0:T(8,128)(2,1)S(1)}, u32[]{:S(2)}) copy-start(bf16[128,4096]{1,0:T(8,128)(2,1)S(1)} %collective-permute-done.1.two_hbm) | copy-start | bytes 3145732
  69.0 2.7 %collective-permute-start.3 = (f32[16,48,128]{2,1,0:T(8,128)S(1)}, f32[16,48,128]{2,1,0:T(8,128)S(1)}, u32[]{:S(2)}, u32[]{:S(2)}) collective-permute-start(f32[16,48,128]{2,1,0:T(8,128)S(1)} %get-tuple-element.41), channel_id=1, source_target_pairs={{0,4},{4,0},{1,5},{5,1},{2,6},{6,2},{3,7},{7,3},{8,12},{12,8},{9,1... | collective-permute-start | bytes 1179656 | tf_op jit(solution)/shard_map/ppermute | solution.py:465
  115.8 5.5 %collective-permute-start.4 = (f32[16,48,128]{2,1,0:T(8,128)S(1)}, f32[16,48,128]{2,1,0:T(8,128)S(1)}, u32[]{:S(2)}, u32[]{:S(2)}) collective-permute-start(f32[16,48,128]{2,1,0:T(8,128)S(1)} %all_to_all.81.mine_ref), channel_id=1, source_target_pairs={{0,4},{4,0},{1,5},{5,1},{2,6},{6,2},{3,7},{7,3},{8,12},{12,8},{9,1... | collective-permute-start | bytes 1179656 | tf_op jit(solution)/shard_map/ppermute | solution.py:469
  207.8 10.2 %all-to-all-start.11 = ((f32[8,32,128]{2,1,0:T(8,128)}), f32[8,32,128]{2,1,0:T(8,128)S(1)}, u32[]{:S(2)}, u32[]{:S(2)}) async-start(f32[8,32,128]{2,1,0:T(8,128)} %get-tuple-element.50), calls=%async_computation.11 | async-start | bytes 262144 | tf_op jit(solution)/shard_map/all_to_all | solution.py:495
  219.1 12.7 %all-to-all-start.12 = ((f32[32,4,128]{2,1,0:T(4,128)}), f32[32,4,128]{2,1,0:T(4,128)S(1)}, u32[]{:S(2)}, u32[]{:S(2)}) async-start(f32[32,4,128]{2,1,0:T(4,128)} %bitcast.17), calls=%async_computation.12 | async-start | bytes 131072 | tf_op jit(solution)/shard_map/all_to_all | solution.py:496

commit v8 on v6

--- a/solution.py
+++ b/solution.py
@@ -177,25 +177,24 @@
 
 def gram_kernel(
     at_ref, own_hbm, one_hbm, two_hbm, three_hbm, curv_ref, lin_ref,
-    mine_ref, other_ref, gram_ref, prod_ref, block_ref, half_ref, full_ref, sems,
+    mine_ref, other_ref, gram_ref, block_ref, half_ref, full_ref, sems,
 ):
     core = at_ref[1]
     columns = Columns((own_hbm, one_hbm, two_hbm, three_hbm), full_ref, sems)
     gram_ref[...] = jnp.zeros_like(gram_ref)
-    prod_ref[...] = jnp.zeros_like(prod_ref)
     for s in range(SHARDS):
         half_ref[s // HALF, s % HALF, SHARD_G:, :] = jnp.zeros((8, 128), F32)
     for chunk in range(CHUNKS):
         block = columns.chunk(chunk)
         curv, lin = flat_rows(curv_ref, chunk), flat_rows(lin_ref, chunk)
         weighted = (block.astype(F32) * curv).astype(BF)
-        gram_ref[...] += lax.dot_general(weighted, block, NT, preferred_element_type=F32)
         moved = jnp.clip(-curv * lin, -move_limit, move_limit)
         moved = jnp.broadcast_to(moved, (16, WIDTH)).astype(BF)
-        prod_ref[...] += lax.dot_general(moved, block, NT, preferred_element_type=F32)
+        both = jnp.concatenate([weighted, moved], axis=0)
+        gram_ref[...] += lax.dot_general(both, block, NT, preferred_element_type=F32)
     where = slots(at_ref)
     for a in range(NB):
-        half_ref[0, pl.ds(where[a], 1), SHARD_G, :] = prod_ref[0:1, a * 128 : (a + 1) * 128]
+        half_ref[0, pl.ds(where[a], 1), SHARD_G, :] = gram_ref[M : M + 1, a * 128 : (a + 1) * 128]
         for b in range(NB):
             block_ref[where[a], where[b]] = gram_ref[
                 a * 128 : (a + 1) * 128, b * 128 : (b + 1) * 128
@@ -445,8 +444,7 @@
         [SM] + [HBM] * NB + [VM] * 2,
         [sds(packed), sds(packed)],
         [
-            pltpu.VMEM((M, M), F32),
-            pltpu.VMEM((16, M), F32),
+            pltpu.VMEM((M + 16, M), F32),
             pltpu.VMEM((NB, NB, 128, 128), F32),
             pltpu.VMEM((2, *packed), F32),
             *FULL,

time: 229 us -> 228 us (level)
  no operation moved by 1% of the time
where the time goes in v8:
time: 228 us; the launch traced here: 227 us
  blocking collectives  104 us (46%)
  waiting for transfers between devices  46.4 us (20%)
  starting transfers between devices  36.2 us (16%)
  Pallas kernels  26.6 us (12%)
  local copies, waits for them, and re-layouts  9.93 us (4%)
  other arithmetic  3.25 us (1%)
    all_to_all x8, blocking collectives, from_everyone(): lax.all_to_all(jnp.broadcast_to(array[None], (devices, *array.shape)), ax...  88.8 us
    ppermute x3, waiting for transfers between devices, on_device(): pieces[k] = lax.ppermute(pieces[k], 'grp', ring)  20.8 us
    all_to_all x1, blocking collectives, on_device(): shard = lax.all_to_all(mine, PLANE, 0, 0, tiled=True).sum(axis=0)  15.2 us
    pallas_call x1, Pallas kernels, on_device(): call(solve_kernel, [SM] + [HBM] * NB + [VM] * 5, [square, vector, vector,...  10.5 us
    all_to_all x1, starting transfers between devices, on_device(): both = lax.all_to_all(both, FAR, 0, 0, tiled=True)  10.4 us
    all_to_all x1, waiting for transfers between devices, on_device(): both = lax.all_to_all(both, FAR, 0, 0, tiled=True)  8.94 us
    all_to_all x1, waiting for transfers between devices, on_device(): arrived = lax.all_to_all(whole[back], FAR, 0, 0, tiled=True)  8.85 us
    pallas_call x2, Pallas kernels, on_device(): call(step_kernel, ins, [vector, vector], FULL, 20)  7.67 us
  transfers between devices with their start and end apart: 9, of which 6 were waited for; matrix products, arithmetic and copies ran while one was open for 3% of the time, Pallas kernels for 0%

profile of v8, /device:TPU:1, one launch (start us, length us, event | category | flops | bytes accessed | tf_op | source)
XLA Modules:
  0.0 227.3 jit_solution(8540008848465919532)
XLA Ops:
  2.1 6.5 %all-to-all-start = ((f32[8,32,256]{2,1,0:T(8,128)}), f32[8,32,256]{2,1,0:T(8,128)S(1)}, u32[]{:S(2)}, u32[]{:S(2)}) async-start(f32[8,32,256]{2,1,0:T(8,128)} %broadcast_in_dim.58), calls=%async_computation | async-start | bytes 524288 | tf_op jit(solution)/shard_map/all_to_all | solution.py:422
  8.6 3.9 %constant_dynamic-slice_fusion.1 = (bf16[128,4096]{1,0:T(8,128)(2,1)}, bf16[128,4096]{1,0:T(8,128)(2,1)}, bf16[128,4096]{1,0:T(8,128)(2,1)S(1)}, bf16[128,4096]{1,0:T(8,128)(2,1)}) fusion(bf16[128,16384]{1,0:T(8,128)(2,1)} %param.5, s32[]{:T(128)S(6)} %select_n.125, s32[]{:T(128)S(6)} %select_n.123, s32[]{:T(128)S(6)} %select_n.122, s32[]{:T(128)S(6)} %select_n.124), kind=kLoop, calls=%fused_computation.55 | loop fusion | bytes 8388624 | tf_op jit(solution)/shard_map/dynamic_slice | solution.py:425
  12.6 1.4 collective-permute-start
  13.9 2.4 %collective-permute-start.1 = (bf16[128,4096]{1,0:T(8,128)(2,1)}, bf16[128,4096]{1,0:T(8,128)(2,1)S(1)}, u32[]{:S(2)}, u32[]{:S(2)}) collective-permute-start(bf16[128,4096]{1,0:T(8,128)(2,1)} %get-tuple-element.24), channel_id=1, source_target_pairs={{0,2},{1,3},{2,0},{3,1},{4,6},{5,7},{6,4},{7,5},{8,10},{9,11},{10,... | collective-permute-start | bytes 3145736 | tf_op jit(solution)/shard_map/ppermute | solution.py:431
  16.3 1.2 collective-permute-start.2
  20.8 10.4 %all-to-all-start.1 = ((f32[32,4,256]{2,1,0:T(4,128)}), f32[32,4,256]{2,1,0:T(4,128)S(1)}, u32[]{:S(2)}, u32[]{:S(2)}) async-start(f32[32,4,256]{2,1,0:T(4,128)} %all_to_all.50), calls=%async_computation.1 | async-start | bytes 262144 | tf_op jit(solution)/shard_map/all_to_all | solution.py:437
  31.5 8.9 %all-to-all-done.1 = f32[32,4,256]{2,1,0:T(4,128)S(1)} async-done(((f32[32,4,256]{2,1,0:T(4,128)}), f32[32,4,256]{2,1,0:T(4,128)S(1)}, u32[]{:S(2)}, u32[]{:S(2)}) %all-to-all-start.1) | async-done | bytes 131104 | tf_op jit(solution)/shard_map/all_to_all | solution.py:437
  41.2 20.8 %collective-permute-done.1.two_hbm = bf16[128,4096]{1,0:T(8,128)(2,1)S(1)} collective-permute-done((bf16[128,4096]{1,0:T(8,128)(2,1)}, bf16[128,4096]{1,0:T(8,128)(2,1)S(1)}, u32[]{:S(2)}, u32[]{:S(2)}) %collective-permute-start.1) | collective-permute-done | bytes 1048608 | tf_op jit(solution)/shard_map/ppermute | solution.py:431
  61.9 4.7 %shard_map.68 = (f32[16,48,128]{2,1,0:T(8,128)S(1)}, f32[16,48,128]{2,1,0:T(8,128)S(1)}) custom-call(s32[2]{0:T(128)S(1)} %pad_add_fusion.3.at_ref, bf16[128,4096]{1,0:T(8,128)(2,1)S(1)} %get-tuple-element.22.own_hbm, bf16[128,4096]{1,0:T(8,128)(2,1)S(1)} %collective-permute-done.one_hbm, bf16[128,4096]{1,0:T(8,128)(2,1)S(1)} %collective-permute-done.1.two_hbm, ...), custom_call_target="tpu_custom_call" | custom-call | tf_op jit(solution)/shard_map/pallas_call | solution.py:442
  66.7 1.3 collective-permute-start.3
  68.0 1.3 collective-permute-done.3
  69.4 15.2 %all_to_all.79 = f32[16,48,128]{2,1,0:T(8,128)} all-to-all(f32[16,48,128]{2,1,0:T(8,128)S(1)} %add.136), channel_id=1, replica_groups=mesh['brick_0'=4,'brick_1'=8,'brick_2'=2,'grp'=4] {'brick_0','grp'}, dimensions={0} | all-to-all | bytes 786432 | tf_op jit(solution)/shard_map/all_to_all | solution.py:459
  85.6 16.7 %all_to_all.80 = f32[8,48,128]{2,1,0:T(8,128)S(1)} all-to-all(f32[8,48,128]{2,1,0:T(8,128)S(1)} %broadcast_in_dim.64), channel_id=1, replica_groups=mesh['brick_0'=4,'brick_1'=8,'brick_2'=2,'grp'=4] {'brick_1'}, dimensions={0} | all-to-all | bytes 393216 | tf_op jit(solution)/shard_map/all_to_all | solution.py:46
  102.3 11.1 %all_to_all.81.mine_ref = f32[16,48,128]{2,1,0:T(8,128)S(1)} all-to-all(f32[16,48,128]{2,1,0:T(8,128)S(1)} %broadcast_in_dim.65), channel_id=1, replica_groups=mesh['brick_0'=4,'brick_1'=8,'brick_2'=2,'grp'=4] {'brick_0','grp'}, dimensions={0} | all-to-all | bytes 786432 | tf_op jit(solution)/shard_map/all_to_all | solution.py:46
  113.5 4.1 %collective-permute-start.4 = (f32[16,48,128]{2,1,0:T(8,128)S(1)}, f32[16,48,128]{2,1,0:T(8,128)S(1)}, u32[]{:S(2)}, u32[]{:S(2)}) collective-permute-start(f32[16,48,128]{2,1,0:T(8,128)S(1)} %all_to_all.81.mine_ref), channel_id=1, source_target_pairs={{0,4},{4,0},{1,5},{5,1},{2,6},{6,2},{3,7},{7,3},{8,12},{12,8},{9,1... | collective-permute-start | bytes 1179656 | tf_op jit(solution)/shard_map/ppermute | solution.py:462
  117.6 1.3 collective-permute-done.4.other_ref
  119.0 10.5 %shard_map.69 = (f32[512,512]{1,0:T(8,128)S(1)}, f32[4,128]{1,0:T(4,128)S(1)}, f32[4,128]{1,0:T(4,128)S(1)}, f32[4,128]{1,0:T(4,128)S(1)}) custom-call(s32[2]{0:T(128)S(1)} %pad_add_fusion.3.at_ref, bf16[128,4096]{1,0:T(8,128)(2,1)} %copy-done, bf16[128,4096]{1,0:T(8,128)(2,1)} %copy-done.1, bf16[128,4096]{1,0:T(8,128)(2,1)} %copy-done.2, ...), custom_call_target="tpu_custom_call" | custom-call | tf_op jit(solution)/shard_map/pallas_call | solution.py:467
  129.5 7.6 %all_to_all.82 = f32[8,4,128]{2,1,0:T(4,128)S(1)} all-to-all(f32[8,4,128]{2,1,0:T(4,128)S(1)} %broadcast_in_dim.66), channel_id=1, replica_groups=mesh['brick_0'=4,'brick_1'=8,'brick_2'=2,'grp'=4] {'brick_2','grp'}, dimensions={0} | all-to-all | bytes 32768 | tf_op jit(solution)/shard_map/all_to_all | solution.py:46
  137.2 11.8 %all_to_all.83.gathered_ref = f32[32,4,128]{2,1,0:T(4,128)S(1)} all-to-all(f32[32,4,128]{2,1,0:T(4,128)S(1)} %broadcast_in_dim.67), channel_id=1, replica_groups=mesh['brick_0'=4,'brick_1'=8,'brick_2'=2,'grp'=4] {'brick_0','brick_1'}, dimensions={0} | all-to-all | bytes 131072 | tf_op jit(solution)/shard_map/all_to_all | solution.py:46
  149.0 3.8 %shard_map.70 = (f32[4,128]{1,0:T(4,128)S(1)}, f32[4,128]{1,0:T(4,128)S(1)}) custom-call(s32[2]{0:T(128)S(1)} %pad_add_fusion.3.at_ref, bf16[128,4096]{1,0:T(8,128)(2,1)} %copy-done, bf16[128,4096]{1,0:T(8,128)(2,1)} %copy-done.1, bf16[128,4096]{1,0:T(8,128)(2,1)} %copy-done.2, bf16[128,4096]{1,0:T(8,128)(2,1)} %collective-permute-done.2.three_hbm, ...), custom_call_target="tpu_custom_call" | custom-call | tf_op jit(solution)/shard_map/pallas_call | solution.py:481
  152.9 8.8 %all_to_all.84 = f32[8,4,128]{2,1,0:T(4,128)S(1)} all-to-all(f32[8,4,128]{2,1,0:T(4,128)S(1)} %broadcast_in_dim.68), channel_id=1, replica_groups=mesh['brick_0'=4,'brick_1'=8,'brick_2'=2,'grp'=4] {'brick_2','grp'}, dimensions={0} | all-to-all | bytes 32768 | tf_op jit(solution)/shard_map/all_to_all | solution.py:46
  161.7 11.9 %all_to_all.85.gathered_ref = f32[32,4,128]{2,1,0:T(4,128)S(1)} all-to-all(f32[32,4,128]{2,1,0:T(4,128)S(1)} %broadcast_in_dim.69), channel_id=1, replica_groups=mesh['brick_0'=4,'brick_1'=8,'brick_2'=2,'grp'=4] {'brick_0','brick_1'}, dimensions={0} | all-to-all | bytes 131072 | tf_op jit(solution)/shard_map/all_to_all | solution.py:46
  173.6 3.8 %shard_map.71 = (f32[4,128]{1,0:T(4,128)S(1)}, f32[4,128]{1,0:T(4,128)S(1)}) custom-call(s32[2]{0:T(128)S(1)} %pad_add_fusion.3.at_ref, bf16[128,4096]{1,0:T(8,128)(2,1)} %copy-done, bf16[128,4096]{1,0:T(8,128)(2,1)} %copy-done.1, bf16[128,4096]{1,0:T(8,128)(2,1)} %copy-done.2, bf16[128,4096]{1,0:T(8,128)(2,1)} %collective-permute-done.2.three_hbm, ...), custom_call_target="tpu_custom_call" | custom-call | tf_op jit(solution)/shard_map/pallas_call | solution.py:481
  177.4 8.9 %all_to_all.86 = f32[8,4,128]{2,1,0:T(4,128)S(1)} all-to-all(f32[8,4,128]{2,1,0:T(4,128)S(1)} %broadcast_in_dim.70), channel_id=1, replica_groups=mesh['brick_0'=4,'brick_1'=8,'brick_2'=2,'grp'=4] {'brick_2','grp'}, dimensions={0} | all-to-all | bytes 32768 | tf_op jit(solution)/shard_map/all_to_all | solution.py:46
  186.4 11.9 %all_to_all.87.gathered_ref = f32[32,4,128]{2,1,0:T(4,128)S(1)} all-to-all(f32[32,4,128]{2,1,0:T(4,128)S(1)} %broadcast_in_dim.122), channel_id=1, replica_groups=mesh['brick_0'=4,'brick_1'=8,'brick_2'=2,'grp'=4] {'brick_0','brick_1'}, dimensions={0} | all-to-all | bytes 131072 | tf_op jit(solution)/shard_map/all_to_all | solution.py:46
  198.3 3.8 %shard_map.72 = (f32[4,128]{1,0:T(4,128)}, f32[8,32,128]{2,1,0:T(8,128)}) custom-call(s32[2]{0:T(128)S(1)} %pad_add_fusion.3.at_ref, bf16[128,4096]{1,0:T(8,128)(2,1)} %copy-done, bf16[128,4096]{1,0:T(8,128)(2,1)} %copy-done.1, bf16[128,4096]{1,0:T(8,128)(2,1)} %copy-done.2, bf16[128,4096]{1,0:T(8,128)(2,1)} %collective-permute-done.2.three_hbm, ...), custom_call_target="tpu_custom_call" | custom-call | tf_op jit(solution)/shard_map/pallas_call | solution.py:484
  202.0 5.0 %all-to-all-start.11 = ((f32[8,32,128]{2,1,0:T(8,128)}), f32[8,32,128]{2,1,0:T(8,128)S(1)}, u32[]{:S(2)}, u32[]{:S(2)}) async-start(f32[8,32,128]{2,1,0:T(8,128)} %get-tuple-element.38), calls=%async_computation.11 | async-start | bytes 262144 | tf_op jit(solution)/shard_map/all_to_all | solution.py:488
  207.0 5.2 %all-to-all-done.11 = f32[8,32,128]{2,1,0:T(8,128)S(1)} async-done(((f32[8,32,128]{2,1,0:T(8,128)}), f32[8,32,128]{2,1,0:T(8,128)S(1)}, u32[]{:S(2)}, u32[]{:S(2)}) %all-to-all-start.11) | async-done | bytes 131104 | tf_op jit(solution)/shard_map/all_to_all | solution.py:488
  212.2 1.2 gather_fusion.2
  213.4 3.9 %all-to-all-start.12 = ((f32[32,4,128]{2,1,0:T(4,128)}), f32[32,4,128]{2,1,0:T(4,128)S(1)}, u32[]{:S(2)}, u32[]{:S(2)}) async-start(f32[32,4,128]{2,1,0:T(4,128)} %bitcast.17), calls=%async_computation.12 | async-start | bytes 131072 | tf_op jit(solution)/shard_map/all_to_all | solution.py:489
  217.3 8.8 %all-to-all-done.12 = f32[32,4,128]{2,1,0:T(4,128)S(1)} async-done(((f32[32,4,128]{2,1,0:T(4,128)}), f32[32,4,128]{2,1,0:T(4,128)S(1)}, u32[]{:S(2)}, u32[]{:S(2)}) %all-to-all-start.12) | async-done | bytes 65568 | tf_op jit(solution)/shard_map/all_to_all | solution.py:489
  226.1 1.2 gather_fusion.3
  (63 shorter events, 6.9 us)
Async XLA Ops:
  2.1 17.3 %all-to-all-start = ((f32[8,32,256]{2,1,0:T(8,128)}), f32[8,32,256]{2,1,0:T(8,128)S(1)}, u32[]{:S(2)}, u32[]{:S(2)}) async-start(f32[8,32,256]{2,1,0:T(8,128)} %broadcast_in_dim.58), calls=%async_computation | async-start | bytes 524288 | tf_op jit(solution)/shard_map/all_to_all | solution.py:422
  8.6 8.9 %copy-start.4 = (s32[8192]{0:T(1024)S(1)}, s32[8192]{0:T(1024)}, u32[]{:S(2)}) copy-start(s32[8192]{0:T(1024)} %param.6) | copy-start | bytes 98308
  12.6 72.0 %copy-start = (bf16[128,4096]{1,0:T(8,128)(2,1)}, bf16[128,4096]{1,0:T(8,128)(2,1)S(1)}, u32[]{:S(2)}) copy-start(bf16[128,4096]{1,0:T(8,128)(2,1)S(1)} %get-tuple-element.22.own_hbm) | copy-start | bytes 3145732
  12.6 28.6 %collective-permute-start = (bf16[128,4096]{1,0:T(8,128)(2,1)}, bf16[128,4096]{1,0:T(8,128)(2,1)S(1)}, u32[]{:S(2)}, u32[]{:S(2)}) collective-permute-start(bf16[128,4096]{1,0:T(8,128)(2,1)} %get-tuple-element.23), channel_id=1, source_target_pairs={{0,1},{1,2},{2,3},{3,0},{4,5},{5,6},{6,7},{7,4},{8,9},{9,10},{10,1... | collective-permute-start | bytes 3145736 | tf_op jit(solution)/shard_map/ppermute | solution.py:431
  13.9 48.0 %collective-permute-start.1 = (bf16[128,4096]{1,0:T(8,128)(2,1)}, bf16[128,4096]{1,0:T(8,128)(2,1)S(1)}, u32[]{:S(2)}, u32[]{:S(2)}) collective-permute-start(bf16[128,4096]{1,0:T(8,128)(2,1)} %get-tuple-element.24), channel_id=1, source_target_pairs={{0,2},{1,3},{2,0},{3,1},{4,6},{5,7},{6,4},{7,5},{8,10},{9,11},{10,... | collective-permute-start | bytes 3145736 | tf_op jit(solution)/shard_map/ppermute | solution.py:431
  16.3 45.6 %collective-permute-start.2 = (bf16[128,4096]{1,0:T(8,128)(2,1)}, bf16[128,4096]{1,0:T(8,128)(2,1)}, u32[]{:S(2)}, u32[]{:S(2)}) collective-permute-start(bf16[128,4096]{1,0:T(8,128)(2,1)} %get-tuple-element.25), channel_id=1, source_target_pairs={{0,3},{1,0},{2,1},{3,2},{4,7},{5,4},{6,5},{7,6},{8,11},{9,8},{10,9... | collective-permute-start | bytes 3145736 | tf_op jit(solution)/shard_map/ppermute | solution.py:431
  20.8 19.6 %all-to-all-start.1 = ((f32[32,4,256]{2,1,0:T(4,128)}), f32[32,4,256]{2,1,0:T(4,128)S(1)}, u32[]{:S(2)}, u32[]{:S(2)}) async-start(f32[32,4,256]{2,1,0:T(4,128)} %all_to_all.50), calls=%async_computation.1 | async-start | bytes 262144 | tf_op jit(solution)/shard_map/all_to_all | solution.py:437
  41.1 77.9 %copy-start.3 = (f32[512]{0:T(512)S(1)}, f32[512]{0:T(512)}, u32[]{:S(2)}) copy-start(f32[512]{0:T(512)} %param.9) | copy-start | bytes 6148
  41.1 72.3 %copy-start.1 = (bf16[128,4096]{1,0:T(8,128)(2,1)}, bf16[128,4096]{1,0:T(8,128)(2,1)S(1)}, u32[]{:S(2)}) copy-start(bf16[128,4096]{1,0:T(8,128)(2,1)S(1)} %collective-permute-done.one_hbm) | copy-start | bytes 3145732
  61.9 51.6 %copy-start.2 = (bf16[128,4096]{1,0:T(8,128)(2,1)}, bf16[128,4096]{1,0:T(8,128)(2,1)S(1)}, u32[]{:S(2)}) copy-start(bf16[128,4096]{1,0:T(8,128)(2,1)S(1)} %collective-permute-done.1.two_hbm) | copy-start | bytes 3145732
  66.7 2.7 %collective-permute-start.3 = (f32[16,48,128]{2,1,0:T(8,128)S(1)}, f32[16,48,128]{2,1,0:T(8,128)S(1)}, u32[]{:S(2)}, u32[]{:S(2)}) collective-permute-start(f32[16,48,128]{2,1,0:T(8,128)S(1)} %get-tuple-element.29), channel_id=1, source_target_pairs={{0,4},{4,0},{1,5},{5,1},{2,6},{6,2},{3,7},{7,3},{8,12},{12,8},{9,1... | collective-permute-start | bytes 1179656 | tf_op jit(solution)/shard_map/ppermute | solution.py:458
  113.5 5.5 %collective-permute-start.4 = (f32[16,48,128]{2,1,0:T(8,128)S(1)}, f32[16,48,128]{2,1,0:T(8,128)S(1)}, u32[]{:S(2)}, u32[]{:S(2)}) collective-permute-start(f32[16,48,128]{2,1,0:T(8,128)S(1)} %all_to_all.81.mine_ref), channel_id=1, source_target_pairs={{0,4},{4,0},{1,5},{5,1},{2,6},{6,2},{3,7},{7,3},{8,12},{12,8},{9,1... | collective-permute-start | bytes 1179656 | tf_op jit(solution)/shard_map/ppermute | solution.py:462
  202.0 10.2 %all-to-all-start.11 = ((f32[8,32,128]{2,1,0:T(8,128)}), f32[8,32,128]{2,1,0:T(8,128)S(1)}, u32[]{:S(2)}, u32[]{:S(2)}) async-start(f32[8,32,128]{2,1,0:T(8,128)} %get-tuple-element.38), calls=%async_computation.11 | async-start | bytes 262144 | tf_op jit(solution)/shard_map/all_to_all | solution.py:488
  213.4 12.7 %all-to-all-start.12 = ((f32[32,4,128]{2,1,0:T(4,128)}), f32[32,4,128]{2,1,0:T(4,128)S(1)}, u32[]{:S(2)}, u32[]{:S(2)}) async-start(f32[32,4,128]{2,1,0:T(4,128)} %bitcast.17), calls=%async_computation.12 | async-start | bytes 131072 | tf_op jit(solution)/shard_map/all_to_all | solution.py:489
